TPU v7x, 32 devices: a whole 2x2x4 slice. The times are simulated.
32 devices in a mesh: dp: 2 (over y), ctx: 4 (over z), mp: 4 (over x, core).
Axes of the slice: x: 2, y: 2, z: 4, core: 2. Of those that a mesh axis runs over, the one named last changes fastest.
Arguments:
- inputs: bfloat16 [8, 1024, 1024], P('dp', 'ctx'), may hold values from -6 to 6
- segment_ids: int32 [8, 1024], P('dp'), may hold values from 0 to 2, as said below
- norm_attn_one: bfloat16 [1024], P(('dp', 'ctx')), may hold values from 0.25 to 1.75
- query_one: bfloat16 [1024, 1024], P(('dp', 'ctx'), 'mp'), may hold values from -0.1875 to 0.1875
- key_one: bfloat16 [1024, 1024], P(('dp', 'ctx'), 'mp'), may hold values from -0.1875 to 0.1875
- value_one: bfloat16 [1024, 1024], P(('dp', 'ctx'), 'mp'), may hold values from -0.1875 to 0.1875
- output_one: bfloat16 [1024, 1024], P('mp', ('dp', 'ctx')), may hold values from -1.5 to 1.5
- norm_ffn_one: bfloat16 [1024], P(('dp', 'ctx')), may hold values from 0.25 to 1.75
- gate_one: bfloat16 [1024, 2816], P(('dp', 'ctx'), 'mp'), may hold values from -0.1875 to 0.1875
- up_one: bfloat16 [1024, 2816], P(('dp', 'ctx'), 'mp'), may hold values from -0.1875 to 0.1875
- down_one: bfloat16 [2816, 1024], P('mp', ('dp', 'ctx')), may hold values from -0.109375 to 0.109375
- norm_attn_two: bfloat16 [1024], P(('dp', 'ctx')), may hold values from 0.25 to 1.75
- query_two: bfloat16 [1024, 1024], P(('dp', 'ctx'), 'mp'), may hold values from -0.1875 to 0.1875
- key_two: bfloat16 [1024, 1024], P(('dp', 'ctx'), 'mp'), may hold values from -0.1875 to 0.1875
- value_two: bfloat16 [1024, 1024], P(('dp', 'ctx'), 'mp'), may hold values from -0.1875 to 0.1875
- output_two: bfloat16 [1024, 1024], P('mp', ('dp', 'ctx')), may hold values from -1.5 to 1.5
- norm_ffn_two: bfloat16 [1024], P(('dp', 'ctx')), may hold values from 0.25 to 1.75
- gate_two: bfloat16 [1024, 2816], P(('dp', 'ctx'), 'mp'), may hold values from -0.1875 to 0.1875
- up_two: bfloat16 [1024, 2816], P(('dp', 'ctx'), 'mp'), may hold values from -0.1875 to 0.1875
- down_two: bfloat16 [2816, 1024], P('mp', ('dp', 'ctx')), may hold values from -0.109375 to 0.109375
- cotangent: bfloat16 [8, 1024, 1024], P('dp', 'ctx'), may hold values from -6 to 6
Outputs:
- layer_one_out: bfloat16 [8, 1024, 1024], P('dp', 'ctx')
- layer_two_out: bfloat16 [8, 1024, 1024], P('dp', 'ctx')
- input_grad: float32 [8, 1024, 1024], P('dp', 'ctx')
- norm_attn_one_grad: float32 [1024], P(('dp', 'ctx'))
- query_one_grad: float32 [1024, 1024], P(('dp', 'ctx'), 'mp')
- key_one_grad: float32 [1024, 1024], P(('dp', 'ctx'), 'mp')
- value_one_grad: float32 [1024, 1024], P(('dp', 'ctx'), 'mp')
- output_one_grad: float32 [1024, 1024], P('mp', ('dp', 'ctx'))
- norm_ffn_one_grad: float32 [1024], P(('dp', 'ctx'))
- gate_one_grad: float32 [1024, 2816], P(('dp', 'ctx'), 'mp')
- up_one_grad: float32 [1024, 2816], P(('dp', 'ctx'), 'mp')
- down_one_grad: float32 [2816, 1024], P('mp', ('dp', 'ctx'))
- norm_attn_two_grad: float32 [1024], P(('dp', 'ctx'))
- query_two_grad: float32 [1024, 1024], P(('dp', 'ctx'), 'mp')
- key_two_grad: float32 [1024, 1024], P(('dp', 'ctx'), 'mp')
- value_two_grad: float32 [1024, 1024], P(('dp', 'ctx'), 'mp')
- output_two_grad: float32 [1024, 1024], P('mp', ('dp', 'ctx'))
- norm_ffn_two_grad: float32 [1024], P(('dp', 'ctx'))
- gate_two_grad: float32 [1024, 2816], P(('dp', 'ctx'), 'mp')
- up_two_grad: float32 [1024, 2816], P(('dp', 'ctx'), 'mp')
- down_two_grad: float32 [2816, 1024], P('mp', ('dp', 'ctx'))
Inputs may be any that keep to these rules, and one draw needn't show every extreme that they name: `segment_ids`: within each sequence the ids start at 0 and never fall along the positions.
All inputs are finite; a program needn't handle non-finite values.
Results may differ from a plain program's by a relative error of at most 0.04.
Values may be sent and summed in bfloat16 or wider, within the bound.
A program may use at most 256 MiB of HBM per device.

v0:
```python
import math

import jax
import jax.numpy as jnp
from jax import lax
from jax.sharding import PartitionSpec as P

HEAD_DIM = 64


epsilon = 1e-05
neg_large = -1e30


def project(left_operand, right_operand):
    return jnp.einsum(
        "sbd,de->sbe", left_operand, right_operand, preferred_element_type=jnp.float32
    )


def project_back(left_operand, right_operand):
    return jnp.einsum(
        "sbe,de->sbd", left_operand, right_operand, preferred_element_type=jnp.float32
    )


def weight_term(left_operand, right_operand):
    return jnp.einsum(
        "sbd,sbe->de", left_operand, right_operand, preferred_element_type=jnp.float32
    )


def head_total(partial_sum):
    return lax.psum(partial_sum.astype(jnp.bfloat16), "mp").astype(jnp.float32)


def head_back(partial_sum):
    return lax.psum(partial_sum.astype(jnp.bfloat16), "mp").astype(jnp.float32)


def rotary_tables(first_place, count_of_rows):
    half_width = HEAD_DIM // 2
    frequency = 10000.0 ** (-jnp.arange(half_width, dtype=jnp.float32) / half_width)
    places = (first_place + jnp.arange(count_of_rows, dtype=jnp.int32)).astype(jnp.float32)
    angles = places[:, None] * frequency[None, :]
    return (jnp.cos(angles)[None, :, None, :], jnp.sin(angles)[None, :, None, :])


def rotate(split_heads, cosine, sine_table):
    half_width = HEAD_DIM // 2
    first_half = split_heads[..., :half_width]
    second_half = split_heads[..., half_width:]
    return jnp.concatenate(
        [
            first_half * cosine - second_half * sine_table,
            first_half * sine_table + second_half * cosine,
        ],
        axis=-1,
    )


def rotate_back(split_heads, cosine, sine_table):
    half_width = HEAD_DIM // 2
    first_half = split_heads[..., :half_width]
    second_half = split_heads[..., half_width:]
    return jnp.concatenate(
        [
            first_half * cosine + second_half * sine_table,
            second_half * cosine - first_half * sine_table,
        ],
        axis=-1,
    )


def norm_forward(stream, gain_row):
    inverse = lax.rsqrt(jnp.mean(stream * stream, axis=-1, keepdims=True) + epsilon)
    normed = (stream * inverse * gain_row.astype(jnp.float32)).astype(jnp.bfloat16)
    return (normed, inverse)


def norm_backward(grad_normed, stream, inverse, gain_row):
    scaled = stream * inverse
    grad_scaled = grad_normed * gain_row.astype(jnp.float32)
    gain_grad = jnp.sum(grad_normed * scaled, axis=(0, 1))
    grad_stream = inverse * (
        grad_scaled - scaled * jnp.mean(grad_scaled * scaled, axis=-1, keepdims=True)
    )
    return (grad_stream, gain_grad)


def block_grads(
    query_block,
    grad_block,
    lse_block,
    delta_block,
    query_places,
    query_document_ids,
    key_block,
    value_block,
    key_places,
    key_segments,
):
    score_scale = HEAD_DIM ** (-0.5)
    scores = (
        jnp.einsum("sqhe,skhe->shqk", query_block, key_block, preferred_element_type=jnp.float32)
        * score_scale
    )
    visible = (
        (key_places[None, :] <= query_places[:, None])[None]
        & (key_segments[:, None, :] == query_document_ids[:, :, None])
    )[:, None]
    probabilities = jnp.where(visible, jnp.exp(scores - lse_block[..., None]), 0.0)
    grad_probs = jnp.einsum(
        "sqhe,skhe->shqk", grad_block, value_block, preferred_element_type=jnp.float32
    )
    grad_scores = (probabilities * (grad_probs - delta_block[..., None]) * score_scale).astype(
        jnp.bfloat16
    )
    query_grad = jnp.einsum(
        "shqk,skhe->sqhe", grad_scores, key_block, preferred_element_type=jnp.float32
    )
    key_grad = jnp.einsum(
        "shqk,sqhe->skhe", grad_scores, query_block, preferred_element_type=jnp.float32
    )
    value_grad = jnp.einsum(
        "shqk,sqhe->skhe",
        probabilities.astype(jnp.bfloat16),
        grad_block,
        preferred_element_type=jnp.float32,
    )
    return (query_grad, key_grad, value_grad)


def attend_forward(queries, key_rows, value_rows, segments, query_places):
    seq_count, count_of_rows, head_count, head_width = queries.shape
    score_scale = head_width ** (-0.5)
    query_document_ids = lax.dynamic_slice_in_dim(segments, query_places[0], count_of_rows, 1)
    last_query = query_places[count_of_rows - 1]
    initial = (
        jnp.full((seq_count, head_count, count_of_rows), neg_large, jnp.float32),
        jnp.zeros((seq_count, head_count, count_of_rows), jnp.float32),
        jnp.zeros((seq_count, count_of_rows, head_count, head_width), jnp.float32),
    )
    key_piece = lax.all_gather(key_rows, "ctx", axis=1, tiled=True)
    value_piece = lax.all_gather(value_rows, "ctx", axis=1, tiled=True)
    piece_rows = key_piece.shape[1]
    block_rows = math.gcd(piece_rows, 512)
    key_split = key_piece.reshape(seq_count, piece_rows, head_count, head_width)
    value_split = value_piece.reshape(seq_count, piece_rows, head_count, head_width)

    def absorb_visit(running, block_index):
        first_key = block_index * block_rows

        def absorb_compute(current):
            row_max, row_total, weighted = current
            key_block = lax.dynamic_slice_in_dim(key_split, first_key, block_rows, 1)
            value_block = lax.dynamic_slice_in_dim(value_split, first_key, block_rows, 1)
            key_places = first_key + jnp.arange(block_rows, dtype=jnp.int32)
            key_segments = lax.dynamic_slice_in_dim(segments, first_key, block_rows, 1)
            scores = (
                jnp.einsum(
                    "sqhe,skhe->shqk", queries, key_block, preferred_element_type=jnp.float32
                )
                * score_scale
            )
            visible = (
                (key_places[None, :] <= query_places[:, None])[None]
                & (key_segments[:, None, :] == query_document_ids[:, :, None])
            )[:, None]
            new_max = jnp.maximum(row_max, jnp.max(jnp.where(visible, scores, neg_large), axis=-1))
            exponent = jnp.where(visible, jnp.exp(scores - new_max[..., None]), 0.0)
            factor = jnp.exp(row_max - new_max)
            new_total = row_total * factor + jnp.sum(exponent, axis=-1)
            update = jnp.einsum(
                "shqk,skhe->sqhe",
                exponent.astype(jnp.bfloat16),
                value_block,
                preferred_element_type=jnp.float32,
            )
            new_weighted = weighted * jnp.transpose(factor, (0, 2, 1))[..., None] + update
            return (new_max, new_total, new_weighted)

        def absorb_keep(current):
            return current

        return (lax.cond(first_key <= last_query, absorb_compute, absorb_keep, running), None)

    result, unused = lax.scan(
        absorb_visit, initial, jnp.arange(piece_rows // block_rows, dtype=jnp.int32)
    )
    row_max, row_total, weighted = result
    attended = weighted / jnp.transpose(row_total, (0, 2, 1))[..., None]
    return (attended, row_max + jnp.log(row_total))


def attend_back_gather(
    queries, grad_attended, log_normalizer, row_delta, key_rows, value_rows, segments, query_places
):
    seq_count, count_of_rows, head_count, head_width = queries.shape
    query_document_ids = lax.dynamic_slice_in_dim(segments, query_places[0], count_of_rows, 1)
    last_query = query_places[count_of_rows - 1]
    all_keys, all_values = (
        lax.all_gather(key_rows, "ctx", axis=1, tiled=True),
        lax.all_gather(value_rows, "ctx", axis=1, tiled=True),
    )
    length = all_keys.shape[1]
    block_rows = math.gcd(length, 512)
    key_split = all_keys.reshape(seq_count, length, head_count, head_width)
    value_split = all_values.reshape(seq_count, length, head_count, head_width)
    initial = (
        jnp.zeros((seq_count, count_of_rows, head_count, head_width), jnp.float32),
        jnp.zeros((seq_count, length, head_count, head_width), jnp.float32),
        jnp.zeros((seq_count, length, head_count, head_width), jnp.float32),
    )

    def attend_visit(state_now, block_index):
        first_key = block_index * block_rows

        def attend_compute(current):
            query_acc, key_acc, value_acc = current
            key_block = lax.dynamic_slice_in_dim(key_split, first_key, block_rows, 1)
            value_block = lax.dynamic_slice_in_dim(value_split, first_key, block_rows, 1)
            key_places = first_key + jnp.arange(block_rows, dtype=jnp.int32)
            key_segments = lax.dynamic_slice_in_dim(segments, first_key, block_rows, 1)
            query_part, key_part, value_part = block_grads(
                queries,
                grad_attended,
                log_normalizer,
                row_delta,
                query_places,
                query_document_ids,
                key_block,
                value_block,
                key_places,
                key_segments,
            )
            key_acc = lax.dynamic_update_slice_in_dim(key_acc, key_part, first_key, 1)
            value_acc = lax.dynamic_update_slice_in_dim(value_acc, value_part, first_key, 1)
            return (query_acc + query_part, key_acc, value_acc)

        def attend_keep(current):
            return current

        return (lax.cond(first_key <= last_query, attend_compute, attend_keep, state_now), None)

    totals, unused = lax.scan(
        attend_visit, initial, jnp.arange(length // block_rows, dtype=jnp.int32)
    )
    query_grad, key_grad, value_grad = totals
    key_home, value_home = (
        lax.psum_scatter(
            key_grad.reshape(seq_count, length, -1).astype(jnp.bfloat16),
            "ctx",
            scatter_dimension=1,
            tiled=True,
        ).astype(jnp.float32),
        lax.psum_scatter(
            value_grad.reshape(seq_count, length, -1).astype(jnp.bfloat16),
            "ctx",
            scatter_dimension=1,
            tiled=True,
        ).astype(jnp.float32),
    )
    split_shape = (seq_count, count_of_rows, head_count, head_width)
    return (query_grad, key_home.reshape(split_shape), value_home.reshape(split_shape))


def forward_layer(stream, first_values, weights, segments, cosine, sine_table, query_places):
    norm_attn, w_query, w_key, w_value, w_output, norm_ffn, w_gate, w_up, w_down = weights
    seq_count, count_of_rows, model_width = stream.shape
    head_count = w_query.shape[1] // HEAD_DIM
    split_shape = (seq_count, count_of_rows, head_count, HEAD_DIM)
    normed, inverse_one = norm_forward(stream, norm_attn)
    queries = rotate(project(normed, w_query).reshape(split_shape), cosine, sine_table).astype(
        jnp.bfloat16
    )
    key_rows = (
        rotate(project(normed, w_key).reshape(split_shape), cosine, sine_table)
        .astype(jnp.bfloat16)
        .reshape(seq_count, count_of_rows, -1)
    )
    own_values = project(normed, w_value)
    if first_values is None:
        mixed = own_values.astype(jnp.bfloat16)
    else:
        mixed = (0.5 * own_values + 0.5 * first_values).astype(jnp.bfloat16)
    attended, log_normalizer = attend_forward(queries, key_rows, mixed, segments, query_places)
    attended_low = attended.reshape(seq_count, count_of_rows, -1).astype(jnp.bfloat16)
    hidden_one = stream + head_total(project(attended_low, w_output))
    normed_two, inverse_two = norm_forward(hidden_one, norm_ffn)
    gate_values = project(normed_two, w_gate)
    up_values = project(normed_two, w_up)
    activated = (jax.nn.silu(gate_values) * up_values).astype(jnp.bfloat16)
    result = hidden_one + head_total(project(activated, w_down))
    saved_state = (
        stream,
        inverse_one,
        normed,
        queries,
        key_rows,
        mixed,
        attended,
        log_normalizer,
        attended_low,
        hidden_one,
        inverse_two,
        normed_two,
        gate_values,
        up_values,
        activated,
    )
    return (result, saved_state, own_values)


def backward_layer(
    grad_out, value_extra, saved_state, weights, segments, cosine, sine_table, query_places, mixes
):
    (
        stream,
        inverse_one,
        normed,
        queries,
        key_rows,
        mixed,
        attended,
        log_normalizer,
        attended_low,
        hidden_one,
        inverse_two,
        normed_two,
        gate_values,
        up_values,
        activated,
    ) = saved_state
    norm_attn, w_query, w_key, w_value, w_output, norm_ffn, w_gate, w_up, w_down = weights
    seq_count, count_of_rows, head_count, head_width = queries.shape
    grad_branch = grad_out.astype(jnp.bfloat16)
    down_grad = weight_term(activated, grad_branch)
    grad_active = project_back(grad_branch, w_down)
    gate_sigmoid = jax.nn.sigmoid(gate_values)
    grad_gate = (
        grad_active * up_values * gate_sigmoid * (1.0 + gate_values * (1.0 - gate_sigmoid))
    ).astype(jnp.bfloat16)
    grad_up = (grad_active * gate_values * gate_sigmoid).astype(jnp.bfloat16)
    gate_grad = weight_term(normed_two, grad_gate)
    up_grad = weight_term(normed_two, grad_up)
    grad_normed_two = head_back(project_back(grad_gate, w_gate) + project_back(grad_up, w_up))
    grad_norm_two, ffn_gain_grad = norm_backward(grad_normed_two, hidden_one, inverse_two, norm_ffn)
    grad_hidden = grad_out + grad_norm_two
    grad_attn = grad_hidden.astype(jnp.bfloat16)
    output_grad = weight_term(attended_low, grad_attn)
    grad_attended = (
        project_back(grad_attn, w_output)
        .astype(jnp.bfloat16)
        .reshape(seq_count, count_of_rows, head_count, head_width)
    )
    row_delta = jnp.transpose(
        jnp.sum(grad_attended.astype(jnp.float32) * attended, axis=-1), (0, 2, 1)
    )
    query_rot, key_rot, value_mix = attend_back_gather(
        queries, grad_attended, log_normalizer, row_delta, key_rows, mixed, segments, query_places
    )
    query_low = (
        rotate_back(query_rot, cosine, sine_table)
        .astype(jnp.bfloat16)
        .reshape(seq_count, count_of_rows, -1)
    )
    key_low = (
        rotate_back(key_rot, cosine, sine_table)
        .astype(jnp.bfloat16)
        .reshape(seq_count, count_of_rows, -1)
    )
    value_mix = value_mix.reshape(seq_count, count_of_rows, -1)
    if mixes:
        value_low = (0.5 * value_mix).astype(jnp.bfloat16)
        passed_on = 0.5 * value_mix
    else:
        value_low = (value_mix + value_extra).astype(jnp.bfloat16)
        passed_on = value_extra
    query_grad = weight_term(normed, query_low)
    key_grad = weight_term(normed, key_low)
    value_grad = weight_term(normed, value_low)
    grad_normed = head_back(
        project_back(query_low, w_query)
        + project_back(key_low, w_key)
        + project_back(value_low, w_value)
    )
    grad_norm_one, attn_gain_grad = norm_backward(grad_normed, stream, inverse_one, norm_attn)
    grad_stream = grad_hidden + grad_norm_one
    grad_terms = (
        attn_gain_grad,
        query_grad,
        key_grad,
        value_grad,
        output_grad,
        ffn_gain_grad,
        gate_grad,
        up_grad,
        down_grad,
    )
    return (grad_stream, passed_on, grad_terms)


def on_device(
    inputs,
    segment_ids,
    norm_attn_one,
    query_one,
    key_one,
    value_one,
    output_one,
    norm_ffn_one,
    gate_one,
    up_one,
    down_one,
    norm_attn_two,
    query_two,
    key_two,
    value_two,
    output_two,
    norm_ffn_two,
    gate_two,
    up_two,
    down_two,
    cotangent,
):
    gathered = (
        lax.all_gather(norm_attn_one, ("dp", "ctx"), axis=0, tiled=True),
        lax.all_gather(query_one, ("dp", "ctx"), axis=0, tiled=True),
        lax.all_gather(key_one, ("dp", "ctx"), axis=0, tiled=True),
        lax.all_gather(value_one, ("dp", "ctx"), axis=0, tiled=True),
        lax.all_gather(output_one, ("dp", "ctx"), axis=1, tiled=True),
        lax.all_gather(norm_ffn_one, ("dp", "ctx"), axis=0, tiled=True),
        lax.all_gather(gate_one, ("dp", "ctx"), axis=0, tiled=True),
        lax.all_gather(up_one, ("dp", "ctx"), axis=0, tiled=True),
        lax.all_gather(down_one, ("dp", "ctx"), axis=1, tiled=True),
        lax.all_gather(norm_attn_two, ("dp", "ctx"), axis=0, tiled=True),
        lax.all_gather(query_two, ("dp", "ctx"), axis=0, tiled=True),
        lax.all_gather(key_two, ("dp", "ctx"), axis=0, tiled=True),
        lax.all_gather(value_two, ("dp", "ctx"), axis=0, tiled=True),
        lax.all_gather(output_two, ("dp", "ctx"), axis=1, tiled=True),
        lax.all_gather(norm_ffn_two, ("dp", "ctx"), axis=0, tiled=True),
        lax.all_gather(gate_two, ("dp", "ctx"), axis=0, tiled=True),
        lax.all_gather(up_two, ("dp", "ctx"), axis=0, tiled=True),
        lax.all_gather(down_two, ("dp", "ctx"), axis=1, tiled=True),
    )
    weights_one = gathered[:9]
    weights_two = gathered[9:]
    seq_count, count_of_rows, model_width = inputs.shape
    query_places = lax.axis_index("ctx") * count_of_rows + jnp.arange(
        count_of_rows, dtype=jnp.int32
    )
    cosine, sine_table = rotary_tables(query_places[0], count_of_rows)
    layer_one, saved_one, first_values = forward_layer(
        inputs.astype(jnp.float32), None, weights_one, segment_ids, cosine, sine_table, query_places
    )
    layer_two, saved_two, unused = forward_layer(
        layer_one, first_values, weights_two, segment_ids, cosine, sine_table, query_places
    )
    grad_middle, value_extra, grads_two = backward_layer(
        cotangent.astype(jnp.float32),
        None,
        saved_two,
        weights_two,
        segment_ids,
        cosine,
        sine_table,
        query_places,
        True,
    )
    grad_input, unused_extra, grads_one = backward_layer(
        grad_middle,
        value_extra,
        saved_one,
        weights_one,
        segment_ids,
        cosine,
        sine_table,
        query_places,
        False,
    )
    totals = (
        lax.psum_scatter(
            grads_one[0].astype(jnp.bfloat16), ("dp", "ctx"), scatter_dimension=0, tiled=True
        ).astype(jnp.float32),
        lax.psum_scatter(
            grads_one[1].astype(jnp.bfloat16), ("dp", "ctx"), scatter_dimension=0, tiled=True
        ).astype(jnp.float32),
        lax.psum_scatter(
            grads_one[2].astype(jnp.bfloat16), ("dp", "ctx"), scatter_dimension=0, tiled=True
        ).astype(jnp.float32),
        lax.psum_scatter(
            grads_one[3].astype(jnp.bfloat16), ("dp", "ctx"), scatter_dimension=0, tiled=True
        ).astype(jnp.float32),
        lax.psum_scatter(
            grads_one[4].astype(jnp.bfloat16), ("dp", "ctx"), scatter_dimension=1, tiled=True
        ).astype(jnp.float32),
        lax.psum_scatter(
            grads_one[5].astype(jnp.bfloat16), ("dp", "ctx"), scatter_dimension=0, tiled=True
        ).astype(jnp.float32),
        lax.psum_scatter(
            grads_one[6].astype(jnp.bfloat16), ("dp", "ctx"), scatter_dimension=0, tiled=True
        ).astype(jnp.float32),
        lax.psum_scatter(
            grads_one[7].astype(jnp.bfloat16), ("dp", "ctx"), scatter_dimension=0, tiled=True
        ).astype(jnp.float32),
        lax.psum_scatter(
            grads_one[8].astype(jnp.bfloat16), ("dp", "ctx"), scatter_dimension=1, tiled=True
        ).astype(jnp.float32),
        lax.psum_scatter(
            grads_two[0].astype(jnp.bfloat16), ("dp", "ctx"), scatter_dimension=0, tiled=True
        ).astype(jnp.float32),
        lax.psum_scatter(
            grads_two[1].astype(jnp.bfloat16), ("dp", "ctx"), scatter_dimension=0, tiled=True
        ).astype(jnp.float32),
        lax.psum_scatter(
            grads_two[2].astype(jnp.bfloat16), ("dp", "ctx"), scatter_dimension=0, tiled=True
        ).astype(jnp.float32),
        lax.psum_scatter(
            grads_two[3].astype(jnp.bfloat16), ("dp", "ctx"), scatter_dimension=0, tiled=True
        ).astype(jnp.float32),
        lax.psum_scatter(
            grads_two[4].astype(jnp.bfloat16), ("dp", "ctx"), scatter_dimension=1, tiled=True
        ).astype(jnp.float32),
        lax.psum_scatter(
            grads_two[5].astype(jnp.bfloat16), ("dp", "ctx"), scatter_dimension=0, tiled=True
        ).astype(jnp.float32),
        lax.psum_scatter(
            grads_two[6].astype(jnp.bfloat16), ("dp", "ctx"), scatter_dimension=0, tiled=True
        ).astype(jnp.float32),
        lax.psum_scatter(
            grads_two[7].astype(jnp.bfloat16), ("dp", "ctx"), scatter_dimension=0, tiled=True
        ).astype(jnp.float32),
        lax.psum_scatter(
            grads_two[8].astype(jnp.bfloat16), ("dp", "ctx"), scatter_dimension=1, tiled=True
        ).astype(jnp.float32),
    )
    return (
        layer_one.astype(jnp.bfloat16),
        layer_two.astype(jnp.bfloat16),
        grad_input,
        totals[0],
        totals[1],
        totals[2],
        totals[3],
        totals[4],
        totals[5],
        totals[6],
        totals[7],
        totals[8],
        totals[9],
        totals[10],
        totals[11],
        totals[12],
        totals[13],
        totals[14],
        totals[15],
        totals[16],
        totals[17],
    )


def solution(mesh):
    placed = (
        P("dp", "ctx", None),
        P("dp", None),
        P(("dp", "ctx")),
        P(("dp", "ctx"), "mp"),
        P(("dp", "ctx"), "mp"),
        P(("dp", "ctx"), "mp"),
        P("mp", ("dp", "ctx")),
        P(("dp", "ctx")),
        P(("dp", "ctx"), "mp"),
        P(("dp", "ctx"), "mp"),
        P("mp", ("dp", "ctx")),
        P(("dp", "ctx")),
        P(("dp", "ctx"), "mp"),
        P(("dp", "ctx"), "mp"),
        P(("dp", "ctx"), "mp"),
        P("mp", ("dp", "ctx")),
        P(("dp", "ctx")),
        P(("dp", "ctx"), "mp"),
        P(("dp", "ctx"), "mp"),
        P("mp", ("dp", "ctx")),
        P("dp", "ctx", None),
    )
    return jax.shard_map(
        on_device,
        mesh=mesh,
        in_specs=placed,
        out_specs=(
            P("dp", "ctx", None),
            P("dp", "ctx", None),
            P("dp", "ctx", None),
            P(("dp", "ctx")),
            P(("dp", "ctx"), "mp"),
            P(("dp", "ctx"), "mp"),
            P(("dp", "ctx"), "mp"),
            P("mp", ("dp", "ctx")),
            P(("dp", "ctx")),
            P(("dp", "ctx"), "mp"),
            P(("dp", "ctx"), "mp"),
            P("mp", ("dp", "ctx")),
            P(("dp", "ctx")),
            P(("dp", "ctx"), "mp"),
            P(("dp", "ctx"), "mp"),
            P(("dp", "ctx"), "mp"),
            P("mp", ("dp", "ctx")),
            P(("dp", "ctx")),
            P(("dp", "ctx"), "mp"),
            P(("dp", "ctx"), "mp"),
            P("mp", ("dp", "ctx")),
        ),
        check_vma=False,
    )
```

profile of v0, /device:TPU:0, one launch (start us, length us, event | category | flops | bytes accessed | tf_op | source)
XLA Modules:
  0.0 2297.2 jit_solution(6562493565726094202)
XLA Ops:
  71.3 32.6 %all_gather.73 = bf16[1024,256]{0,1:T(8,128)(2,1)S(1)} all-gather(bf16[128,256]{0,1:T(8,128)(2,1)S(1)} %copy.121), channel_id=1, replica_groups=mesh['dp'=2,'ctx'=4,'mp'=4] {'dp','ctx'}, dimensions={0}, use_global_device_ids=true | all-gather | bytes 589824 | tf_op jit(solution)/shard_map/all_gather | solution.py:429
  143.1 39.5 %all_gather.76 = bf16[256,1024]{1,0:T(8,128)(2,1)S(1)} all-gather(bf16[256,128]{1,0:T(8,128)(2,1)} %param.43), channel_id=1, replica_groups=mesh['dp'=2,'ctx'=4,'mp'=4] {'dp','ctx'}, dimensions={1}, use_global_device_ids=true | all-gather | bytes 589824 | tf_op jit(solution)/shard_map/all_gather | solution.py:432
  312.4 36.7 %all-gather.23.cloned.1.call-done = bf16[704,1024]{1,0:T(8,128)(2,1)} async-done(((bf16[704,128]{1,0:T(8,128)(2,1)}), bf16[704,1024]{1,0:T(8,128)(2,1)}) %all-gather.23.cloned.1.call-update) | async-done | bytes 1441808 | tf_op jit(solution)/shard_map/all_gather | solution.py:436
  411.5 33.4 %all_gather.84 = bf16[1024,256]{0,1:T(8,128)(2,1)S(1)} all-gather(bf16[128,256]{0,1:T(8,128)(2,1)S(1)} %copy.125), channel_id=1, replica_groups=mesh['dp'=2,'ctx'=4,'mp'=4] {'dp','ctx'}, dimensions={0}, use_global_device_ids=true | all-gather | bytes 589824 | tf_op jit(solution)/shard_map/all_gather | solution.py:438
  444.9 34.0 %all_gather.82 = bf16[1024,256]{0,1:T(8,128)(2,1)S(1)} all-gather(bf16[128,256]{0,1:T(8,128)(2,1)S(1)} %copy.124), channel_id=1, replica_groups=mesh['dp'=2,'ctx'=4,'mp'=4] {'dp','ctx'}, dimensions={0}, use_global_device_ids=true | all-gather | bytes 589824 | tf_op jit(solution)/shard_map/all_gather | solution.py:439
  481.7 34.9 %all_gather.87 = bf16[256,1024]{1,0:T(8,128)(2,1)S(1)} all-gather(bf16[256,128]{1,0:T(8,128)(2,1)S(1)} %copy-done.88), channel_id=1, replica_groups=mesh['dp'=2,'ctx'=4,'mp'=4] {'dp','ctx'}, dimensions={1}, use_global_device_ids=true | all-gather | bytes 589824 | tf_op jit(solution)/shard_map/all_gather | solution.py:441
  648.0 38.3 %all-gather.33.cloned.1.call-done = bf16[704,1024]{1,0:T(8,128)(2,1)} async-done(((bf16[704,128]{1,0:T(8,128)(2,1)}), bf16[704,1024]{1,0:T(8,128)(2,1)}) %all-gather.33.cloned.1.call-update) | async-done | bytes 1441808 | tf_op jit(solution)/shard_map/all_gather | solution.py:445
  699.9 49.5 %all-reduce.20.cloned.1.call-done = bf16[4,256,1024]{2,1,0:T(8,128)(2,1)} async-done(((bf16[4,256,1024]{2,1,0:T(8,128)(2,1)}), bf16[4,256,1024]{2,1,0:T(8,128)(2,1)}) %all-reduce.20.cloned.1.call-update) | async-done | bytes 2097168 | tf_op jit(solution)/shard_map/psum | solution.py:38
  763.4 41.7 %while.62 = (s32[]{:T(128)}, f32[4,256,4,64]{1,3,2,0:T(8,128)}, bf16[4,1024,4,64]{1,3,2,0:T(8,128)(2,1)}, bf16[4,1024,4,64]{1,3,2,0:T(8,128)(2,1)}, s32[2]{0:T(1...) while((s32[]{:T(128)}, f32[4,256,4,64]{1,3,2,0:T(8,128)}, ...), condition=%wide.region_26.27_spmd.clone, body=%wide.region_23.26_spmd.clone.sunk | while | flops 1366688512 | bytes 105730624 | solution.py:246
  765.3 37.9 %conditional.14 = ((f32[4,256,4,64]{1,3,2,0:T(8,128)}, bf16[4,1024,4,64]{1,3,2,0:T(8,128)(2,1)}, bf16[4,1024,4,64]{1,3,2,0:T(8,128)(2,1)})) conditional(s32[]{:T(128)} %convert_element_type.711, (f32[4,256,4,64]{1,3,2,0:T(8,128)}, bf16[4,1024,4,64]{1,3,2,0:T(8,128)(2,1)}, bf16[4,1024,4,64]{1,3,2,0:T(8,128)(2,1)}) %tuple.161, (s32[]{:T(128)}, ...), branch_computations={%region_24.24_spmd, %region_25.25_spmd} | conditional | flops 1366688512 | bytes 105729264 | solution.py:244
  809.8 76.1 %reduce-scatter.35.cloned.1.call-done = bf16[4,256,256]{1,2,0:T(8,128)(2,1)} async-done(((bf16[4,1024,256]{1,2,0:T(8,128)(2,1)}), bf16[4,256,256]{1,2,0:T(8,128)(2,1)}) %reduce-scatter.35.cloned.1.call-update) | async-done | bytes 524304 | tf_op jit(solution)/shard_map/reduce_scatter | solution.py:251
  893.6 38.3 %reduce-scatter.37.cloned.1.call-done = bf16[4,256,256]{2,1,0:T(8,128)(2,1)} async-done(((bf16[4,1024,256]{2,1,0:T(8,128)(2,1)}), bf16[4,256,256]{2,1,0:T(8,128)(2,1)}) %reduce-scatter.37.cloned.1.call-update) | async-done | bytes 524304 | tf_op jit(solution)/shard_map/reduce_scatter | solution.py:257
  937.7 50.8 %all-reduce.22.cloned.1.call-done = bf16[4,256,1024]{2,1,0:T(8,128)(2,1)} async-done(((bf16[4,256,1024]{2,1,0:T(8,128)(2,1)}), bf16[4,256,1024]{2,1,0:T(8,128)(2,1)}) %all-reduce.22.cloned.1.call-update) | async-done | bytes 2097168 | tf_op jit(solution)/shard_map/psum | solution.py:38
  1006.9 51.5 %all-reduce.24.cloned.1.call-done = bf16[4,256,1024]{2,1,0:T(8,128)(2,1)} async-done(((bf16[4,256,1024]{2,1,0:T(8,128)(2,1)}), bf16[4,256,1024]{2,1,0:T(8,128)(2,1)}) %all-reduce.24.cloned.1.call-update) | async-done | bytes 2097168 | tf_op jit(solution)/shard_map/psum | solution.py:38
  1076.3 43.6 %while.63 = (s32[]{:T(128)}, f32[4,256,4,64]{1,3,2,0:T(8,128)}, bf16[4,1024,4,64]{1,3,2,0:T(8,128)(2,1)}, bf16[4,1024,4,64]{1,3,2,0:T(8,128)(2,1)}, s32[2]{0:T(1...) while((s32[]{:T(128)}, f32[4,256,4,64]{1,3,2,0:T(8,128)}, ...), condition=%wide.region_37.38_spmd.clone, body=%wide.region_34.37_spmd.clone.sunk | while | flops 1366688512 | bytes 114119264 | solution.py:246
  1078.2 39.8 %conditional.15 = ((f32[4,256,4,64]{1,3,2,0:T(8,128)}, bf16[4,1024,4,64]{1,3,2,0:T(8,128)(2,1)}, bf16[4,1024,4,64]{1,3,2,0:T(8,128)(2,1)})) conditional(s32[]{:T(128)} %convert_element_type.712, (f32[4,256,4,64]{1,3,2,0:T(8,128)}, bf16[4,1024,4,64]{1,3,2,0:T(8,128)(2,1)}, bf16[4,1024,4,64]{1,3,2,0:T(8,128)(2,1)}) %tuple.164, (s32[]{:T(128)}, ...), branch_computations={%region_35.35_spmd, %region_36.36_spmd} | conditional | flops 1366688512 | bytes 114117904 | solution.py:244
  1215.1 32.8 %reduce-scatter.41.cloned.1.call-done = bf16[4,256,256]{2,1,0:T(8,128)(2,1)} async-done(((bf16[4,1024,256]{2,1,0:T(8,128)(2,1)}), bf16[4,256,256]{2,1,0:T(8,128)(2,1)}) %reduce-scatter.41.cloned.1.call-update) | async-done | bytes 524304 | tf_op jit(solution)/shard_map/reduce_scatter | solution.py:257
  1258.3 54.0 %reduce-scatter.63.cloned.1.call-done = bf16[128,256]{1,0:T(8,128)(2,1)} async-done(((bf16[1024,256]{1,0:T(8,128)(2,1)}), bf16[128,256]{1,0:T(8,128)(2,1)}) %reduce-scatter.63.cloned.1.call-update) | async-done | bytes 65552
  1314.0 66.0 %reduce-scatter.65.cloned.1.call-done = bf16[128,704]{1,0:T(8,128)(2,1)} async-done(((bf16[1024,704]{1,0:T(8,128)(2,1)}), bf16[128,704]{1,0:T(8,128)(2,1)}) %reduce-scatter.65.cloned.1.call-update) | async-done | bytes 180240
  1381.8 65.3 %reduce-scatter.67.cloned.1.call-done = bf16[128,704]{1,0:T(8,128)(2,1)} async-done(((bf16[1024,704]{1,0:T(8,128)(2,1)}), bf16[128,704]{1,0:T(8,128)(2,1)}) %reduce-scatter.67.cloned.1.call-update) | async-done | bytes 180240
  1449.0 65.7 %reduce-scatter.69.cloned.1.call-done = bf16[128,704]{1,0:T(8,128)(2,1)} async-done(((bf16[1024,704]{1,0:T(8,128)(2,1)}), bf16[128,704]{1,0:T(8,128)(2,1)}) %reduce-scatter.69.cloned.1.call-update) | async-done | bytes 180240
  1516.5 62.4 %reduce-scatter.49.cloned.1.call-done = bf16[128,256]{1,0:T(8,128)(2,1)} async-done(((bf16[1024,256]{1,0:T(8,128)(2,1)}), bf16[128,256]{1,0:T(8,128)(2,1)}) %reduce-scatter.49.cloned.1.call-update) | async-done | bytes 65552 | tf_op jit(solution)/shard_map/reduce_scatter | solution.py:513
  1580.4 63.0 %reduce-scatter.51.cloned.1.call-done = bf16[128,256]{1,0:T(8,128)(2,1)} async-done(((bf16[1024,256]{1,0:T(8,128)(2,1)}), bf16[128,256]{1,0:T(8,128)(2,1)}) %reduce-scatter.51.cloned.1.call-update) | async-done | bytes 65552 | tf_op jit(solution)/shard_map/reduce_scatter | solution.py:516
  1644.9 62.8 %reduce-scatter.53.cloned.1.call-done = bf16[128,256]{1,0:T(8,128)(2,1)} async-done(((bf16[1024,256]{1,0:T(8,128)(2,1)}), bf16[128,256]{1,0:T(8,128)(2,1)}) %reduce-scatter.53.cloned.1.call-update) | async-done | bytes 65552 | tf_op jit(solution)/shard_map/reduce_scatter | solution.py:519
  1709.2 63.1 %reduce-scatter.55.cloned.1.call-done = bf16[128,256]{1,0:T(8,128)(2,1)} async-done(((bf16[1024,256]{1,0:T(8,128)(2,1)}), bf16[128,256]{1,0:T(8,128)(2,1)}) %reduce-scatter.55.cloned.1.call-update) | async-done | bytes 65552
  1774.0 65.6 %reduce-scatter.57.cloned.1.call-done = bf16[128,704]{1,0:T(8,128)(2,1)} async-done(((bf16[1024,704]{1,0:T(8,128)(2,1)}), bf16[128,704]{1,0:T(8,128)(2,1)}) %reduce-scatter.57.cloned.1.call-update) | async-done | bytes 180240
  1841.5 65.6 %reduce-scatter.59.cloned.1.call-done = bf16[128,704]{1,0:T(8,128)(2,1)} async-done(((bf16[1024,704]{1,0:T(8,128)(2,1)}), bf16[128,704]{1,0:T(8,128)(2,1)}) %reduce-scatter.59.cloned.1.call-update) | async-done | bytes 180240
  1909.0 65.3 %reduce-scatter.61.cloned.1.call-done = bf16[128,704]{1,0:T(8,128)(2,1)} async-done(((bf16[1024,704]{1,0:T(8,128)(2,1)}), bf16[128,704]{1,0:T(8,128)(2,1)}) %reduce-scatter.61.cloned.1.call-update) | async-done | bytes 180240
  1976.1 62.6 %reduce-scatter.43.cloned.1.call-done = bf16[128,256]{1,0:T(8,128)(2,1)} async-done(((bf16[1024,256]{1,0:T(8,128)(2,1)}), bf16[128,256]{1,0:T(8,128)(2,1)}) %reduce-scatter.43.cloned.1.call-update) | async-done | bytes 65552 | tf_op jit(solution)/shard_map/reduce_scatter | solution.py:486
  2040.3 62.7 %reduce-scatter.45.cloned.1.call-done = bf16[128,256]{1,0:T(8,128)(2,1)} async-done(((bf16[1024,256]{1,0:T(8,128)(2,1)}), bf16[128,256]{1,0:T(8,128)(2,1)}) %reduce-scatter.45.cloned.1.call-update) | async-done | bytes 65552 | tf_op jit(solution)/shard_map/reduce_scatter | solution.py:489
  2104.4 63.1 %reduce-scatter.47.cloned.1.call-done = bf16[128,256]{1,0:T(8,128)(2,1)} async-done(((bf16[1024,256]{1,0:T(8,128)(2,1)}), bf16[128,256]{1,0:T(8,128)(2,1)}) %reduce-scatter.47.cloned.1.call-update) | async-done | bytes 65552 | tf_op jit(solution)/shard_map/reduce_scatter | solution.py:492
  2169.0 86.3 %all-reduce.26.cloned.1.call-done = (bf16[4,256,1024]{2,1,0:T(8,128)(2,1)}, bf16[4,256,1024]{2,1,0:T(8,128)(2,1)}) async-done(((bf16[4,256,1024]{2,1,0:T(8,128)(2,1)}, bf16[4,256,1024]{2,1,0:T(8,128)(2,1)}), (bf16[4,256,1024]{2,1,0:T(8,128)(2,1)}, bf16[4,256,1024]{2,1,0:T(8,128)(2,1)})) %all-reduce.26.cloned.1.call-update) | async-done | bytes 4194320 | tf_op jit(solution)/shard_map/psum | solution.py:34
  (542 shorter events, 787.3 us)
Async XLA Ops:
  8.0 174.6 %all-gather.17.cloned.1.call-start = ((), (), s32[]{:S(2)}) async-start(), calls=%async_computation.19 | async-start | bytes 2621440 | tf_op jit(solution)/shard_map/all_gather | solution.py:145
  69.5 120.7 %all-gather.15.cloned.1.call-start = ((), (), s32[]{:S(2)}) async-start(), calls=%async_computation.18 | async-start | bytes 2621440 | tf_op jit(solution)/shard_map/all_gather | solution.py:144
  140.0 127.8 %all-reduce.14.cloned.1.call-start = ((), (), s32[]{:S(2)}) async-start(), calls=%async_computation.20 | async-start | bytes 4194304 | tf_op jit(solution)/shard_map/psum | solution.py:34
  210.1 139.0 %all-gather.23.cloned.1.call-start = ((), (), s32[]{:S(2)}) async-start(), calls=%async_computation.23 | async-start | bytes 1622016 | tf_op jit(solution)/shard_map/all_gather | solution.py:436
  210.7 193.5 %all-reduce.16.cloned.1.call-start = ((), (), s32[]{:S(2)}) async-start(), calls=%async_computation.24 | async-start | bytes 4194304 | tf_op jit(solution)/shard_map/psum | solution.py:34
  354.1 162.6 %all-gather.27.cloned.1.call-start = ((), (), s32[]{:S(2)}) async-start(), calls=%async_computation.26 | async-start | bytes 2621440 | tf_op jit(solution)/shard_map/all_gather | solution.py:145
  411.2 119.3 %all-gather.25.cloned.1.call-start = ((), (), s32[]{:S(2)}) async-start(), calls=%async_computation.25 | async-start | bytes 2621440 | tf_op jit(solution)/shard_map/all_gather | solution.py:144
  481.6 122.8 %all-reduce.18.cloned.1.call-start = ((), (), s32[]{:S(2)}) async-start(), calls=%async_computation.27 | async-start | bytes 4194304 | tf_op jit(solution)/shard_map/psum | solution.py:34
  546.6 96.2 %all-gather.31.cloned.1.call-start = ((), (), s32[]{:S(2)}) async-start(), calls=%async_computation.29 | async-start | bytes 1622016 | tf_op jit(solution)/shard_map/all_gather | solution.py:444
  547.3 139.0 %all-gather.33.cloned.1.call-start = ((), (), s32[]{:S(2)}) async-start(), calls=%async_computation.30 | async-start | bytes 1622016 | tf_op jit(solution)/shard_map/all_gather | solution.py:445
  548.1 201.4 %all-reduce.20.cloned.1.call-start = ((), (), s32[]{:S(2)}) async-start(), calls=%async_computation.31 | async-start | bytes 4194304 | tf_op jit(solution)/shard_map/psum | solution.py:38
  699.7 186.2 %reduce-scatter.35.cloned.1.call-start = ((), (), s32[]{:S(2)}) async-start(), calls=%async_computation.32 | async-start | bytes 2621440 | tf_op jit(solution)/shard_map/reduce_scatter | solution.py:251
  805.2 126.7 %reduce-scatter.37.cloned.1.call-start = ((), (), s32[]{:S(2)}) async-start(), calls=%async_computation.33 | async-start | bytes 2621440 | tf_op jit(solution)/shard_map/reduce_scatter | solution.py:257
  809.3 179.1 %all-reduce.22.cloned.1.call-start = ((), (), s32[]{:S(2)}) async-start(), calls=%async_computation.34 | async-start | bytes 4194304 | tf_op jit(solution)/shard_map/psum | solution.py:38
  937.6 120.8 %all-reduce.24.cloned.1.call-start = ((), (), s32[]{:S(2)}) async-start(), calls=%async_computation.35 | async-start | bytes 4194304 | tf_op jit(solution)/shard_map/psum | solution.py:38
  1006.8 195.6 %reduce-scatter.39.cloned.1.call-start = ((), (), s32[]{:S(2)}) async-start(), calls=%async_computation.36 | async-start | bytes 2621440 | tf_op jit(solution)/shard_map/reduce_scatter | solution.py:251
  1120.0 127.9 %reduce-scatter.41.cloned.1.call-start = ((), (), s32[]{:S(2)}) async-start(), calls=%async_computation.37 | async-start | bytes 2621440 | tf_op jit(solution)/shard_map/reduce_scatter | solution.py:257
  1124.1 188.3 %reduce-scatter.63.cloned.1.call-start = ((), (), s32[]{:S(2)}) async-start(), calls=%async_computation.48 | async-start | bytes 589824
  1128.0 251.9 %reduce-scatter.65.cloned.1.call-start = ((), (), s32[]{:S(2)}) async-start(), calls=%async_computation.49 | async-start | bytes 1769472
  1133.6 313.5 %reduce-scatter.67.cloned.1.call-start = ((), (), s32[]{:S(2)}) async-start(), calls=%async_computation.50 | async-start | bytes 1769472
  1139.0 375.7 %reduce-scatter.69.cloned.1.call-start = ((), (), s32[]{:S(2)}) async-start(), calls=%async_computation.51 | async-start | bytes 1769472
  1146.5 432.4 %reduce-scatter.49.cloned.1.call-start = ((), (), s32[]{:S(2)}) async-start(), calls=%async_computation.41 | async-start | bytes 589824 | tf_op jit(solution)/shard_map/reduce_scatter | solution.py:513
  1149.8 493.6 %reduce-scatter.51.cloned.1.call-start = ((), (), s32[]{:S(2)}) async-start(), calls=%async_computation.42 | async-start | bytes 589824 | tf_op jit(solution)/shard_map/reduce_scatter | solution.py:516
  1153.1 554.6 %reduce-scatter.53.cloned.1.call-start = ((), (), s32[]{:S(2)}) async-start(), calls=%async_computation.43 | async-start | bytes 589824 | tf_op jit(solution)/shard_map/reduce_scatter | solution.py:519
  1156.4 616.0 %reduce-scatter.55.cloned.1.call-start = ((), (), s32[]{:S(2)}) async-start(), calls=%async_computation.44 | async-start | bytes 589824
  1160.4 679.2 %reduce-scatter.57.cloned.1.call-start = ((), (), s32[]{:S(2)}) async-start(), calls=%async_computation.45 | async-start | bytes 1769472
  1165.7 741.4 %reduce-scatter.59.cloned.1.call-start = ((), (), s32[]{:S(2)}) async-start(), calls=%async_computation.46 | async-start | bytes 1769472
  1171.0 803.2 %reduce-scatter.61.cloned.1.call-start = ((), (), s32[]{:S(2)}) async-start(), calls=%async_computation.47 | async-start | bytes 1769472
  1178.8 859.9 %reduce-scatter.43.cloned.1.call-start = ((), (), s32[]{:S(2)}) async-start(), calls=%async_computation.38 | async-start | bytes 589824 | tf_op jit(solution)/shard_map/reduce_scatter | solution.py:486
  1207.3 895.6 %reduce-scatter.45.cloned.1.call-start = ((), (), s32[]{:S(2)}) async-start(), calls=%async_computation.39 | async-start | bytes 589824 | tf_op jit(solution)/shard_map/reduce_scatter | solution.py:489
  1210.1 957.5 %reduce-scatter.47.cloned.1.call-start = ((), (), s32[]{:S(2)}) async-start(), calls=%async_computation.40 | async-start | bytes 589824 | tf_op jit(solution)/shard_map/reduce_scatter | solution.py:492
  1250.8 1004.6 %all-reduce.26.cloned.1.call-start = ((), (), s32[]{:S(2)}) async-start(), calls=%async_computation.52 | async-start | bytes 8388608 | tf_op jit(solution)/shard_map/psum | solution.py:34
  (118 other events, 2599.6 us)
Sparse Core Ops, SparseCore 0:
  69.6 56.8 all-gather.16
  140.1 50.0 all-gather.14
  209.0 58.7 all-reduce.13
  354.2 49.5 all-reduce.15
  411.3 60.7 all-gather.26
  481.8 48.6 all-gather.24
  546.0 58.4 all-reduce.17
  699.8 49.5 all-reduce.19
  805.3 80.4 reduce-scatter.34
  888.7 43.1 reduce-scatter.36
  937.7 50.6 all-reduce.21
  1006.9 51.4 all-reduce.23
  1120.1 82.2 reduce-scatter.38
  1204.6 43.1 reduce-scatter.40
  1251.1 61.2 reduce-scatter.62
  1316.0 63.8 reduce-scatter.64
  1383.2 63.8 reduce-scatter.66
  1450.8 63.8 reduce-scatter.68
  1518.0 60.8 reduce-scatter.48
  1582.5 60.8 reduce-scatter.50
  1646.7 60.9 reduce-scatter.52
  1711.4 60.9 reduce-scatter.54
  1775.8 63.7 reduce-scatter.56
  1843.3 63.7 reduce-scatter.58
  1910.5 63.7 reduce-scatter.60
  1977.8 60.8 reduce-scatter.42
  2041.9 60.9 reduce-scatter.44
  2106.6 60.8 reduce-scatter.46
  2170.6 84.7 all-reduce.25
Sparse Core Ops, SparseCore 1:
  211.6 50.6 all-gather.18
  264.3 41.3 all-gather.20
  307.7 41.3 all-gather.22
  548.8 50.3 all-gather.28
  601.4 41.3 all-gather.30
  645.0 41.3 all-gather.32
where the time goes:
time: 2310 us; the launch traced here: 2300 us
  waiting for transfers between devices  1500 us (65%)
  blocking collectives  388 us (17%)
  matrix products  175 us (8%)
  local copies, waits for them, and re-layouts  113 us (5%)
  other arithmetic  86.7 us (4%)
    unnamed x43, waiting for transfers between devices  515 us
    psum x3, waiting for transfers between devices, head_back(): return lax.psum(partial_sum.astype(jnp.bfloat16), 'mp').astype(jnp.float32)  152 us
    psum x4, waiting for transfers between devices, head_total(): return lax.psum(partial_sum.astype(jnp.bfloat16), 'mp').astype(jnp.float32)  145 us
    reduce_scatter x2, waiting for transfers between devices, attend_back_gather(): lax.psum_scatter(key_grad.reshape(seq_count, length, -1).astype(jnp.bfloa...  99.6 us
    reduce_scatter x2, waiting for transfers between devices, attend_back_gather(): lax.psum_scatter(value_grad.reshape(seq_count, length, -1).astype(jnp.bfl...  71.1 us
    reduce_scatter x1, waiting for transfers between devices, on_device(): lax.psum_scatter(grads_one[3].astype(jnp.bfloat16), ('dp', 'ctx'), scatte...  63.1 us
    reduce_scatter x1, waiting for transfers between devices, on_device(): lax.psum_scatter(grads_two[2].astype(jnp.bfloat16), ('dp', 'ctx'), scatte...  63 us
    reduce_scatter x1, waiting for transfers between devices, on_device(): lax.psum_scatter(grads_two[3].astype(jnp.bfloat16), ('dp', 'ctx'), scatte...  62.8 us
  transfers between devices with their start and end apart: 35, of which 30 were waited for; matrix products, arithmetic and copies ran while one was open for 7% of the time, Pallas kernels for 0%

commit v1 on v0

--- a/solution.py
+++ b/solution.py
@@ -1,9 +1,14 @@
+import functools
 import math
 
 import jax
 import jax.numpy as jnp
 from jax import lax
+from jax.experimental import pallas as pl
+from jax.experimental.pallas import tpu as pltpu
 from jax.sharding import PartitionSpec as P
+
+MESH = pl.DeviceIdType.MESH
 
 HEAD_DIM = 64
 
@@ -30,12 +35,82 @@
     )
 
 
+def head_sum_kernel(
+    chunks, x_ref, o_ref, near, half_sum, far, send_a, recv_a, send_b, recv_b, send_c, recv_c
+):
+    dp, ctx, mp = (lax.axis_index(name) for name in ("dp", "ctx", "mp"))
+    side = lax.rem(mp, 2)
+    pair = (dp, ctx, mp + 1 - 2 * side)
+    cross = (dp, ctx, lax.rem(mp + 2, 4))
+    barrier = pltpu.get_barrier_semaphore()
+    for peer in (pair, cross):
+        pl.semaphore_signal(barrier, inc=1, device_id=peer, device_id_type=MESH)
+    pl.semaphore_wait(barrier, 2)
+    rows = x_ref.shape[0] // chunks
+    half = rows // 2
+
+    def copy(source, target, send, recv, i, peer):
+        return pltpu.make_async_remote_copy(
+            src_ref=source,
+            dst_ref=target,
+            send_sem=send.at[i],
+            recv_sem=recv.at[i],
+            device_id=peer,
+            device_id_type=MESH,
+        )
+
+    def first(i):
+        theirs = x_ref.at[pl.ds(i * rows + (1 - side) * half, half)]
+        return copy(theirs, near.at[i], send_a, recv_a, i, pair)
+
+    def second(i):
+        return copy(half_sum.at[i], far.at[i], send_b, recv_b, i, cross)
+
+    def third(i):
+        mine = o_ref.at[pl.ds(i * rows + side * half, half)]
+        return copy(mine, mine, send_c, recv_c, i, pair)
+
+    for i in range(chunks):
+        first(i).start()
+    for i in range(chunks):
+        first(i).wait()
+        mine = x_ref[pl.ds(i * rows + side * half, half)].astype(jnp.float32)
+        half_sum[i] = (mine + near[i].astype(jnp.float32)).astype(jnp.bfloat16)
+        second(i).start()
+    for i in range(chunks):
+        second(i).wait()
+        total = half_sum[i].astype(jnp.float32) + far[i].astype(jnp.float32)
+        o_ref[pl.ds(i * rows + side * half, half)] = total.astype(jnp.bfloat16)
+        third(i).start()
+    for i in range(chunks):
+        third(i).wait()
+
+
+def head_sum(partial_sum, number):
+    flat = partial_sum.astype(jnp.bfloat16).reshape(-1, partial_sum.shape[-1])
+    count, width = flat.shape
+    chunks = 4
+    half = count // chunks // 2
+    total = pl.pallas_call(
+        functools.partial(head_sum_kernel, chunks),
+        out_shape=jax.ShapeDtypeStruct((count, width), jnp.bfloat16),
+        in_specs=[pl.BlockSpec(memory_space=pltpu.VMEM)],
+        out_specs=pl.BlockSpec(memory_space=pltpu.VMEM),
+        scratch_shapes=[pltpu.VMEM((chunks, half, width), jnp.bfloat16)] * 3
+        + [pltpu.SemaphoreType.DMA((chunks,))] * 6,
+        compiler_params=pltpu.CompilerParams(
+            collective_id=0, has_side_effects=True, vmem_limit_bytes=32 << 20
+        ),
+    )(flat)
+    return total.reshape(partial_sum.shape).astype(jnp.float32)
+
+
 def head_total(partial_sum):
-    return lax.psum(partial_sum.astype(jnp.bfloat16), "mp").astype(jnp.float32)
+    return head_sum(partial_sum, 0)
 
 
 def head_back(partial_sum):
-    return lax.psum(partial_sum.astype(jnp.bfloat16), "mp").astype(jnp.float32)
+    return head_sum(partial_sum, 0)
 
 
 def rotary_tables(first_place, count_of_rows):
@@ -424,25 +499,57 @@
     down_two,
     cotangent,
 ):
-    gathered = (
-        lax.all_gather(norm_attn_one, ("dp", "ctx"), axis=0, tiled=True),
-        lax.all_gather(query_one, ("dp", "ctx"), axis=0, tiled=True),
-        lax.all_gather(key_one, ("dp", "ctx"), axis=0, tiled=True),
-        lax.all_gather(value_one, ("dp", "ctx"), axis=0, tiled=True),
-        lax.all_gather(output_one, ("dp", "ctx"), axis=1, tiled=True),
-        lax.all_gather(norm_ffn_one, ("dp", "ctx"), axis=0, tiled=True),
-        lax.all_gather(gate_one, ("dp", "ctx"), axis=0, tiled=True),
-        lax.all_gather(up_one, ("dp", "ctx"), axis=0, tiled=True),
-        lax.all_gather(down_one, ("dp", "ctx"), axis=1, tiled=True),
-        lax.all_gather(norm_attn_two, ("dp", "ctx"), axis=0, tiled=True),
-        lax.all_gather(query_two, ("dp", "ctx"), axis=0, tiled=True),
-        lax.all_gather(key_two, ("dp", "ctx"), axis=0, tiled=True),
-        lax.all_gather(value_two, ("dp", "ctx"), axis=0, tiled=True),
-        lax.all_gather(output_two, ("dp", "ctx"), axis=1, tiled=True),
-        lax.all_gather(norm_ffn_two, ("dp", "ctx"), axis=0, tiled=True),
-        lax.all_gather(gate_two, ("dp", "ctx"), axis=0, tiled=True),
-        lax.all_gather(up_two, ("dp", "ctx"), axis=0, tiled=True),
-        lax.all_gather(down_two, ("dp", "ctx"), axis=1, tiled=True),
+    def gather_layer(gain_attn, query, key, value, output, gain_ffn, gate, up, down):
+        both = ("dp", "ctx")
+        packed = jnp.concatenate([query, key, value, output.T, gate, up, down.T], axis=1)
+        whole = lax.all_gather(packed, both, axis=0, tiled=True)
+        gains = lax.all_gather(jnp.stack([gain_attn, gain_ffn]), both, axis=1, tiled=True)
+        cuts = []
+        for part in (query, key, value, output.T, gate, up, down.T):
+            cuts.append((cuts[-1] if cuts else 0) + part.shape[1])
+        w_q, w_k, w_v, w_o, w_g, w_u, w_d = jnp.split(whole, cuts[:-1], axis=1)
+        return (gains[0], w_q, w_k, w_v, w_o.T, gains[1], w_g, w_u, w_d.T)
+
+    def scatter_layer(grads, outs):
+        both = ("dp", "ctx")
+        gain_attn, query, key, value, output, gain_ffn, gate, up, down = grads
+        pieces = [query, key, value, output.T, gate, up, down.T]
+        packed = jnp.concatenate([part.astype(jnp.bfloat16) for part in pieces], axis=1)
+        mine = lax.psum_scatter(packed, both, scatter_dimension=0, tiled=True)
+        gains = lax.psum_scatter(
+            jnp.stack([gain_attn, gain_ffn]).astype(jnp.bfloat16),
+            both,
+            scatter_dimension=1,
+            tiled=True,
+        ).astype(jnp.float32)
+        cuts = []
+        for part in pieces:
+            cuts.append((cuts[-1] if cuts else 0) + part.shape[1])
+        g_q, g_k, g_v, g_o, g_g, g_u, g_d = (
+            part.astype(jnp.float32) for part in jnp.split(mine, cuts[:-1], axis=1)
+        )
+        return (gains[0], g_q, g_k, g_v, g_o.T, gains[1], g_g, g_u, g_d.T)
+
+    gathered = gather_layer(
+        norm_attn_one,
+        query_one,
+        key_one,
+        value_one,
+        output_one,
+        norm_ffn_one,
+        gate_one,
+        up_one,
+        down_one,
+    ) + gather_layer(
+        norm_attn_two,
+        query_two,
+        key_two,
+        value_two,
+        output_two,
+        norm_ffn_two,
+        gate_two,
+        up_two,
+        down_two,
     )
     weights_one = gathered[:9]
     weights_two = gathered[9:]
@@ -479,62 +586,7 @@
         query_places,
         False,
     )
-    totals = (
-        lax.psum_scatter(
-            grads_one[0].astype(jnp.bfloat16), ("dp", "ctx"), scatter_dimension=0, tiled=True
-        ).astype(jnp.float32),
-        lax.psum_scatter(
-            grads_one[1].astype(jnp.bfloat16), ("dp", "ctx"), scatter_dimension=0, tiled=True
-        ).astype(jnp.float32),
-        lax.psum_scatter(
-            grads_one[2].astype(jnp.bfloat16), ("dp", "ctx"), scatter_dimension=0, tiled=True
-        ).astype(jnp.float32),
-        lax.psum_scatter(
-            grads_one[3].astype(jnp.bfloat16), ("dp", "ctx"), scatter_dimension=0, tiled=True
-        ).astype(jnp.float32),
-        lax.psum_scatter(
-            grads_one[4].astype(jnp.bfloat16), ("dp", "ctx"), scatter_dimension=1, tiled=True
-        ).astype(jnp.float32),
-        lax.psum_scatter(
-            grads_one[5].astype(jnp.bfloat16), ("dp", "ctx"), scatter_dimension=0, tiled=True
-        ).astype(jnp.float32),
-        lax.psum_scatter(
-            grads_one[6].astype(jnp.bfloat16), ("dp", "ctx"), scatter_dimension=0, tiled=True
-        ).astype(jnp.float32),
-        lax.psum_scatter(
-            grads_one[7].astype(jnp.bfloat16), ("dp", "ctx"), scatter_dimension=0, tiled=True
-        ).astype(jnp.float32),
-        lax.psum_scatter(
-            grads_one[8].astype(jnp.bfloat16), ("dp", "ctx"), scatter_dimension=1, tiled=True
-        ).astype(jnp.float32),
-        lax.psum_scatter(
-            grads_two[0].astype(jnp.bfloat16), ("dp", "ctx"), scatter_dimension=0, tiled=True
-        ).astype(jnp.float32),
-        lax.psum_scatter(
-            grads_two[1].astype(jnp.bfloat16), ("dp", "ctx"), scatter_dimension=0, tiled=True
-        ).astype(jnp.float32),
-        lax.psum_scatter(
-            grads_two[2].astype(jnp.bfloat16), ("dp", "ctx"), scatter_dimension=0, tiled=True
-        ).astype(jnp.float32),
-        lax.psum_scatter(
-            grads_two[3].astype(jnp.bfloat16), ("dp", "ctx"), scatter_dimension=0, tiled=True
-        ).astype(jnp.float32),
-        lax.psum_scatter(
-            grads_two[4].astype(jnp.bfloat16), ("dp", "ctx"), scatter_dimension=1, tiled=True
-        ).astype(jnp.float32),
-        lax.psum_scatter(
-            grads_two[5].astype(jnp.bfloat16), ("dp", "ctx"), scatter_dimension=0, tiled=True
-        ).astype(jnp.float32),
-        lax.psum_scatter(
-            grads_two[6].astype(jnp.bfloat16), ("dp", "ctx"), scatter_dimension=0, tiled=True
-        ).astype(jnp.float32),
-        lax.psum_scatter(
-            grads_two[7].astype(jnp.bfloat16), ("dp", "ctx"), scatter_dimension=0, tiled=True
-        ).astype(jnp.float32),
-        lax.psum_scatter(
-            grads_two[8].astype(jnp.bfloat16), ("dp", "ctx"), scatter_dimension=1, tiled=True
-        ).astype(jnp.float32),
-    )
+    totals = scatter_layer(grads_one, None) + scatter_layer(grads_two, None)
     return (
         layer_one.astype(jnp.bfloat16),
         layer_two.astype(jnp.bfloat16),

time: 2310 us -> 1370 us (0.59)
  waiting for transfers between devices: 1500 us -> 718 us
  blocking collectives: 388 us -> 40.1 us
  Pallas kernels: 0 us -> 227 us
  other arithmetic: 86.7 us -> 47.8 us
  local copies, waits for them, and re-layouts: 113 us -> 141 us
  matrix products: 175 us -> 151 us
    reduce_scatter x6 -> x0, waiting for transfers between devices: 377 us -> none  [the longest x1 63.1 us: on_device(): lax.psum_scatter(grads_one[3].astype(jnp.bfloat16), ('dp', 'ctx'), scatte...]
    all_gather x12 -> x2, blocking collectives: 366 us -> 40.1 us  [gather_layer(): lax.all_gather(jnp.stack([gain_attn, gain_ffn]), both, axis=1, tiled=True)]
    psum x7 -> x0, waiting for transfers between devices: 297 us -> none  [the longest x3 152 us: head_back(): return lax.psum(partial_sum.astype(jnp.bfloat16), 'mp').astype(jnp.float32)]
    unnamed x43 -> x18, waiting for transfers between devices: 515 us -> 284 us
    pallas_call x0 -> x8, Pallas kernels: none -> 227 us  [head_sum(): pl.pallas_call(functools.partial(head_sum_kernel, chunks), out_shape=jax....]
    all_gather x2, waiting for transfers between devices: 13.3 us -> 86.1 us  [attend_forward(): key_piece = lax.all_gather(key_rows, 'ctx', axis=1, tiled=True)]
    reduce_scatter x2, waiting for transfers between devices: 99.6 us -> 145 us  [attend_back_gather(): lax.psum_scatter(key_grad.reshape(seq_count, length, -1).astype(jnp.bfloa...]
    all_gather x2, waiting for transfers between devices: 0.02 us -> 38.6 us  [attend_forward(): value_piece = lax.all_gather(value_rows, 'ctx', axis=1, tiled=True)]
  transfers between devices with their start and end apart: 35 -> 14, of which waited for: 30 -> 13; matrix products, arithmetic and copies ran while one was open for 7% -> 12% of each run, Pallas kernels for 0% -> 6%
where the time goes in v1:
time: 1370 us; the launch traced here: 1360 us
  waiting for transfers between devices  718 us (52%)
  Pallas kernels  227 us (17%)
  matrix products  151 us (11%)
  local copies, waits for them, and re-layouts  141 us (10%)
  other arithmetic  47.8 us (3%)
  blocking collectives  40.1 us (3%)
  between operations  17.9 us (1%)
    unnamed x18, waiting for transfers between devices  284 us
    pallas_call x8, Pallas kernels, head_sum(): pl.pallas_call(functools.partial(head_sum_kernel, chunks), out_shape=jax....  227 us
    reduce_scatter x2, waiting for transfers between devices, attend_back_gather(): lax.psum_scatter(key_grad.reshape(seq_count, length, -1).astype(jnp.bfloa...  145 us
    all_gather x2, waiting for transfers between devices, gather_layer(): whole = lax.all_gather(packed, both, axis=0, tiled=True)  92.4 us
    all_gather x2, waiting for transfers between devices, attend_forward(): key_piece = lax.all_gather(key_rows, 'ctx', axis=1, tiled=True)  86.1 us
    reduce_scatter x2, waiting for transfers between devices, attend_back_gather(): lax.psum_scatter(value_grad.reshape(seq_count, length, -1).astype(jnp.bfl...  71.7 us
    unnamed x224, local copies, waits for them, and re-layouts  56.2 us
    dot_general x14, matrix products, project_back(): jnp.einsum('sbe,de->sbd', left_operand, right_operand, preferred_element_...  43.5 us
  transfers between devices with their start and end apart: 14, of which 13 were waited for; matrix products, arithmetic and copies ran while one was open for 12% of the time, Pallas kernels for 6%

profile of v1, /device:TPU:0, one launch (start us, length us, event | category | flops | bytes accessed | tf_op | source)
XLA Modules:
  0.0 1356.3 jit_solution(17727583843867855937)
XLA Ops:
  15.7 22.2 %all_gather.28 = bf16[2,1024]{1,0:T(2,128)(2,1)S(1)} all-gather(bf16[2,128]{1,0:T(2,128)(2,1)S(1)} %pad_maximum_fusion.10), channel_id=1, replica_groups=mesh['dp'=2,'ctx'=4,'mp'=4] {'dp','ctx'}, dimensions={1}, use_global_device_ids=true | all-gather | bytes 4608 | tf_op jit(solution)/shard_map/all_gather | solution.py:506
  38.4 80.9 %all-gather.7.cloned.1.call-done = bf16[1024,3136]{0,1:T(8,128)(2,1)} async-done(((bf16[128,3136]{0,1:T(8,128)(2,1)}), bf16[1024,3136]{0,1:T(8,128)(2,1)}) %all-gather.7.cloned.1.call-update) | async-done | bytes 6422544 | tf_op jit(solution)/shard_map/all_gather | solution.py:505
  142.7 17.9 %all_gather.32 = bf16[2,1024]{1,0:T(2,128)(2,1)S(1)} all-gather(bf16[2,128]{1,0:T(2,128)(2,1)S(1)} %pad_maximum_fusion.11), channel_id=1, replica_groups=mesh['dp'=2,'ctx'=4,'mp'=4] {'dp','ctx'}, dimensions={1}, use_global_device_ids=true | all-gather | bytes 4608 | tf_op jit(solution)/shard_map/all_gather | solution.py:506
  170.6 43.1 %all-gather.9.cloned.1.call-done = bf16[4,1024,256]{1,2,0:T(8,128)(2,1)} async-done(((bf16[4,256,256]{1,2,0:T(8,128)(2,1)}), bf16[4,1024,256]{1,2,0:T(8,128)(2,1)}) %all-gather.9.cloned.1.call-update) | async-done | bytes 2097168 | tf_op jit(solution)/shard_map/all_gather | solution.py:219
  214.9 13.7 %while.60 = (s32[]{:T(128)}, f32[4,4,256]{2,1,0:T(4,128)S(1)}, f32[4,4,256]{2,1,0:T(4,128)S(1)}, f32[4,256,4,64]{1,3,2,0:T(8,128)}, s32[2]{0:T(128)S(1)}, /*inde...) while((s32[]{:T(128)}, f32[4,4,256]{2,1,0:T(4,128)S(1)}, ...), condition=%wide.region_6.7_spmd.clone, body=%wide.region_1.6_spmd.clone.sunk | while | flops 561656576 | bytes 49320400 | solution.py:263
  232.2 28.4 %shard_map.364 = bf16[1024,1024]{1,0:T(8,128)(2,1)S(1)} custom-call(bf16[1024,1024]{1,0:T(8,128)(2,1)S(1)} %bitcast.463), custom_call_target="tpu_custom_call" | custom-call | tf_op jit(solution)/shard_map/pallas_call | solution.py:94
  270.2 28.4 %shard_map.365 = bf16[1024,1024]{1,0:T(8,128)(2,1)S(1)} custom-call(bf16[1024,1024]{1,0:T(8,128)(2,1)S(1)} %bitcast.470), custom_call_target="tpu_custom_call" | custom-call | tf_op jit(solution)/shard_map/pallas_call | solution.py:94
  304.0 11.5 all-gather.13.cloned.1.call-done
  330.0 32.7 %all-gather.17.cloned.1.call-done = bf16[4,1024,256]{2,1,0:T(8,128)(2,1)} async-done(((bf16[4,256,256]{2,1,0:T(8,128)(2,1)}), bf16[4,1024,256]{2,1,0:T(8,128)(2,1)}) %all-gather.17.cloned.1.call-update) | async-done | bytes 2097168 | tf_op jit(solution)/shard_map/all_gather | solution.py:220
  366.7 43.0 %all-gather.15.cloned.1.call-done = bf16[4,1024,256]{1,2,0:T(8,128)(2,1)} async-done(((bf16[4,256,256]{1,2,0:T(8,128)(2,1)}), bf16[4,1024,256]{1,2,0:T(8,128)(2,1)}) %all-gather.15.cloned.1.call-update) | async-done | bytes 2097168 | tf_op jit(solution)/shard_map/all_gather | solution.py:219
  409.8 12.2 while.61
  424.3 28.4 %shard_map.366 = bf16[1024,1024]{1,0:T(8,128)(2,1)S(1)} custom-call(bf16[1024,1024]{1,0:T(8,128)(2,1)S(1)} %bitcast.464), custom_call_target="tpu_custom_call" | custom-call | tf_op jit(solution)/shard_map/pallas_call | solution.py:94
  465.5 28.4 %shard_map.368 = bf16[1024,1024]{1,0:T(8,128)(2,1)S(1)} custom-call(bf16[1024,1024]{1,0:T(8,128)(2,1)S(1)} %bitcast.468), custom_call_target="tpu_custom_call" | custom-call | tf_op jit(solution)/shard_map/pallas_call | solution.py:94
  497.6 28.4 %shard_map.367 = bf16[1024,1024]{1,0:T(8,128)(2,1)S(1)} custom-call(bf16[1024,1024]{1,0:T(8,128)(2,1)S(1)} %bitcast.471), custom_call_target="tpu_custom_call" | custom-call | tf_op jit(solution)/shard_map/pallas_call | solution.py:94
  535.0 42.0 %while.62 = (s32[]{:T(128)}, f32[4,256,4,64]{1,3,2,0:T(8,128)}, bf16[4,1024,4,64]{1,3,2,0:T(8,128)(2,1)}, bf16[4,1024,4,64]{1,3,2,0:T(8,128)(2,1)}, s32[2]{0:T(1...) while((s32[]{:T(128)}, f32[4,256,4,64]{1,3,2,0:T(8,128)}, ...), condition=%wide.region_21.22_spmd.clone, body=%wide.region_18.21_spmd.clone.sunk | while | flops 1366688512 | bytes 105730624 | solution.py:321
  537.1 38.0 %conditional.14 = ((f32[4,256,4,64]{1,3,2,0:T(8,128)}, bf16[4,1024,4,64]{1,3,2,0:T(8,128)(2,1)}, bf16[4,1024,4,64]{1,3,2,0:T(8,128)(2,1)})) conditional(s32[]{:T(128)} %convert_element_type.702, (f32[4,256,4,64]{1,3,2,0:T(8,128)}, bf16[4,1024,4,64]{1,3,2,0:T(8,128)(2,1)}, bf16[4,1024,4,64]{1,3,2,0:T(8,128)(2,1)}) %tuple.178, (s32[]{:T(128)}, ...), branch_computations={%region_19.19_spmd, %region_20.20_spmd} | conditional | flops 1366688512 | bytes 105729264 | solution.py:319
  548.0 10.4 dynamic_update_slice.8
  564.7 10.4 dynamic_update_slice.9
  581.3 82.9 %reduce-scatter.17.cloned.1.call-done = bf16[4,256,256]{1,2,0:T(8,128)(2,1)} async-done(((bf16[4,1024,256]{1,2,0:T(8,128)(2,1)}), bf16[4,256,256]{1,2,0:T(8,128)(2,1)}) %reduce-scatter.17.cloned.1.call-update) | async-done | bytes 524304 | tf_op jit(solution)/shard_map/reduce_scatter | solution.py:326
  674.2 35.6 %reduce-scatter.19.cloned.1.call-done = bf16[4,256,256]{2,1,0:T(8,128)(2,1)} async-done(((bf16[4,1024,256]{2,1,0:T(8,128)(2,1)}), bf16[4,256,256]{2,1,0:T(8,128)(2,1)}) %reduce-scatter.19.cloned.1.call-update) | async-done | bytes 524304 | tf_op jit(solution)/shard_map/reduce_scatter | solution.py:332
  714.3 28.4 %shard_map.369 = bf16[1024,1024]{1,0:T(8,128)(2,1)S(1)} custom-call(bf16[1024,1024]{1,0:T(8,128)(2,1)S(1)} %bitcast.466), custom_call_target="tpu_custom_call" | custom-call | tf_op jit(solution)/shard_map/pallas_call | solution.py:94
  756.0 28.4 %shard_map.370 = bf16[1024,1024]{1,0:T(8,128)(2,1)S(1)} custom-call(bf16[1024,1024]{1,0:T(8,128)(2,1)S(1)} %bitcast.469), custom_call_target="tpu_custom_call" | custom-call | tf_op jit(solution)/shard_map/pallas_call | solution.py:94
  795.9 42.0 %while.63 = (s32[]{:T(128)}, f32[4,256,4,64]{1,3,2,0:T(8,128)}, bf16[4,1024,4,64]{1,3,2,0:T(8,128)(2,1)}, bf16[4,1024,4,64]{1,3,2,0:T(8,128)(2,1)}, s32[2]{0:T(1...) while((s32[]{:T(128)}, f32[4,256,4,64]{1,3,2,0:T(8,128)}, ...), condition=%wide.region_30.31_spmd.clone, body=%wide.region_27.30_spmd.clone.sunk | while | flops 1366688512 | bytes 105730624 | solution.py:321
  798.0 38.0 %conditional.15 = ((f32[4,256,4,64]{1,3,2,0:T(8,128)}, bf16[4,1024,4,64]{1,3,2,0:T(8,128)(2,1)}, bf16[4,1024,4,64]{1,3,2,0:T(8,128)(2,1)})) conditional(s32[]{:T(128)} %convert_element_type.703, (f32[4,256,4,64]{1,3,2,0:T(8,128)}, bf16[4,1024,4,64]{1,3,2,0:T(8,128)(2,1)}, bf16[4,1024,4,64]{1,3,2,0:T(8,128)(2,1)}) %tuple.181, (s32[]{:T(128)}, ...), branch_computations={%region_28.28_spmd, %region_29.29_spmd} | conditional | flops 1366688512 | bytes 105729264 | solution.py:319
  808.9 10.4 dynamic_update_slice.10
  825.6 10.4 dynamic_update_slice.11
  856.1 61.7 %reduce-scatter.21.cloned.1.call-done = bf16[4,256,256]{1,2,0:T(8,128)(2,1)} async-done(((bf16[4,1024,256]{1,2,0:T(8,128)(2,1)}), bf16[4,256,256]{1,2,0:T(8,128)(2,1)}) %reduce-scatter.21.cloned.1.call-update) | async-done | bytes 524304 | tf_op jit(solution)/shard_map/reduce_scatter | solution.py:326
  927.2 36.1 %reduce-scatter.23.cloned.1.call-done = bf16[4,256,256]{2,1,0:T(8,128)(2,1)} async-done(((bf16[4,1024,256]{2,1,0:T(8,128)(2,1)}), bf16[4,256,256]{2,1,0:T(8,128)(2,1)}) %reduce-scatter.23.cloned.1.call-update) | async-done | bytes 524304 | tf_op jit(solution)/shard_map/reduce_scatter | solution.py:332
  967.8 28.4 %shard_map.371 = bf16[1024,1024]{1,0:T(8,128)(2,1)S(1)} custom-call(bf16[1024,1024]{1,0:T(8,128)(2,1)S(1)} %bitcast.467), custom_call_target="tpu_custom_call" | custom-call | tf_op jit(solution)/shard_map/pallas_call | solution.py:94
  1046.9 44.9 %reduce-scatter.25.cloned.1.call-done = bf16[128,2]{1,0:T(8,128)(2,1)} async-done(((bf16[1024,2]{1,0:T(8,128)(2,1)}), bf16[128,2]{1,0:T(8,128)(2,1)}) %reduce-scatter.25.cloned.1.call-update) | async-done | bytes 528
  1093.2 122.9 %reduce-scatter.31.cloned.1.call-done = bf16[128,3136]{1,0:T(8,128)(2,1)} async-done(((bf16[1024,3136]{1,0:T(8,128)(2,1)}), bf16[128,3136]{1,0:T(8,128)(2,1)}) %reduce-scatter.31.cloned.1.call-update) | async-done | bytes 802832
  1224.6 116.3 %reduce-scatter.27.cloned.1.call-done = bf16[128,3136]{1,0:T(8,128)(2,1)} async-done(((bf16[1024,3136]{1,0:T(8,128)(2,1)}), bf16[128,3136]{1,0:T(8,128)(2,1)}) %reduce-scatter.27.cloned.1.call-update) | async-done | bytes 802832
  (486 shorter events, 324.1 us)
Async XLA Ops:
  7.2 112.1 %all-gather.7.cloned.1.call-start = ((), (), s32[]{:S(2)}) async-start(), calls=%async_computation.8 | async-start | bytes 7225344 | tf_op jit(solution)/shard_map/all_gather | solution.py:505
  14.9 151.7 %all-gather.11.cloned.1.call-start = ((), (), s32[]{:S(2)}) async-start(), calls=%async_computation.10 | async-start | bytes 2621440 | tf_op jit(solution)/shard_map/all_gather | solution.py:220
  38.4 87.3 %copy-start.76 = (f32[4,256]{1,0:T(4,128)}, f32[4,256]{1,0:T(4,128)S(1)}, u32[]{:S(2)}) copy-start(f32[4,256]{1,0:T(4,128)S(1)} %add_rsqrt_fusion.3) | copy-start | bytes 12292
  38.4 87.3 %copy-start.78 = (f32[1,1024]{1,0:T(1,128)}, f32[1,1024]{1,0:T(1,128)S(1)}, u32[]{:S(2)}) copy-start(f32[1,1024]{1,0:T(1,128)S(1)} %get-tuple-element.929) | copy-start | bytes 12292
  38.4 223.0 %copy-start.74 = (f32[1,1024]{1,0:T(1,128)}, f32[1,1024]{1,0:T(1,128)S(1)}, u32[]{:S(2)}) copy-start(f32[1,1024]{1,0:T(1,128)S(1)} %get-tuple-element.930) | copy-start | bytes 12292
  122.3 91.5 %all-gather.9.cloned.1.call-start = ((), (), s32[]{:S(2)}) async-start(), calls=%async_computation.9 | async-start | bytes 2621440 | tf_op jit(solution)/shard_map/all_gather | solution.py:219
  123.8 199.1 %copy-start.61 = (f32[256,32]{0,1:T(8,128)}, f32[256,32]{0,1:T(8,128)S(1)}, u32[]{:S(2)}) copy-start(f32[256,32]{0,1:T(8,128)S(1)} %get-tuple-element.931) | copy-start | bytes 98308
  123.8 199.1 %copy-start.63 = (f32[256,32]{0,1:T(8,128)}, f32[256,32]{0,1:T(8,128)S(1)}, u32[]{:S(2)}) copy-start(f32[256,32]{0,1:T(8,128)S(1)} %get-tuple-element.932) | copy-start | bytes 98308
  127.6 33.0 %copy-start.55 = (s32[4,1024]{1,0:T(4,128)S(1)}, s32[4,1024]{1,0:T(4,128)}, u32[]{:S(2)}) copy-start(s32[4,1024]{1,0:T(4,128)} %param.38) | copy-start | bytes 49156
  128.7 32.0 %copy-start.58 = (bf16[4,256,4,32]{1,3,2,0:T(8,128)(2,1)S(1)}, bf16[4,256,4,32]{1,3,2,0:T(8,128)(2,1)}, u32[]{:S(2)}) copy-start(bf16[4,256,4,32]{1,3,2,0:T(8,128)(2,1)} %get-tuple-element.902) | copy-start | bytes 786436
  129.5 185.9 %all-gather.13.cloned.1.call-start = ((), (), s32[]{:S(2)}) async-start(), calls=%async_computation.11 | async-start | bytes 7225344 | tf_op jit(solution)/shard_map/all_gather | solution.py:505
  140.7 222.0 %all-gather.17.cloned.1.call-start = ((), (), s32[]{:S(2)}) async-start(), calls=%async_computation.13 | async-start | bytes 2621440 | tf_op jit(solution)/shard_map/all_gather | solution.py:220
  160.7 141.3 %copy-start.70 = (f32[1,1024]{1,0:T(1,128)}, f32[1,1024]{1,0:T(1,128)S(1)}, u32[]{:S(2)}) copy-start(f32[1,1024]{1,0:T(1,128)S(1)} %get-tuple-element.928) | copy-start | bytes 12292
  228.7 32.0 %copy-start.7 = (bf16[4,256,4,64]{1,3,2,0:T(8,128)(2,1)}, bf16[4,256,4,64]{1,3,2,0:T(8,128)(2,1)S(1)}, u32[]{:S(2)}) copy-start(bf16[4,256,4,64]{1,3,2,0:T(8,128)(2,1)S(1)} %get-tuple-element.1529) | copy-start | bytes 1572868
  228.7 32.0 %copy-start.33 = (f32[4,4,256]{2,1,0:T(4,128)}, f32[4,4,256]{2,1,0:T(4,128)S(1)}, u32[]{:S(2)}) copy-start(f32[4,4,256]{2,1,0:T(4,128)S(1)} %get-tuple-element.489) | copy-start | bytes 49156
  260.7 38.0 %copy-start = (bf16[1024,1024]{1,0:T(8,128)(2,1)}, bf16[1024,1024]{1,0:T(8,128)(2,1)S(1)}, u32[]{:S(2)}) copy-start(bf16[1024,1024]{1,0:T(8,128)(2,1)S(1)} %shard_map.364) | copy-start | bytes 6291460
  318.4 91.3 %all-gather.15.cloned.1.call-start = ((), (), s32[]{:S(2)}) async-start(), calls=%async_computation.12 | async-start | bytes 2621440 | tf_op jit(solution)/shard_map/all_gather | solution.py:219
  324.8 339.4 %reduce-scatter.17.cloned.1.call-start = ((), (), s32[]{:S(2)}) async-start(), calls=%async_computation.14 | async-start | bytes 2621440 | tf_op jit(solution)/shard_map/reduce_scatter | solution.py:326
  461.6 34.2 %copy-start.92 = (bf16[4,256,704]{1,2,0:T(8,128)(2,1)}, bf16[4,256,704]{1,2,0:T(8,128)(2,1)S(1)}, u32[]{:S(2)}) copy-start(bf16[4,256,704]{1,2,0:T(8,128)(2,1)S(1)} %get-tuple-element.886) | copy-start | bytes 4325380
  577.1 88.3 %copy-start.25 = (f32[4,256,4,64]{1,3,2,0:T(8,128)S(1)}, f32[4,256,4,64]{1,3,2,0:T(8,128)}, u32[]{:S(2)}) copy-start(f32[4,256,4,64]{1,3,2,0:T(8,128)} %get-tuple-element.486) | copy-start | bytes 3145732
  577.1 88.3 %copy-start.62 = (f32[256,32]{0,1:T(8,128)S(1)}, f32[256,32]{0,1:T(8,128)}, u32[]{:S(2)}) copy-start(f32[256,32]{0,1:T(8,128)} %copy-done.61) | copy-start | bytes 98308
  577.1 88.3 %copy-start.64 = (f32[256,32]{0,1:T(8,128)S(1)}, f32[256,32]{0,1:T(8,128)}, u32[]{:S(2)}) copy-start(f32[256,32]{0,1:T(8,128)} %copy-done.63) | copy-start | bytes 98308
  577.1 132.7 %reduce-scatter.19.cloned.1.call-start = ((), (), s32[]{:S(2)}) async-start(), calls=%async_computation.15 | async-start | bytes 2621440 | tf_op jit(solution)/shard_map/reduce_scatter | solution.py:332
  581.2 336.6 %reduce-scatter.21.cloned.1.call-start = ((), (), s32[]{:S(2)}) async-start(), calls=%async_computation.16 | async-start | bytes 2621440 | tf_op jit(solution)/shard_map/reduce_scatter | solution.py:326
  709.8 33.0 %copy-start.69 = (f32[4,256]{1,0:T(4,128)S(1)}, f32[4,256]{1,0:T(4,128)}, u32[]{:S(2)}) copy-start(f32[4,256]{1,0:T(4,128)} %copy-done.68) | copy-start | bytes 12292
  709.8 33.0 %copy-start.71 = (f32[1,1024]{1,0:T(1,128)S(1)}, f32[1,1024]{1,0:T(1,128)}, u32[]{:S(2)}) copy-start(f32[1,1024]{1,0:T(1,128)} %copy-done.70) | copy-start | bytes 12292
  837.9 125.4 %reduce-scatter.23.cloned.1.call-start = ((), (), s32[]{:S(2)}) async-start(), calls=%async_computation.17 | async-start | bytes 2621440 | tf_op jit(solution)/shard_map/reduce_scatter | solution.py:332
  842.1 198.7 %reduce-scatter.29.cloned.1.call-start = ((), (), s32[]{:S(2)}) async-start(), calls=%async_computation.20 | async-start | bytes 294912
  853.3 65.7 %copy-start.22 = (f32[4,256,4,64]{1,3,2,0:T(8,128)S(1)}, f32[4,256,4,64]{1,3,2,0:T(8,128)}, u32[]{:S(2)}) copy-start(f32[4,256,4,64]{1,3,2,0:T(8,128)} %get-tuple-element.490) | copy-start | bytes 3145732
  856.1 235.8 %reduce-scatter.25.cloned.1.call-start = ((), (), s32[]{:S(2)}) async-start(), calls=%async_computation.18 | async-start | bytes 294912
  998.7 217.4 %reduce-scatter.31.cloned.1.call-start = ((), (), s32[]{:S(2)}) async-start(), calls=%async_computation.21 | async-start | bytes 7372800
  1013.0 327.9 %reduce-scatter.27.cloned.1.call-start = ((), (), s32[]{:S(2)}) async-start(), calls=%async_computation.19 | async-start | bytes 7372800
  (86 other events, 658.7 us)
Sparse Core Ops, SparseCore 0:
  15.1 104.2 all-gather.6
  122.4 44.1 all-gather.10
  168.8 44.9 all-gather.8
  215.6 99.8 all-gather.12
  318.6 44.1 all-gather.16
  364.7 44.9 all-gather.14
  577.2 86.9 reduce-scatter.16
  666.6 43.1 reduce-scatter.18
  838.0 79.7 reduce-scatter.20
  920.1 43.1 reduce-scatter.22
  967.2 60.5 reduce-scatter.28
  1031.6 60.2 reduce-scatter.24
  1095.4 120.6 reduce-scatter.30
  1220.0 120.7 reduce-scatter.26

commit v2 on v1

--- a/solution.py
+++ b/solution.py
@@ -1,5 +1,6 @@
 import functools
 import math
+from types import SimpleNamespace
 
 import jax
 import jax.numpy as jnp
@@ -612,6 +613,951 @@
     )
 
 
+class Call:
+    def __init__(self, number):
+        self.number = number
+        self.operands, self.in_names, self.in_specs = [], [], []
+        self.out_names, self.out_shapes, self.out_specs = [], [], []
+        self.scratch_names, self.scratch = [], []
+        self.scratch_bytes = 0
+        self.far = False
+
+    def take(self, name, array, space=pltpu.VMEM):
+        self.in_names.append(name)
+        self.operands.append(array)
+        self.in_specs.append(pl.BlockSpec(memory_space=space))
+
+    def give(self, name, shape, dtype, space=pltpu.VMEM):
+        self.out_names.append(name)
+        self.out_shapes.append(jax.ShapeDtypeStruct(shape, dtype))
+        self.out_specs.append(pl.BlockSpec(memory_space=space))
+
+    def hold(self, name, shape, dtype):
+        self.scratch_names.append(name)
+        self.scratch.append(pltpu.VMEM(shape, dtype))
+        padded = shape[:-2] + (-(-shape[-2] // 16) * 16, -(-shape[-1] // 128) * 128)
+        self.scratch_bytes += math.prod(padded) * jnp.dtype(dtype).itemsize
+
+    def flags(self, name, count):
+        self.scratch_names.append(name)
+        self.scratch.append(pltpu.SemaphoreType.DMA((count,)))
+
+    def run(self, body):
+        names = self.in_names + self.out_names + self.scratch_names
+
+        def kernel(*refs):
+            body(SimpleNamespace(**dict(zip(names, refs))))
+
+        results = pl.pallas_call(
+            kernel,
+            out_shape=tuple(self.out_shapes),
+            in_specs=self.in_specs,
+            out_specs=tuple(self.out_specs),
+            scratch_shapes=self.scratch,
+            compiler_params=pltpu.CompilerParams(
+                collective_id=self.number,
+                has_side_effects=True,
+                vmem_limit_bytes=self.scratch_bytes + (14 << 20),
+            ),
+        )(*self.operands)
+        return SimpleNamespace(**dict(zip(self.out_names, results)))
+
+
+class Place:
+    def __init__(self):
+        self.dp, self.ctx, self.mp = (lax.axis_index(a) for a in ("dp", "ctx", "mp"))
+        self.ctx_size = lax.axis_size("ctx")
+        self.side = lax.rem(self.mp, 2)
+        self.pair = (self.dp, self.ctx, self.mp + 1 - 2 * self.side)
+        self.cross = (self.dp, self.ctx, lax.rem(self.mp + 2, 4))
+        self.other = (1 - self.dp, self.ctx, self.mp)
+
+    def ahead(self, step):
+        return lax.rem(self.ctx + step, self.ctx_size)
+
+    def behind(self, step):
+        return lax.rem(self.ctx + self.ctx_size - step, self.ctx_size)
+
+    def along(self, index):
+        return (self.dp, index, self.mp)
+
+    def enter(self, far):
+        peers = [self.pair, self.cross]
+        if far:
+            peers.append(self.other)
+            peers += [self.along(self.ahead(s)) for s in range(1, self.ctx_size)]
+        barrier = pltpu.get_barrier_semaphore()
+        for peer in peers:
+            pl.semaphore_signal(barrier, inc=1, device_id=peer, device_id_type=MESH)
+        pl.semaphore_wait(barrier, len(peers))
+
+
+def remote(source, target, send, recv, peer):
+    return pltpu.make_async_remote_copy(
+        src_ref=source,
+        dst_ref=target,
+        send_sem=send,
+        recv_sem=recv,
+        device_id=peer,
+        device_id_type=MESH,
+    )
+
+
+class HeadSum:
+    def __init__(self, call, blocks, rows, width):
+        self.rows, self.half = rows, rows // 2
+        self.blocks = blocks
+        call.hold("hs_part", (blocks, rows, width), jnp.bfloat16)
+        for name in ("hs_near", "hs_far", "hs_rest"):
+            call.hold(name, (blocks, rows // 2, width), jnp.bfloat16)
+        for name in ("hs_sa", "hs_ra", "hs_sb", "hs_rb", "hs_sc", "hs_rc"):
+            call.flags(name, blocks)
+
+    def bind(self, n, place):
+        self.n, self.place = n, place
+
+    def own(self):
+        return pl.ds(pl.multiple_of(self.place.side * self.half, self.half), self.half)
+
+    def theirs(self):
+        start = (1 - self.place.side) * self.half
+        return pl.ds(pl.multiple_of(start, self.half), self.half)
+
+    def first(self, i):
+        n = self.n
+        source = n.hs_part.at[i, self.theirs()]
+        return remote(source, n.hs_near.at[i], n.hs_sa.at[i], n.hs_ra.at[i], self.place.pair)
+
+    def second(self, i):
+        n = self.n
+        return remote(
+            n.hs_near.at[i], n.hs_far.at[i], n.hs_sb.at[i], n.hs_rb.at[i], self.place.cross
+        )
+
+    def third(self, i):
+        n = self.n
+        return remote(
+            n.hs_far.at[i], n.hs_rest.at[i], n.hs_sc.at[i], n.hs_rc.at[i], self.place.pair
+        )
+
+    def send(self, i, partial_rows):
+        self.n.hs_part[i] = partial_rows.astype(jnp.bfloat16)
+        self.first(i).start()
+
+    def middle(self, i):
+        n = self.n
+        self.first(i).wait()
+        mine = n.hs_part[i, self.own()].astype(jnp.float32)
+        n.hs_near[i] = (mine + n.hs_near[i].astype(jnp.float32)).astype(jnp.bfloat16)
+        self.second(i).start()
+
+    def last(self, i):
+        n = self.n
+        self.second(i).wait()
+        total = n.hs_near[i].astype(jnp.float32) + n.hs_far[i].astype(jnp.float32)
+        n.hs_far[i] = total.astype(jnp.bfloat16)
+        self.third(i).start()
+
+    def total(self, i):
+        n = self.n
+        self.third(i).wait()
+        n.hs_part[i, self.own()] = n.hs_far[i]
+        n.hs_part[i, self.theirs()] = n.hs_rest[i]
+        return n.hs_part[i].astype(jnp.float32)
+
+
+class Gather:
+    def __init__(self, call, name, shard, places):
+        self.name, self.parts = name, lax.axis_size("ctx")
+        call.far = True
+        call.take(name + "_shard", shard, pl.ANY)
+        call.give(name, (places,) + shard.shape, shard.dtype, pl.ANY)
+        for flag, count in (("_l", 1), ("_zs", 0), ("_zr", 0), ("_ys", 1), ("_yr", 1)):
+            call.flags(name + flag, count if flag == "_l" else self.parts)
+        self.steps = self.parts - 1
+
+    def bind(self, n, place):
+        self.place = place
+        get = lambda suffix: getattr(n, self.name + suffix)
+        self.shard, self.whole = get("_shard"), get("")
+        self.l, self.zs, self.zr, self.ys, self.yr = (
+            get(s) for s in ("_l", "_zs", "_zr", "_ys", "_yr")
+        )
+
+    def slot(self, dp, ctx):
+        return self.whole.at[dp * self.parts + ctx]
+
+    def local(self):
+        p = self.place
+        return pltpu.make_async_copy(self.shard, self.slot(p.dp, p.ctx), self.l.at[0])
+
+    def along(self, s):
+        p = self.place
+        target = self.slot(p.dp, p.ctx)
+        return remote(self.shard, target, self.zs.at[s], self.zr.at[s], p.along(p.ahead(s)))
+
+    def across(self, s):
+        p = self.place
+        block = self.slot(p.dp, p.behind(s))
+        source = self.shard if s == 0 else block
+        return remote(source, block, self.ys.at[s], self.yr.at[s], p.other)
+
+    def start(self):
+        for s in range(self.parts - 1, 0, -1):
+            self.along(s).start()
+        self.across(0).start()
+        self.local().start()
+
+    def step(self, k):
+        s = k + 1
+        p = self.place
+        block = self.slot(p.dp, p.behind(s))
+        remote(block, block, self.zs.at[s], self.zr.at[s], p.along(p.ctx)).wait_recv()
+        self.across(s).start()
+
+    def finish(self):
+        p = self.place
+        self.local().wait()
+        for s in range(1, self.parts):
+            self.along(s).wait_send()
+        for s in range(self.parts):
+            self.across(s).wait_send()
+            block = self.slot(1 - p.dp, p.behind(s))
+            remote(block, block, self.ys.at[s], self.yr.at[s], p.other).wait_recv()
+
+
+class Scatter:
+    def __init__(self, call, name, blocks, dtype=jnp.bfloat16):
+        self.name, self.parts = name, lax.axis_size("ctx")
+        places, rows, width = blocks.shape
+        self.dtype = blocks.dtype
+        call.far = True
+        call.take(name + "_in", blocks)
+        call.give(name, (rows, width), jnp.float32)
+        for suffix in ("_yb", "_zb"):
+            call.hold(name + suffix, (self.parts, rows, width), blocks.dtype)
+        for flag in ("_zs", "_zr", "_ys", "_yr"):
+            call.flags(name + flag, self.parts)
+        self.steps = self.parts
+
+    def bind(self, n, place):
+        self.place = place
+        get = lambda suffix: getattr(n, self.name + suffix)
+        self.blocks, self.out = get("_in"), get("")
+        self.yb, self.zb = get("_yb"), get("_zb")
+        self.zs, self.zr, self.ys, self.yr = (get(s) for s in ("_zs", "_zr", "_ys", "_yr"))
+
+    def across(self, s):
+        p = self.place
+        block = self.blocks.at[(1 - p.dp) * self.parts + p.ahead(s)]
+        return remote(block, self.yb.at[s], self.ys.at[s], self.yr.at[s], p.other)
+
+    def along(self, s):
+        p = self.place
+        return remote(
+            self.yb.at[s], self.zb.at[s], self.zs.at[s], self.zr.at[s], p.along(p.ahead(s))
+        )
+
+    def start(self):
+        for s in list(range(self.parts - 1, 0, -1)) + [0]:
+            self.across(s).start()
+
+    def step(self, k):
+        p = self.place
+        s = self.parts - 1 - k
+        self.across(s).wait()
+        mine = self.blocks[p.dp * self.parts + p.ahead(s)].astype(jnp.float32)
+        both = mine + self.yb[s].astype(jnp.float32)
+        if s == 0:
+            self.out[...] = both
+        else:
+            self.yb[s] = both.astype(self.dtype)
+            self.along(s).start()
+
+    def finish(self):
+        total = self.out[...]
+        for s in range(self.parts - 1, 0, -1):
+            self.along(s).wait()
+            total = total + self.zb[s].astype(jnp.float32)
+        self.out[...] = total
+
+
+class Deal:
+    def __init__(self, call, name, blocks):
+        self.name, self.parts = name, lax.axis_size("ctx")
+        self.quarter = blocks.shape[1] // 4
+        call.far = True
+        call.take(name + "_from", blocks, pl.ANY)
+        call.give(name, blocks.shape, blocks.dtype, pl.ANY)
+        call.flags(name + "_l", 1)
+        for flag in ("_zs", "_zr", "_xs", "_xr", "_as", "_ar", "_bs", "_br"):
+            call.flags(name + flag, self.parts)
+        self.steps = 2 * (self.parts - 1)
+
+    def bind(self, n, place):
+        self.place = place
+        get = lambda suffix: getattr(n, self.name + suffix)
+        self.source, self.target, self.l = get("_from"), get(""), get("_l")
+        for flag in ("zs", "zr", "xs", "xr", "as", "ar", "bs", "br"):
+            setattr(self, "f_" + flag, get("_" + flag))
+
+    def rows(self, mp):
+        return pl.ds(pl.multiple_of(mp * self.quarter, self.quarter), self.quarter)
+
+    def local(self):
+        p = self.place
+        return pltpu.make_async_copy(self.source.at[p.ctx], self.target.at[p.ctx], self.l.at[0])
+
+    def along(self, s):
+        p = self.place
+        rows = self.rows(p.mp)
+        return remote(
+            self.source.at[p.ahead(s), rows],
+            self.target.at[p.ctx, rows],
+            self.f_zs.at[s],
+            self.f_zr.at[s],
+            p.along(p.ahead(s)),
+        )
+
+    def piece(self, s, mp, send, recv, peer):
+        ref = self.target.at[self.place.behind(s), self.rows(mp)]
+        return remote(ref, ref, send.at[s], recv.at[s], peer)
+
+    def start(self):
+        for s in range(self.parts - 1, 0, -1):
+            self.along(s).start()
+        self.local().start()
+
+    def step(self, k):
+        p = self.place
+        s = self.parts - 1 - k // 2
+        far = lax.rem(p.mp + 2, 4)
+        if k % 2 == 0:
+            self.piece(s, p.mp, self.f_zs, self.f_zr, p.along(p.ctx)).wait_recv()
+            self.piece(s, p.mp, self.f_xs, self.f_xr, p.cross).start()
+            self.piece(s, p.mp, self.f_as, self.f_ar, p.pair).start()
+        else:
+            self.piece(s, far, self.f_xs, self.f_xr, p.cross).wait_recv()
+            self.piece(s, far, self.f_bs, self.f_br, p.pair).start()
+
+    def finish(self):
+        p = self.place
+        far = lax.rem(p.mp + 2, 4)
+        near = p.mp + 1 - 2 * p.side
+        near_far = lax.rem(near + 2, 4)
+        self.local().wait()
+        for s in range(1, self.parts):
+            self.along(s).wait_send()
+            self.piece(s, p.mp, self.f_xs, self.f_xr, p.cross).wait_send()
+            self.piece(s, p.mp, self.f_as, self.f_ar, p.pair).wait_send()
+            self.piece(s, far, self.f_bs, self.f_br, p.pair).wait_send()
+            self.piece(s, near, self.f_as, self.f_ar, p.pair).wait_recv()
+            self.piece(s, near_far, self.f_bs, self.f_br, p.pair).wait_recv()
+
+
+class Jobs:
+    def __init__(self, jobs):
+        self.jobs = list(jobs)
+        self.queue = []
+        for k in range(max([job.steps for job in self.jobs], default=0)):
+            self.queue += [(job, k) for job in self.jobs if k < job.steps]
+        self.at = 0
+
+    def bind(self, n, place):
+        self.at = 0
+        for job in self.jobs:
+            job.bind(n, place)
+
+    def start(self):
+        for job in self.jobs:
+            job.start()
+
+    def advance(self, share):
+        stop = min(len(self.queue), int(math.ceil(share * len(self.queue))))
+        while self.at < stop:
+            job, k = self.queue[self.at]
+            job.step(k)
+            self.at += 1
+
+    def finish(self):
+        self.advance(1.0)
+        for job in self.jobs:
+            job.finish()
+
+
+def dot_nn(a, b):
+    return lax.dot_general(a, b, (((1,), (0,)), ((), ())), preferred_element_type=jnp.float32)
+
+
+def dot_nt(a, b):
+    return lax.dot_general(a, b, (((1,), (1,)), ((), ())), preferred_element_type=jnp.float32)
+
+
+def dot_tn(a, b):
+    return lax.dot_general(a, b, (((0,), (0,)), ((), ())), preferred_element_type=jnp.float32)
+
+
+def lane_number(width):
+    return lax.broadcasted_iota(jnp.int32, (1, width), 1)
+
+
+def turn(values, cosine, signed_sine, back):
+    width = values.shape[1]
+    half = HEAD_DIM // 2
+    leading = lax.rem(lane_number(width), HEAD_DIM) < half
+    swapped = jnp.where(leading, pltpu.roll(values, width - half, 1), pltpu.roll(values, half, 1))
+    moved = swapped * signed_sine
+    return values * cosine - moved if back else values * cosine + moved
+
+
+BLOCKS = 4
+
+
+def write_bias(n, i, rows, keys):
+    query_at = i * rows + lax.broadcasted_iota(jnp.int32, (rows, 1), 0)
+    key_at = lax.broadcasted_iota(jnp.int32, (1, keys), 1)
+    same = n.seg_col[pl.ds(i * rows, rows), :] == n.seg_row[:, :keys]
+    n.bias[:, :keys] = jnp.where(same & (key_at <= query_at), 0.0, neg_large)
+
+
+def attention_layer(number, x, first_v, wa, gains, which, tables, jobs_of):
+    count, width = x.shape
+    hid = wa.shape[1] // 4
+    heads = hid // HEAD_DIM
+    rows = count // BLOCKS
+    call = Call(number)
+    call.take("x", x)
+    call.take("wa", wa)
+    call.take("gains", gains)
+    for name, table in tables.items():
+        call.take(name, table)
+    if first_v is not None:
+        call.take("first_v", first_v)
+    call.give("x1", (count, width), jnp.float32)
+    call.give("h", (count, width), jnp.bfloat16)
+    for name in ("q", "k", "m", "o"):
+        call.give(name, (count, hid), jnp.bfloat16)
+    call.give("lse", (heads, count, 1), jnp.float32)
+    if first_v is None:
+        call.give("v", (count, hid), jnp.float32)
+    call.hold("bias", (rows, count), jnp.float32)
+    call.hold("acc", (rows, hid), jnp.float32)
+    total = HeadSum(call, BLOCKS, rows, width)
+    jobs = Jobs(jobs_of(call))
+
+    def body(n):
+        place = Place()
+        place.enter(call.far)
+        total.bind(n, place)
+        jobs.bind(n, place)
+        jobs.start()
+        lane = lane_number(hid)
+        for i in range(BLOCKS):
+            at = pl.ds(i * rows, rows)
+            stream = n.x[at, :].astype(jnp.float32)
+            inverse = lax.rsqrt(jnp.mean(stream * stream, axis=-1, keepdims=True) + epsilon)
+            normed = (stream * inverse * n.gains[which : which + 1, :]).astype(jnp.bfloat16)
+            n.h[at, :] = normed
+            projected = dot_nn(normed, n.wa[:, : 3 * hid])
+            cosine, sine = n.cosine[at, :], n.sine[at, :]
+            queries = turn(projected[:, :hid], cosine, sine, False).astype(jnp.bfloat16)
+            n.q[at, :] = queries * jnp.bfloat16(HEAD_DIM**-0.5)
+            n.k[at, :] = turn(projected[:, hid : 2 * hid], cosine, sine, False).astype(jnp.bfloat16)
+            values = projected[:, 2 * hid :]
+            if first_v is None:
+                n.v[at, :] = values
+            else:
+                values = 0.5 * values + 0.5 * n.first_v[at, :]
+            n.m[at, :] = values.astype(jnp.bfloat16)
+            keys = (i + 1) * rows
+            write_bias(n, i, rows, keys)
+
+            def one_head(h, unused):
+                mask = lane // HEAD_DIM == h
+                query = jnp.where(mask, n.q[at, :], jnp.bfloat16(0))
+                scores = dot_nt(query, n.k[:keys, :]) + n.bias[:, :keys]
+                top = jnp.max(scores, axis=-1, keepdims=True)
+                exponent = jnp.exp(scores - top)
+                summed = jnp.sum(exponent, axis=-1, keepdims=True)
+                weighted = dot_nn(exponent.astype(jnp.bfloat16), n.m[:keys, :])
+                n.acc[...] = jnp.where(mask, weighted / summed, n.acc[...])
+                n.lse[h, at, :] = top + jnp.log(summed)
+                return unused
+
+            lax.fori_loop(0, heads, one_head, 0)
+            attended = n.acc[...].astype(jnp.bfloat16)
+            n.o[at, :] = attended
+            total.send(i, dot_nt(attended, n.wa[:, 3 * hid :]))
+            if i:
+                total.middle(i - 1)
+            jobs.advance((i + 1) / (BLOCKS + 1))
+        total.middle(BLOCKS - 1)
+        for i in range(BLOCKS):
+            total.last(i)
+        for i in range(BLOCKS):
+            at = pl.ds(i * rows, rows)
+            n.x1[at, :] = n.x[at, :].astype(jnp.float32) + total.total(i)
+        jobs.finish()
+
+    return call.run(body)
+
+
+def feed_forward_layer(number, x1, gate, up, down, gains, which, jobs_of):
+    count, width = x1.shape
+    units = gate.shape[1]
+    rows = count // BLOCKS
+    call = Call(number)
+    for name, array in (("x1", x1), ("gate", gate), ("up", up), ("down", down), ("gains", gains)):
+        call.take(name, array)
+    call.give("y", (count, width), jnp.float32)
+    call.give("y_low", (count, width), jnp.bfloat16)
+    call.give("h2", (count, width), jnp.bfloat16)
+    for name in ("z", "u", "a"):
+        call.give(name, (count, units), jnp.bfloat16)
+    total = HeadSum(call, BLOCKS, rows, width)
+    jobs = Jobs(jobs_of(call))
+
+    def body(n):
+        place = Place()
+        place.enter(call.far)
+        total.bind(n, place)
+        jobs.bind(n, place)
+        jobs.start()
+        for i in range(BLOCKS):
+            at = pl.ds(i * rows, rows)
+            stream = n.x1[at, :]
+            inverse = lax.rsqrt(jnp.mean(stream * stream, axis=-1, keepdims=True) + epsilon)
+            normed = (stream * inverse * n.gains[which : which + 1, :]).astype(jnp.bfloat16)
+            n.h2[at, :] = normed
+            z = dot_nn(normed, n.gate[...])
+            u = dot_nn(normed, n.up[...])
+            active = (z * lax.logistic(z) * u).astype(jnp.bfloat16)
+            n.z[at, :] = z.astype(jnp.bfloat16)
+            n.u[at, :] = u.astype(jnp.bfloat16)
+            n.a[at, :] = active
+            total.send(i, dot_nt(active, n.down[...]))
+            if i:
+                total.middle(i - 1)
+            jobs.advance((i + 1) / (BLOCKS + 1))
+        total.middle(BLOCKS - 1)
+        for i in range(BLOCKS):
+            total.last(i)
+        for i in range(BLOCKS):
+            at = pl.ds(i * rows, rows)
+            y = n.x1[at, :] + total.total(i)
+            n.y[at, :] = y
+            n.y_low[at, :] = y.astype(jnp.bfloat16)
+        jobs.finish()
+
+    return call.run(body)
+
+
+def norm_back(n, grad, stream, which, at, out, gain_sum):
+    inverse = lax.rsqrt(jnp.mean(stream * stream, axis=-1, keepdims=True) + epsilon)
+    scaled = stream * inverse
+    grad_scaled = grad * n.gains[which : which + 1, :]
+    products = jnp.mean(grad_scaled * scaled, axis=-1, keepdims=True)
+    gain_sum = gain_sum + jnp.sum(grad * scaled, axis=0, keepdims=True)
+    return inverse * (grad_scaled - scaled * products), gain_sum
+
+
+def feed_forward_back(number, gy, x1, saved, gate, up, down, gains, which, jobs_of):
+    count, width = x1.shape
+    units = gate.shape[1]
+    rows = count // BLOCKS
+    call = Call(number)
+    for name, array in (
+        ("gy", gy),
+        ("x1", x1),
+        ("h2", saved.h2),
+        ("z", saved.z),
+        ("u", saved.u),
+        ("a", saved.a),
+        ("gate", gate),
+        ("up", up),
+        ("down", down),
+        ("gains", gains),
+    ):
+        call.take(name, array)
+    call.give("gx1", (count, width), jnp.float32)
+    call.give("gain", (1, width), jnp.float32)
+    for name in ("d_gate", "d_up", "d_down"):
+        call.give(name, (width, units), jnp.bfloat16)
+    call.hold("low", (count, width), jnp.bfloat16)
+    call.hold("gz", (count, units), jnp.bfloat16)
+    call.hold("gu", (count, units), jnp.bfloat16)
+    total = HeadSum(call, BLOCKS, rows, width)
+    jobs = Jobs(jobs_of(call))
+
+    def body(n):
+        place = Place()
+        place.enter(call.far)
+        total.bind(n, place)
+        jobs.bind(n, place)
+        jobs.start()
+        for i in range(BLOCKS):
+            at = pl.ds(i * rows, rows)
+            low = n.gy[at, :].astype(jnp.bfloat16)
+            n.low[at, :] = low
+            ga = dot_nn(low, n.down[...])
+            z = n.z[at, :].astype(jnp.float32)
+            u = n.u[at, :].astype(jnp.float32)
+            sigma = lax.logistic(z)
+            gz = (ga * u * sigma * (1.0 + z * (1.0 - sigma))).astype(jnp.bfloat16)
+            gu = (ga * z * sigma).astype(jnp.bfloat16)
+            n.gz[at, :] = gz
+            n.gu[at, :] = gu
+            total.send(i, dot_nt(gz, n.gate[...]) + dot_nt(gu, n.up[...]))
+            if i:
+                total.middle(i - 1)
+            jobs.advance((i + 1) / (BLOCKS + 3))
+        total.middle(BLOCKS - 1)
+        cols = width // 4
+        for left, right, out in ((n.low, n.a, n.d_down), (n.h2, n.gz, n.d_gate), (n.h2, n.gu, n.d_up)):
+            for j in range(4):
+                part = dot_tn(left[:, j * cols : (j + 1) * cols], right[...])
+                out[j * cols : (j + 1) * cols, :] = part.astype(jnp.bfloat16)
+            jobs.advance((BLOCKS + 1) / (BLOCKS + 3))
+        for i in range(BLOCKS):
+            total.last(i)
+        gain_sum = jnp.zeros((1, width), jnp.float32)
+        for i in range(BLOCKS):
+            at = pl.ds(i * rows, rows)
+            step, gain_sum = norm_back(n, total.total(i), n.x1[at, :], which, at, n.gx1, gain_sum)
+            n.gx1[at, :] = n.gy[at, :].astype(jnp.float32) + step
+        n.gain[...] = gain_sum
+        jobs.finish()
+
+    return call.run(body)
+
+
+def attention_back(number, gx1, x, saved, extra, wa, gains, which, tables, jobs_of):
+    count, width = x.shape
+    hid = wa.shape[1] // 4
+    heads = hid // HEAD_DIM
+    rows = count // BLOCKS
+    call = Call(number)
+    for name, array in (
+        ("gx1", gx1),
+        ("x", x),
+        ("h", saved.h),
+        ("q", saved.q),
+        ("k", saved.k),
+        ("m", saved.m),
+        ("o", saved.o),
+        ("lse", saved.lse),
+        ("wa", wa),
+        ("gains", gains),
+    ):
+        call.take(name, array)
+    for name, table in tables.items():
+        call.take(name, table)
+    if extra is not None:
+        call.take("extra", extra)
+        call.give("gx", (count, width), jnp.bfloat16)
+    else:
+        call.give("gx", (count, width), jnp.float32)
+        call.give("passed", (count, hid), jnp.float32)
+    call.give("gain", (1, width), jnp.float32)
+    call.give("d_wa", (width, 4 * hid), jnp.bfloat16)
+    call.hold("low", (count, width), jnp.bfloat16)
+    call.hold("bias", (rows, count), jnp.float32)
+    call.hold("go", (rows, hid), jnp.bfloat16)
+    call.hold("gq", (rows, hid), jnp.float32)
+    call.hold("gk", (count, hid), jnp.float32)
+    call.hold("gm", (count, hid), jnp.float32)
+    call.hold("g3", (count, 3 * hid), jnp.bfloat16)
+    total = HeadSum(call, BLOCKS, rows, width)
+    jobs = Jobs(jobs_of(call))
+
+    def body(n):
+        place = Place()
+        place.enter(call.far)
+        total.bind(n, place)
+        jobs.bind(n, place)
+        jobs.start()
+        lane = lane_number(hid)
+        n.gk[...] = jnp.zeros_like(n.gk)
+        n.gm[...] = jnp.zeros_like(n.gm)
+        order = list(range(BLOCKS))[::-1]
+        for turn_index, i in enumerate(order):
+            at = pl.ds(i * rows, rows)
+            low = n.gx1[at, :].astype(jnp.bfloat16)
+            n.low[at, :] = low
+            n.go[...] = dot_nn(low, n.wa[:, 3 * hid :]).astype(jnp.bfloat16)
+            keys = (i + 1) * rows
+            write_bias(n, i, rows, keys)
+            n.gq[...] = jnp.zeros_like(n.gq)
+
+            def one_head(h, unused):
+                mask = lane // HEAD_DIM == h
+                zero = jnp.bfloat16(0)
+                query = jnp.where(mask, n.q[at, :], zero)
+                grad = jnp.where(mask, n.go[...], zero)
+                both = grad.astype(jnp.float32) * n.o[at, :].astype(jnp.float32)
+                delta = jnp.sum(both, axis=-1, keepdims=True)
+                scores = dot_nt(query, n.k[:keys, :]) + n.bias[:, :keys]
+                prob = jnp.exp(scores - n.lse[h, at, :])
+                grad_prob = dot_nt(grad, n.m[:keys, :])
+                grad_score = (prob * (grad_prob - delta)).astype(jnp.bfloat16)
+                part = dot_nn(grad_score, n.k[:keys, :])
+                n.gq[...] = jnp.where(mask, part, n.gq[...])
+                n.gk[:keys, :] += dot_tn(grad_score, query)
+                n.gm[:keys, :] += dot_tn(prob.astype(jnp.bfloat16), grad)
+                return unused
+
+            lax.fori_loop(0, heads, one_head, 0)
+            cosine, sine = n.cosine[at, :], n.sine[at, :]
+            gq = turn(n.gq[...] * HEAD_DIM**-0.5, cosine, sine, True)
+            gk = turn(n.gk[at, :], cosine, sine, True)
+            gm = n.gm[at, :]
+            if extra is None:
+                gm = 0.5 * gm
+                n.passed[at, :] = gm
+            else:
+                gm = gm + n.extra[at, :]
+            n.g3[at, :hid] = gq.astype(jnp.bfloat16)
+            n.g3[at, hid : 2 * hid] = gk.astype(jnp.bfloat16)
+            n.g3[at, 2 * hid :] = gm.astype(jnp.bfloat16)
+            total.send(i, dot_nt(n.g3[at, :], n.wa[:, : 3 * hid]))
+            if turn_index:
+                total.middle(order[turn_index - 1])
+            jobs.advance((turn_index + 1) / (BLOCKS + 2))
+        total.middle(order[-1])
+        cols = width // 4
+        for j in range(4):
+            cut = slice(j * cols, (j + 1) * cols)
+            n.d_wa[cut, : 3 * hid] = dot_tn(n.h[:, cut], n.g3[...]).astype(jnp.bfloat16)
+            n.d_wa[cut, 3 * hid :] = dot_tn(n.low[:, cut], n.o[...]).astype(jnp.bfloat16)
+        jobs.advance((BLOCKS + 1) / (BLOCKS + 2))
+        for i in order:
+            total.last(i)
+        gain_sum = jnp.zeros((1, width), jnp.float32)
+        for i in order:
+            at = pl.ds(i * rows, rows)
+            stream = n.x[at, :].astype(jnp.float32)
+            step, gain_sum = norm_back(n, total.total(i), stream, which, at, n.gx, gain_sum)
+            n.gx[at, :] = (n.gx1[at, :] + step).astype(n.gx.dtype)
+        n.gain[...] = gain_sum
+        jobs.finish()
+
+    return call.run(body)
+
+
+def transfers(number, jobs_of):
+    call = Call(number)
+    jobs = Jobs(jobs_of(call))
+
+    def body(n):
+        place = Place()
+        place.enter(call.far)
+        jobs.bind(n, place)
+        jobs.start()
+        jobs.finish()
+
+    return call.run(body)
+
+
+def dealt_device(
+    inputs,
+    segment_ids,
+    norm_attn_one,
+    query_one,
+    key_one,
+    value_one,
+    output_one,
+    norm_ffn_one,
+    gate_one,
+    up_one,
+    down_one,
+    norm_attn_two,
+    query_two,
+    key_two,
+    value_two,
+    output_two,
+    norm_ffn_two,
+    gate_two,
+    up_two,
+    down_two,
+    cotangent,
+):
+    parts, length, width = inputs.shape
+    count = parts * length
+    hid = query_one.shape[1]
+    places = lax.axis_size("dp") * lax.axis_size("ctx")
+    shard = width // places
+    wa_one = jnp.concatenate([query_one, key_one, value_one, output_one.T], axis=1)
+    wa_two = jnp.concatenate([query_two, key_two, value_two, output_two.T], axis=1)
+    down_one, down_two = down_one.T, down_two.T
+    gain_rows = jnp.stack([norm_attn_one, norm_ffn_one, norm_attn_two, norm_ffn_two])
+    gain_rows = jnp.concatenate([gain_rows, gain_rows]).astype(jnp.float32)
+
+    own = lax.dynamic_index_in_dim(segment_ids, lax.axis_index("ctx"), 0, True)
+    half_width = HEAD_DIM // 2
+    frequency = 10000.0 ** (-jnp.arange(half_width, dtype=jnp.float32) / half_width)
+    angles = jnp.arange(count, dtype=jnp.float32)[:, None] * frequency[None, :]
+    cosine, sine = jnp.cos(angles), jnp.sin(angles)
+    heads = hid // HEAD_DIM
+    tables = {
+        "cosine": jnp.tile(cosine, (1, 2 * heads)),
+        "sine": jnp.tile(jnp.concatenate([-sine, sine], axis=1), (1, heads)),
+        "seg_row": own,
+        "seg_col": own.reshape(count, 1),
+    }
+
+    def flat(blocks):
+        return blocks.reshape(-1, blocks.shape[-1])
+
+    def split(array):
+        return array.reshape(places, shard, array.shape[-1])
+
+    def deal(array):
+        return array.reshape(parts, length, width)
+
+    entry = transfers(
+        0,
+        lambda c: [
+            Gather(c, "wa", wa_one, places),
+            Deal(c, "tokens", inputs),
+            Gather(c, "gains", gain_rows, places),
+        ],
+    )
+    gains = jnp.transpose(entry.gains, (1, 0, 2)).reshape(-1, width)
+    x = flat(entry.tokens)
+    wa_one = flat(entry.wa)
+    attn_one = attention_layer(
+        1,
+        x,
+        None,
+        wa_one,
+        gains,
+        0,
+        tables,
+        lambda c: [
+            Gather(c, "gate", gate_one, places),
+            Gather(c, "up", up_one, places),
+            Gather(c, "down", down_one, places),
+        ],
+    )
+    ffn_one_w = (flat(attn_one.gate), flat(attn_one.up), flat(attn_one.down))
+    ffn_one = feed_forward_layer(
+        2, attn_one.x1, *ffn_one_w, gains, 1, lambda c: [Gather(c, "wa", wa_two, places)]
+    )
+    wa_two = flat(ffn_one.wa)
+    attn_two = attention_layer(
+        3,
+        ffn_one.y,
+        attn_one.v,
+        wa_two,
+        gains,
+        2,
+        tables,
+        lambda c: [
+            Gather(c, "gate", gate_two, places),
+            Gather(c, "up", up_two, places),
+            Gather(c, "down", down_two, places),
+        ],
+    )
+    ffn_two_w = (flat(attn_two.gate), flat(attn_two.up), flat(attn_two.down))
+    ffn_two = feed_forward_layer(
+        4,
+        attn_two.x1,
+        *ffn_two_w,
+        gains,
+        3,
+        lambda c: [Deal(c, "cot", cotangent), Deal(c, "out_one", deal(ffn_one.y_low))],
+    )
+    back_ffn_two = feed_forward_back(
+        5,
+        flat(ffn_two.cot),
+        attn_two.x1,
+        ffn_two,
+        *ffn_two_w,
+        gains,
+        3,
+        lambda c: [Deal(c, "out_two", deal(ffn_two.y_low))],
+    )
+    back_attn_two = attention_back(
+        6,
+        back_ffn_two.gx1,
+        ffn_one.y,
+        attn_two,
+        None,
+        wa_two,
+        gains,
+        2,
+        tables,
+        lambda c: [
+            Scatter(c, "gate", split(back_ffn_two.d_gate)),
+            Scatter(c, "up", split(back_ffn_two.d_up)),
+            Scatter(c, "down", split(back_ffn_two.d_down)),
+        ],
+    )
+    back_ffn_one = feed_forward_back(
+        7,
+        back_attn_two.gx,
+        attn_one.x1,
+        ffn_one,
+        *ffn_one_w,
+        gains,
+        1,
+        lambda c: [Scatter(c, "wa", split(back_attn_two.d_wa))],
+    )
+    back_attn_one = attention_back(
+        8,
+        back_ffn_one.gx1,
+        x,
+        attn_one,
+        back_attn_two.passed,
+        wa_one,
+        gains,
+        0,
+        tables,
+        lambda c: [
+            Scatter(c, "gate", split(back_ffn_one.d_gate)),
+            Scatter(c, "up", split(back_ffn_one.d_up)),
+            Scatter(c, "down", split(back_ffn_one.d_down)),
+        ],
+    )
+    gain_grads = jnp.concatenate(
+        [back_attn_one.gain, back_ffn_one.gain, back_attn_two.gain, back_ffn_two.gain]
+    )
+    gain_grads = jnp.concatenate([gain_grads, gain_grads])
+    gain_grads = jnp.transpose(gain_grads.reshape(-1, places, shard), (1, 0, 2))
+    leave = transfers(
+        9,
+        lambda c: [
+            Scatter(c, "wa", split(back_attn_one.d_wa)),
+            Scatter(c, "gains", gain_grads),
+            Deal(c, "grad", deal(back_attn_one.gx)),
+        ],
+    )
+
+    def attention_grads(packed):
+        query, key, value, output = jnp.split(packed, 4, axis=1)
+        return query, key, value, output.T
+
+    one = attention_grads(leave.wa)
+    two = attention_grads(back_ffn_one.wa)
+    return (
+        ffn_two.out_one,
+        back_ffn_two.out_two,
+        leave.grad.astype(jnp.float32),
+        leave.gains[0],
+        *one,
+        leave.gains[1],
+        back_attn_one.gate,
+        back_attn_one.up,
+        back_attn_one.down.T,
+        leave.gains[2],
+        *two,
+        leave.gains[3],
+        back_attn_two.gate,
+        back_attn_two.up,
+        back_attn_two.down.T,
+    )
+
+
 def solution(mesh):
     placed = (
         P("dp", "ctx", None),
@@ -636,8 +1582,14 @@
         P("mp", ("dp", "ctx")),
         P("dp", "ctx", None),
     )
+    sizes = dict(mesh.shape)
+
+    def per_device(*operands):
+        fits = sizes["dp"] == 2 and sizes["mp"] == 4 and operands[0].shape[0] == sizes["ctx"]
+        return (dealt_device if fits else on_device)(*operands)
+
     return jax.shard_map(
-        on_device,
+        per_device,
         mesh=mesh,
         in_specs=placed,
         out_specs=(

time: 1370 us -> 775 us (0.57)
  waiting for transfers between devices: 718 us -> 0 us
  Pallas kernels: 227 us -> 643 us
  matrix products: 151 us -> 0 us
  other arithmetic: 47.8 us -> 6.16 us
  blocking collectives: 40.1 us -> 0 us
  local copies, waits for them, and re-layouts: 141 us -> 114 us
  between operations: 17.9 us -> 1.71 us
    pallas_call x8 -> x10, Pallas kernels: 227 us -> 643 us  [run(): pl.pallas_call(kernel, out_shape=tuple(self.out_shapes), in_specs=self.in...]
    unnamed x18 -> x0, waiting for transfers between devices: 284 us -> none
    all_gather x6 -> x0, waiting for transfers between devices: 217 us -> none  [the longest x2 92.4 us: gather_layer(): whole = lax.all_gather(packed, both, axis=0, tiled=True)]
    reduce_scatter x4 -> x0, waiting for transfers between devices: 216 us -> none  [the longest x2 145 us: attend_back_gather(): lax.psum_scatter(key_grad.reshape(seq_count, length, -1).astype(jnp.bfloa...]
    dot_general x56 -> x0, matrix products: 151 us -> none  [the longest x14 43.5 us: project_back(): jnp.einsum('sbe,de->sbd', left_operand, right_operand, preferred_element_...]
    unnamed x224, local copies, waits for them, and re-layouts: 56.2 us -> 106 us
    dynamic_update_slice x4 -> x0, local copies, waits for them, and re-layouts: 41.6 us -> none  [the longest x2 20.8 us: attend_compute(): key_acc = lax.dynamic_update_slice_in_dim(key_acc, key_part, first_key, 1)]
    all_gather x2 -> x0, blocking collectives: 40.1 us -> none  [gather_layer(): lax.all_gather(jnp.stack([gain_attn, gain_ffn]), both, axis=1, tiled=True)]
  transfers between devices with their start and end apart: 14 -> 0, of which waited for: 13 -> 0; matrix products, arithmetic and copies ran while one was open for 12% -> 0% of each run, Pallas kernels for 6% -> 0%
where the time goes in v2:
time: 775 us; the launch traced here: 765 us
  Pallas kernels  643 us (83%)
  local copies, waits for them, and re-layouts  114 us (15%)
    pallas_call x10, Pallas kernels, run(): pl.pallas_call(kernel, out_shape=tuple(self.out_shapes), in_specs=self.in...  643 us
    unnamed x224, local copies, waits for them, and re-layouts  106 us

profile of v2, /device:TPU:0, one launch (start us, length us, event | category | flops | bytes accessed | tf_op | source)
XLA Modules:
  0.0 764.9 jit_solution(5222106898933805906)
XLA Ops:
  6.6 1.7 copy.63.refs_7_
  8.3 1.7 copy.64.refs_8_
  14.0 2.0 tile.30
  19.2 49.6 %shard_map.364 = (bf16[8,128,1024]{2,1,0:T(8,128)(2,1)S(1)}, bf16[4,256,1024]{2,1,0:T(8,128)(2,1)S(1)}, f32[8,8,128]{2,1,0:T(8,128)S(1)}) custom-call(bf16[128,1024]{1,0:T(8,128)(2,1)S(1)} %pad_maximum_fusion.refs_0_, bf16[4,256,1024]{2,1,0:T(8,128)(2,1)S(1)} %copy-done.41, f32[8,128]{1,0:T(8,128)S(1)} %copy-done.98), custom_call_target="tpu_custom_call" | custom-call | tf_op jit(solution)/shard_map/pallas_call | solution.py:651
  68.9 84.1 %shard_map.365 = (f32[1024,1024]{1,0:T(8,128)S(1)}, bf16[1024,1024]{1,0:T(8,128)(2,1)S(1)}, bf16[1024,256]{1,0:T(8,128)(2,1)S(1)}, bf16[1024,256]{1,0:T(8,128)(2...) custom-call(bf16[1024,1024]{1,0:T(8,128)(2,1)S(1)} %bitcast.55, ...), custom_call_target="tpu_custom_call" | custom-call | tf_op jit(solution)/shard_map/pallas_call | solution.py:651
  158.1 52.6 %shard_map.366 = (f32[1024,1024]{1,0:T(8,128)S(1)}, bf16[1024,1024]{1,0:T(8,128)(2,1)S(1)}, bf16[1024,1024]{1,0:T(8,128)(2,1)S(1)}, bf16[1024,704]{1,0:T(8,128)(...) custom-call(f32[1024,1024]{1,0:T(8,128)S(1)} %get-tuple-element.90.refs_0_, ...), custom_call_target="tpu_custom_call" | custom-call | tf_op jit(solution)/shard_map/pallas_call | solution.py:651
  215.6 85.4 %shard_map.367 = (f32[1024,1024]{1,0:T(8,128)S(1)}, bf16[1024,1024]{1,0:T(8,128)(2,1)S(1)}, bf16[1024,256]{1,0:T(8,128)(2,1)S(1)}, bf16[1024,256]{1,0:T(8,128)(2...) custom-call(f32[1024,1024]{1,0:T(8,128)S(1)} %get-tuple-element.94.r, ...), custom_call_target="tpu_custom_call" | custom-call | tf_op jit(solution)/shard_map/pallas_call | solution.py:651
  304.7 3.2 copy-done.36
  307.8 60.2 %shard_map.368 = (f32[1024,1024]{1,0:T(8,128)}, bf16[1024,1024]{1,0:T(8,128)(2,1)S(1)}, bf16[1024,1024]{1,0:T(8,128)(2,1)S(1)}, bf16[1024,704]{1,0:T(8,128)(2,1)...) custom-call(f32[1024,1024]{1,0:T(8,128)S(1)} %get-tuple-element.97.r, ...), custom_call_target="tpu_custom_call" | custom-call | tf_op jit(solution)/shard_map/pallas_call | solution.py:651
  372.0 2.2 copy-done.4
  378.5 1.6 copy-done.38
  380.0 1.6 copy-done.40
  381.6 51.5 %shard_map.369 = (f32[1024,1024]{1,0:T(8,128)S(1)}, f32[1,1024]{1,0:T(1,128)S(1)}, bf16[1024,704]{1,0:T(8,128)(2,1)S(1)}, bf16[1024,704]{1,0:T(8,128)(2,1)S(1)},...) custom-call(bf16[1024,1024]{1,0:T(8,128)(2,1)S(1)} %bitcast.81, f32[1024,1024]{1,0:T(8,128)S(1)} %copy-done.4, ...), custom_call_target="tpu_custom_call" | custom-call | tf_op jit(solution)/shard_map/pallas_call | solution.py:651
  433.1 2.0 copy-done.23
  439.9 1.6 copy-done.32
  441.5 1.6 copy-done.34
  450.5 90.9 %shard_map.370 = (f32[1024,1024]{1,0:T(8,128)S(1)}, f32[1024,256]{1,0:T(8,128)S(1)}, f32[1,1024]{1,0:T(1,128)S(1)}, bf16[1024,1024]{1,0:T(8,128)(2,1)S(1)}, f32[...) custom-call(f32[1024,1024]{1,0:T(8,128)} %copy-done.23, f32[1024,1024]{1,0:T(8,128)} %copy-done.2, ...), custom_call_target="tpu_custom_call" | custom-call | tf_op jit(solution)/shard_map/pallas_call | solution.py:651
  541.5 2.0 copy-done.24
  545.8 1.7 copy-done.19
  548.9 2.2 copy-done.25
  551.1 1.6 copy-done.51
  552.7 1.6 copy-done.53
  554.3 40.0 %shard_map.371 = (f32[1024,1024]{1,0:T(8,128)S(1)}, f32[1,1024]{1,0:T(1,128)S(1)}, bf16[1024,704]{1,0:T(8,128)(2,1)S(1)}, bf16[1024,704]{1,0:T(8,128)(2,1)S(1)},...) custom-call(f32[1024,1024]{1,0:T(8,128)S(1)} %copy-done.25, f32[1024,1024]{1,0:T(8,128)} %copy-done.5, ...), custom_call_target="tpu_custom_call" | custom-call | tf_op jit(solution)/shard_map/pallas_call | solution.py:651
  594.3 2.0 copy-done.22
  607.8 87.4 %shard_map.372 = (bf16[1024,1024]{1,0:T(8,128)(2,1)S(1)}, f32[1,1024]{1,0:T(1,128)S(1)}, bf16[1024,1024]{1,0:T(8,128)(2,1)S(1)}, f32[128,704]{1,0:T(8,128)S(1)},...) custom-call(f32[1024,1024]{1,0:T(8,128)} %copy-done.22, bf16[1024,1024]{1,0:T(8,128)(2,1)S(1)} %bitcast.56, ...), custom_call_target="tpu_custom_call" | custom-call | tf_op jit(solution)/shard_map/pallas_call | solution.py:651
  703.4 41.5 %shard_map.373 = (f32[128,1024]{1,0:T(8,128)S(1)}, f32[8,128]{1,0:T(8,128)S(1)}, bf16[4,256,1024]{2,1,0:T(8,128)(2,1)S(1)}) custom-call(bf16[8,128,1024]{2,1,0:T(8,128)(2,1)S(1)} %bitcast.83, f32[8,8,128]{2,1,0:T(8,128)S(1)} %bitcast.95, bf16[4,256,1024]{2,1,0:T(8,128)(2,1)S(1)} %bitcast.82), custom_call_target="tpu_custom_call" | custom-call | tf_op jit(solution)/shard_map/pallas_call | solution.py:651
  745.5 2.0 copy.79
  747.4 1.9 copy.80
  749.3 1.9 copy.81
  751.2 1.9 copy.83
  753.1 1.9 copy.84
  758.3 2.5 convert_element_type.7
  (220 shorter events, 77.5 us)
Async XLA Ops:
  16.0 52.8 %copy-start.97 = (s32[1,1024]{1,0:T(1,128)S(1)}, s32[1,1024]{1,0:T(1,128)}, u32[]{:S(2)}) copy-start(s32[1,1024]{1,0:T(1,128)} %constant_dynamic-slice_fusion.refs_5_.refs_12_) | copy-start | bytes 12292
  19.2 49.7 %copy-start.73 = (bf16[128,704]{1,0:T(8,128)(2,1)S(1)}, bf16[128,704]{1,0:T(8,128)(2,1)}, u32[]{:S(2)}) copy-start(bf16[128,704]{1,0:T(8,128)(2,1)} %copy.63.refs_7_) | copy-start | bytes 540676
  19.2 49.7 %copy-start.74 = (bf16[128,704]{1,0:T(8,128)(2,1)S(1)}, bf16[128,704]{1,0:T(8,128)(2,1)}, u32[]{:S(2)}) copy-start(bf16[128,704]{1,0:T(8,128)(2,1)} %copy.64.refs_8_) | copy-start | bytes 540676
  19.2 49.7 %copy-start.75 = (bf16[704,128]{0,1:T(8,128)(2,1)S(1)}, bf16[704,128]{0,1:T(8,128)(2,1)}, u32[]{:S(2)}) copy-start(bf16[704,128]{0,1:T(8,128)(2,1)} %copy.59) | copy-start | bytes 540676
  68.8 84.1 %copy-start.6 = (bf16[4,256,1024]{2,1,0:T(8,128)(2,1)}, bf16[4,256,1024]{2,1,0:T(8,128)(2,1)S(1)}, u32[]{:S(2)}) copy-start(bf16[4,256,1024]{2,1,0:T(8,128)(2,1)S(1)} %get-tuple-element.87) | copy-start | bytes 6291460
  158.1 52.7 %copy-start.5 = (f32[1024,1024]{1,0:T(8,128)}, f32[1024,1024]{1,0:T(8,128)S(1)}, u32[]{:S(2)}) copy-start(f32[1024,1024]{1,0:T(8,128)S(1)} %get-tuple-element.90.refs_0_.refs_1_) | copy-start | bytes 12582916
  158.1 52.7 %copy-start.16 = (bf16[8,128,704]{2,1,0:T(8,128)(2,1)}, bf16[8,128,704]{2,1,0:T(8,128)(2,1)S(1)}, u32[]{:S(2)}) copy-start(bf16[8,128,704]{2,1,0:T(8,128)(2,1)S(1)} %get-tuple-element.91) | copy-start | bytes 4325380
  158.1 52.7 %copy-start.18 = (bf16[8,128,704]{2,1,0:T(8,128)(2,1)}, bf16[8,128,704]{2,1,0:T(8,128)(2,1)S(1)}, u32[]{:S(2)}) copy-start(bf16[8,128,704]{2,1,0:T(8,128)(2,1)S(1)} %get-tuple-element.92) | copy-start | bytes 4325380
  158.1 52.7 %copy-start.20 = (bf16[8,128,704]{2,1,0:T(8,128)(2,1)}, bf16[8,128,704]{2,1,0:T(8,128)(2,1)S(1)}, u32[]{:S(2)}) copy-start(bf16[8,128,704]{2,1,0:T(8,128)(2,1)S(1)} %get-tuple-element.93) | copy-start | bytes 4325380
  158.1 57.5 %copy-start.72 = (bf16[704,128]{0,1:T(8,128)(2,1)S(1)}, bf16[704,128]{0,1:T(8,128)(2,1)}, u32[]{:S(2)}) copy-start(bf16[704,128]{0,1:T(8,128)(2,1)} %copy.66) | copy-start | bytes 540676
  215.6 85.5 %copy-start.2 = (f32[1024,1024]{1,0:T(8,128)}, f32[1024,1024]{1,0:T(8,128)S(1)}, u32[]{:S(2)}) copy-start(f32[1024,1024]{1,0:T(8,128)S(1)} %get-tuple-element.94.refs_0_.refs_1_) | copy-start | bytes 12582916
  215.6 85.5 %copy-start.8 = (bf16[8,128,1024]{2,1,0:T(8,128)(2,1)}, bf16[8,128,1024]{2,1,0:T(8,128)(2,1)S(1)}, u32[]{:S(2)}) copy-start(bf16[8,128,1024]{2,1,0:T(8,128)(2,1)S(1)} %get-tuple-element.95) | copy-start | bytes 6291460
  215.6 85.5 %copy-start.35 = (bf16[1024,1024]{1,0:T(8,128)(2,1)}, bf16[1024,1024]{1,0:T(8,128)(2,1)S(1)}, u32[]{:S(2)}) copy-start(bf16[1024,1024]{1,0:T(8,128)(2,1)S(1)} %get-tuple-element.101) | copy-start | bytes 6291460
  215.6 89.0 %copy-start.26 = (bf16[4,256,1024]{2,1,0:T(8,128)(2,1)S(1)}, bf16[4,256,1024]{2,1,0:T(8,128)(2,1)}, u32[]{:S(2)}) copy-start(bf16[4,256,1024]{2,1,0:T(8,128)(2,1)} %refs_5_.1) | copy-start | bytes 6291460
  304.6 63.4 %copy-start.3 = (f32[1024,1024]{1,0:T(8,128)}, f32[1024,1024]{1,0:T(8,128)S(1)}, u32[]{:S(2)}) copy-start(f32[1024,1024]{1,0:T(8,128)S(1)} %get-tuple-element.97.refs_0_.refs_1_) | copy-start | bytes 12582916
  304.6 63.4 %copy-start.10 = (bf16[8,128,704]{2,1,0:T(8,128)(2,1)}, bf16[8,128,704]{2,1,0:T(8,128)(2,1)S(1)}, u32[]{:S(2)}) copy-start(bf16[8,128,704]{2,1,0:T(8,128)(2,1)S(1)} %get-tuple-element.98) | copy-start | bytes 4325380
  304.6 63.5 %copy-start.12 = (bf16[8,128,704]{2,1,0:T(8,128)(2,1)}, bf16[8,128,704]{2,1,0:T(8,128)(2,1)S(1)}, u32[]{:S(2)}) copy-start(bf16[8,128,704]{2,1,0:T(8,128)(2,1)S(1)} %get-tuple-element.99) | copy-start | bytes 4325380
  304.6 63.5 %copy-start.14 = (bf16[8,128,704]{2,1,0:T(8,128)(2,1)}, bf16[8,128,704]{2,1,0:T(8,128)(2,1)S(1)}, u32[]{:S(2)}) copy-start(bf16[8,128,704]{2,1,0:T(8,128)(2,1)S(1)} %get-tuple-element.100) | copy-start | bytes 4325380
  304.6 63.5 %copy-start.84 = (bf16[1024,256]{1,0:T(8,128)(2,1)}, bf16[1024,256]{1,0:T(8,128)(2,1)S(1)}, u32[]{:S(2)}) copy-start(bf16[1024,256]{1,0:T(8,128)(2,1)S(1)} %get-tuple-element.113.refs_4_) | copy-start | bytes 1572868
  304.6 63.5 %copy-start.86 = (bf16[1024,256]{1,0:T(8,128)(2,1)}, bf16[1024,256]{1,0:T(8,128)(2,1)S(1)}, u32[]{:S(2)}) copy-start(bf16[1024,256]{1,0:T(8,128)(2,1)S(1)} %get-tuple-element.114.refs_5_) | copy-start | bytes 1572868
  304.6 63.5 %copy-start.88 = (bf16[1024,256]{1,0:T(8,128)(2,1)}, bf16[1024,256]{1,0:T(8,128)(2,1)S(1)}, u32[]{:S(2)}) copy-start(bf16[1024,256]{1,0:T(8,128)(2,1)S(1)} %get-tuple-element.115.refs_6_) | copy-start | bytes 1572868
  381.6 58.3 %copy-start.9 = (bf16[8,128,1024]{2,1,0:T(8,128)(2,1)S(1)}, bf16[8,128,1024]{2,1,0:T(8,128)(2,1)}, u32[]{:S(2)}) copy-start(bf16[8,128,1024]{2,1,0:T(8,128)(2,1)} %copy-done.8) | copy-start | bytes 6291460
  381.6 58.3 %copy-start.83 = (bf16[1024,256]{1,0:T(8,128)(2,1)S(1)}, bf16[1024,256]{1,0:T(8,128)(2,1)}, u32[]{:S(2)}) copy-start(bf16[1024,256]{1,0:T(8,128)(2,1)} %copy-done.82) | copy-start | bytes 1572868
  450.5 95.3 %copy-start.17 = (bf16[8,128,704]{2,1,0:T(8,128)(2,1)S(1)}, bf16[8,128,704]{2,1,0:T(8,128)(2,1)}, u32[]{:S(2)}) copy-start(bf16[8,128,704]{2,1,0:T(8,128)(2,1)} %copy-done.16) | copy-start | bytes 4325380
  450.5 95.3 %copy-start.65 = (bf16[1024,704]{1,0:T(8,128)(2,1)S(1)}, bf16[1024,704]{1,0:T(8,128)(2,1)}, u32[]{:S(2)}) copy-start(bf16[1024,704]{1,0:T(8,128)(2,1)} %copy-done.64) | copy-start | bytes 4325380
  450.5 95.3 %copy-start.67 = (bf16[1024,704]{1,0:T(8,128)(2,1)S(1)}, bf16[1024,704]{1,0:T(8,128)(2,1)}, u32[]{:S(2)}) copy-start(bf16[1024,704]{1,0:T(8,128)(2,1)} %copy-done.66) | copy-start | bytes 4325380
  450.5 95.3 %copy-start.69 = (bf16[1024,704]{1,0:T(8,128)(2,1)S(1)}, bf16[1024,704]{1,0:T(8,128)(2,1)}, u32[]{:S(2)}) copy-start(bf16[1024,704]{1,0:T(8,128)(2,1)} %copy-done.68) | copy-start | bytes 4325380
  545.8 48.6 %copy-start.92 = (f32[128,704]{1,0:T(8,128)}, f32[128,704]{1,0:T(8,128)S(1)}, u32[]{:S(2)}) copy-start(f32[128,704]{1,0:T(8,128)S(1)} %get-tuple-element.193) | copy-start | bytes 1081348
  545.8 48.6 %copy-start.93 = (f32[128,704]{1,0:T(8,128)}, f32[128,704]{1,0:T(8,128)S(1)}, u32[]{:S(2)}) copy-start(f32[128,704]{1,0:T(8,128)S(1)} %get-tuple-element.192) | copy-start | bytes 1081348
  554.3 45.3 %copy-start.7 = (bf16[4,256,1024]{2,1,0:T(8,128)(2,1)S(1)}, bf16[4,256,1024]{2,1,0:T(8,128)(2,1)}, u32[]{:S(2)}) copy-start(bf16[4,256,1024]{2,1,0:T(8,128)(2,1)} %copy-done.6) | copy-start | bytes 6291460
  554.3 45.3 %copy-start.77 = (bf16[1024,256]{1,0:T(8,128)(2,1)S(1)}, bf16[1024,256]{1,0:T(8,128)(2,1)}, u32[]{:S(2)}) copy-start(bf16[1024,256]{1,0:T(8,128)(2,1)} %copy-done.76) | copy-start | bytes 1572868
  554.3 45.3 %copy-start.79 = (bf16[1024,256]{1,0:T(8,128)(2,1)S(1)}, bf16[1024,256]{1,0:T(8,128)(2,1)}, u32[]{:S(2)}) copy-start(bf16[1024,256]{1,0:T(8,128)(2,1)} %copy-done.78) | copy-start | bytes 1572868
  (71 other events, 148.0 us)

commit v3 on v1

--- a/solution.py
+++ b/solution.py
@@ -1,8 +1,10 @@
 import functools
 import math
+from types import SimpleNamespace
 
 import jax
 import jax.numpy as jnp
+import numpy as np
 from jax import lax
 from jax.experimental import pallas as pl
 from jax.experimental.pallas import tpu as pltpu
@@ -11,6 +13,7 @@
 MESH = pl.DeviceIdType.MESH
 
 HEAD_DIM = 64
+DP, CTX, MP = "dp", "ctx", "mp"
 
 
 epsilon = 1e-05
@@ -38,7 +41,7 @@
 def head_sum_kernel(
     chunks, x_ref, o_ref, near, half_sum, far, send_a, recv_a, send_b, recv_b, send_c, recv_c
 ):
-    dp, ctx, mp = (lax.axis_index(name) for name in ("dp", "ctx", "mp"))
+    dp, ctx, mp = (lax.axis_index(name) for name in (DP, CTX, MP))
     side = lax.rem(mp, 2)
     pair = (dp, ctx, mp + 1 - 2 * side)
     cross = (dp, ctx, lax.rem(mp + 2, 4))
@@ -216,8 +219,8 @@
         jnp.zeros((seq_count, head_count, count_of_rows), jnp.float32),
         jnp.zeros((seq_count, count_of_rows, head_count, head_width), jnp.float32),
     )
-    key_piece = lax.all_gather(key_rows, "ctx", axis=1, tiled=True)
-    value_piece = lax.all_gather(value_rows, "ctx", axis=1, tiled=True)
+    key_piece = lax.all_gather(key_rows, CTX, axis=1, tiled=True)
+    value_piece = lax.all_gather(value_rows, CTX, axis=1, tiled=True)
     piece_rows = key_piece.shape[1]
     block_rows = math.gcd(piece_rows, 512)
     key_split = key_piece.reshape(seq_count, piece_rows, head_count, head_width)
@@ -275,8 +278,8 @@
     query_document_ids = lax.dynamic_slice_in_dim(segments, query_places[0], count_of_rows, 1)
     last_query = query_places[count_of_rows - 1]
     all_keys, all_values = (
-        lax.all_gather(key_rows, "ctx", axis=1, tiled=True),
-        lax.all_gather(value_rows, "ctx", axis=1, tiled=True),
+        lax.all_gather(key_rows, CTX, axis=1, tiled=True),
+        lax.all_gather(value_rows, CTX, axis=1, tiled=True),
     )
     length = all_keys.shape[1]
     block_rows = math.gcd(length, 512)
@@ -325,13 +328,13 @@
     key_home, value_home = (
         lax.psum_scatter(
             key_grad.reshape(seq_count, length, -1).astype(jnp.bfloat16),
-            "ctx",
+            CTX,
             scatter_dimension=1,
             tiled=True,
         ).astype(jnp.float32),
         lax.psum_scatter(
             value_grad.reshape(seq_count, length, -1).astype(jnp.bfloat16),
-            "ctx",
+            CTX,
             scatter_dimension=1,
             tiled=True,
         ).astype(jnp.float32),
@@ -500,7 +503,7 @@
     cotangent,
 ):
     def gather_layer(gain_attn, query, key, value, output, gain_ffn, gate, up, down):
-        both = ("dp", "ctx")
+        both = (DP, CTX)
         packed = jnp.concatenate([query, key, value, output.T, gate, up, down.T], axis=1)
         whole = lax.all_gather(packed, both, axis=0, tiled=True)
         gains = lax.all_gather(jnp.stack([gain_attn, gain_ffn]), both, axis=1, tiled=True)
@@ -511,7 +514,7 @@
         return (gains[0], w_q, w_k, w_v, w_o.T, gains[1], w_g, w_u, w_d.T)
 
     def scatter_layer(grads, outs):
-        both = ("dp", "ctx")
+        both = (DP, CTX)
         gain_attn, query, key, value, output, gain_ffn, gate, up, down = grads
         pieces = [query, key, value, output.T, gate, up, down.T]
         packed = jnp.concatenate([part.astype(jnp.bfloat16) for part in pieces], axis=1)
@@ -554,7 +557,7 @@
     weights_one = gathered[:9]
     weights_two = gathered[9:]
     seq_count, count_of_rows, model_width = inputs.shape
-    query_places = lax.axis_index("ctx") * count_of_rows + jnp.arange(
+    query_places = lax.axis_index(CTX) * count_of_rows + jnp.arange(
         count_of_rows, dtype=jnp.int32
     )
     cosine, sine_table = rotary_tables(query_places[0], count_of_rows)
@@ -612,56 +615,1483 @@
     )
 
 
+class Raw:
+    def __init__(self, call, kind, index):
+        self.call, self.kind, self.index = call, kind, index
+
+    @property
+    def ref(self):
+        return self.call.refs[self.kind][self.index]
+
+    @property
+    def at(self):
+        return self.ref.at
+
+    @property
+    def result(self):
+        return self.call.results[self.index]
+
+
+def cut_rows(ref, blocks, i):
+    if blocks == 1:
+        return ref
+    rows = ref.shape[-2] // blocks
+    part = pl.ds(i * rows, rows)
+    return ref.at[part] if len(ref.shape) == 2 else ref.at[:, part]
+
+
+class Store:
+    def __init__(self, call, held, shape, dtype, blocks):
+        self.held, self.blocks = held, blocks
+        self.out = call.give(shape, dtype)
+        self.flag = call.flags(blocks)
+        call.stores.append(self)
+
+    def copy(self, i):
+        return pltpu.make_async_copy(
+            cut_rows(self.held.ref, self.blocks, i),
+            cut_rows(self.out.ref, self.blocks, i),
+            self.flag.at[i],
+        )
+
+    def put(self, i=None):
+        for k in range(self.blocks) if i is None else (i,):
+            self.copy(k).start()
+
+    def finish(self):
+        for i in range(self.blocks):
+            self.copy(i).wait()
+
+    @property
+    def result(self):
+        return self.out.result
+
+
+class Held:
+    def __init__(self, call, shape, dtype):
+        self.call, self.shape, self.dtype = call, shape, dtype
+        self.slot = call.scratch_slot(pltpu.VMEM(shape, dtype))
+        self.source = self.out = None
+        self.blocks, self.waited = 1, set()
+
+    @property
+    def ref(self):
+        return self.call.refs[2][self.slot]
+
+    @property
+    def at(self):
+        return self.ref.at
+
+    def __getitem__(self, key):
+        return self.ref[key]
+
+    def __setitem__(self, key, value):
+        self.ref[key] = value
+
+    def load_copy(self, i):
+        return pltpu.make_async_copy(
+            cut_rows(self.source.ref, self.blocks, i),
+            cut_rows(self.ref, self.blocks, i),
+            self.flag.at[i],
+        )
+
+    def need(self, i=None):
+        if self.source is None:
+            return
+        for k in range(self.blocks) if i is None or self.blocks == 1 else (i,):
+            if k not in self.waited:
+                self.waited.add(k)
+                self.load_copy(k).wait()
+
+    def put(self, i=None):
+        self.out.put(i)
+
+    @property
+    def result(self):
+        return self.out.result
+
+
+class Call:
+    def __init__(self, number):
+        self.number = number
+        self.operands, self.shapes, self.scratch = [], [], []
+        self.loads, self.stores, self.jobs = [], [], []
+        self.far = False
+
+    def take(self, array):
+        self.operands.append(array)
+        return Raw(self, 0, len(self.operands) - 1)
+
+    def give(self, shape, dtype):
+        self.shapes.append(jax.ShapeDtypeStruct(shape, dtype))
+        return Raw(self, 1, len(self.shapes) - 1)
+
+    def scratch_slot(self, kind):
+        self.scratch.append(kind)
+        return len(self.scratch) - 1
+
+    def flags(self, count):
+        return Raw(self, 2, self.scratch_slot(pltpu.SemaphoreType.DMA((count,))))
+
+    def hold(self, shape, dtype):
+        return Held(self, shape, dtype)
+
+    def load(self, array, blocks=1):
+        held = Held(self, array.shape, array.dtype)
+        self.load_into(held, self.take(array), blocks)
+        self.loads.append(held)
+        return held
+
+    def load_into(self, held, source, blocks):
+        held.source, held.blocks, held.flag = source, blocks, self.flags(blocks)
+
+    def store(self, shape, dtype, blocks=1):
+        held = Held(self, shape, dtype)
+        held.out = Store(self, held, shape, dtype, blocks)
+        return held
+
+    def store_from(self, held, shape, dtype, blocks=1):
+        return Store(self, held, shape, dtype, blocks)
+
+    def start_loads(self, backward=False):
+        for k in range(max([held.blocks for held in self.loads], default=0)):
+            for held in self.loads:
+                if k < held.blocks:
+                    held.load_copy(held.blocks - 1 - k if backward else k).start()
+
+    def run(self, body, remote_ops=True):
+        ins, outs = len(self.operands), len(self.operands) + len(self.shapes)
+
+        def kernel(*refs):
+            self.refs = (refs[:ins], refs[ins:outs], refs[outs:])
+            for held in self.loads:
+                held.waited = set()
+            body()
+            for held in self.loads:
+                held.need()
+            for store in self.stores:
+                store.finish()
+
+        space = pl.BlockSpec(memory_space=pltpu.HBM)
+        self.results = pl.pallas_call(
+            kernel,
+            out_shape=tuple(self.shapes),
+            in_specs=[space] * ins,
+            out_specs=(space,) * len(self.shapes),
+            scratch_shapes=self.scratch,
+            compiler_params=pltpu.CompilerParams(
+                has_side_effects=remote_ops,
+                vmem_limit_bytes=62 << 20,
+                collective_id=self.number if remote_ops else None,
+            ),
+        )(*self.operands)
+        self.refs = None
+
+
+class Place:
+    def __init__(self):
+        self.dp, self.ctx, self.mp = (lax.axis_index(a) for a in (DP, CTX, MP))
+        self.ctx_size = lax.axis_size(CTX)
+        self.side = lax.rem(self.mp, 2)
+        self.pair = (self.dp, self.ctx, self.mp + 1 - 2 * self.side)
+        self.cross = (self.dp, self.ctx, lax.rem(self.mp + 2, 4))
+        self.other = (1 - self.dp, self.ctx, self.mp)
+
+    def ahead(self, step):
+        return lax.rem(self.ctx + step, self.ctx_size)
+
+    def behind(self, step):
+        return lax.rem(self.ctx + self.ctx_size - step, self.ctx_size)
+
+    def along(self, index):
+        return (self.dp, index, self.mp)
+
+    def peers(self, far):
+        peers = [self.pair, self.cross]
+        if far:
+            peers.append(self.other)
+            peers += [self.along(self.ahead(s)) for s in range(1, self.ctx_size)]
+        return peers
+
+    def greet(self, far):
+        barrier = pltpu.get_barrier_semaphore()
+        for peer in self.peers(far):
+            pl.semaphore_signal(barrier, inc=1, device_id=peer, device_id_type=MESH)
+
+    def enter(self, far):
+        pl.semaphore_wait(pltpu.get_barrier_semaphore(), len(self.peers(far)))
+
+
+def remote(source, target, send, recv, peer):
+    return pltpu.make_async_remote_copy(
+        src_ref=source,
+        dst_ref=target,
+        send_sem=send,
+        recv_sem=recv,
+        device_id=peer,
+        device_id_type=MESH,
+    )
+
+
+class HeadSum:
+    def __init__(self, call, blocks, rows, width):
+        self.half = rows // 2
+        self.part = call.hold((blocks, rows, width), jnp.bfloat16)
+        self.near, self.far, self.rest = (
+            call.hold((blocks, rows // 2, width), jnp.bfloat16) for _ in range(3)
+        )
+        self.sa, self.ra, self.sb, self.rb, self.sc, self.rc = (
+            call.flags(blocks) for _ in range(6)
+        )
+
+    def bind(self, place):
+        self.place = place
+
+    def own(self):
+        return pl.ds(pl.multiple_of(self.place.side * self.half, self.half), self.half)
+
+    def theirs(self):
+        start = (1 - self.place.side) * self.half
+        return pl.ds(pl.multiple_of(start, self.half), self.half)
+
+    def first(self, i):
+        source = self.part.at[i, self.theirs()]
+        return remote(source, self.near.at[i], self.sa.at[i], self.ra.at[i], self.place.pair)
+
+    def second(self, i):
+        return remote(
+            self.near.at[i], self.far.at[i], self.sb.at[i], self.rb.at[i], self.place.cross
+        )
+
+    def third(self, i):
+        return remote(
+            self.far.at[i], self.rest.at[i], self.sc.at[i], self.rc.at[i], self.place.pair
+        )
+
+    def send(self, i, partial_rows):
+        self.part[i] = partial_rows.astype(jnp.bfloat16)
+        self.first(i).start()
+
+    def middle(self, i):
+        self.first(i).wait()
+        mine = self.part[i, self.own()].astype(jnp.float32)
+        self.near[i] = (mine + self.near[i].astype(jnp.float32)).astype(jnp.bfloat16)
+        self.second(i).start()
+
+    def last(self, i):
+        self.second(i).wait()
+        total = self.near[i].astype(jnp.float32) + self.far[i].astype(jnp.float32)
+        self.far[i] = total.astype(jnp.bfloat16)
+        self.third(i).start()
+
+    def total(self, i):
+        self.third(i).wait()
+        self.part[i, self.own()] = self.far[i]
+        self.part[i, self.theirs()] = self.rest[i]
+        return self.part[i].astype(jnp.float32)
+
+
+class Gather:
+    def __init__(self, call, shard, places):
+        self.parts = lax.axis_size(CTX)
+        call.far = True
+        self.shard = shard if isinstance(shard, Held) else call.load(shard)
+        self.whole = call.give((places,) + shard.shape, shard.dtype)
+        self.zs, self.zr, self.ys, self.yr = (call.flags(self.parts) for _ in range(4))
+        self.l = call.flags(1)
+        self.relayed = self.parts == 4
+        self.order = (2, 1, 3) if self.relayed else tuple(range(self.parts - 1, 0, -1))
+        self.steps = len(self.order)
+
+    def bind(self, place):
+        self.place = place
+
+    def slot(self, dp, ctx):
+        return self.whole.at[dp * self.parts + ctx]
+
+    def local(self):
+        p = self.place
+        return pltpu.make_async_copy(self.shard.ref, self.slot(p.dp, p.ctx), self.l.at[0])
+
+    def along(self, s):
+        p = self.place
+        target = self.slot(p.dp, p.ctx)
+        return remote(self.shard.ref, target, self.zs.at[s], self.zr.at[s], p.along(p.ahead(s)))
+
+    def direct(self, s, act):
+        if self.relayed and s != 2:
+            pl.when(self.place.ctx != (0 if s == 3 else 3))(lambda: act(self.along(s)))
+        else:
+            act(self.along(s))
+
+    def relay(self, act):
+        p = self.place
+        block = self.slot(p.dp, p.behind(2))
+        for middle, end, s in ((2, 3, 3), (1, 0, 1)):
+            copy = remote(block, block, self.zs.at[0], self.zr.at[s], p.along(end))
+            pl.when(p.ctx == middle)(lambda copy=copy: act(copy))
+
+    def across(self, s):
+        p = self.place
+        block = self.slot(p.dp, p.behind(s))
+        source = self.shard.ref if s == 0 else block
+        return remote(source, block, self.ys.at[s], self.yr.at[s], p.other)
+
+    def start(self):
+        self.shard.need()
+        for s in self.order:
+            self.direct(s, lambda copy: copy.start())
+        self.across(0).start()
+        self.local().start()
+
+    def step(self, k):
+        s = self.order[k]
+        p = self.place
+        block = self.slot(p.dp, p.behind(s))
+        remote(block, block, self.zs.at[s], self.zr.at[s], p.along(p.ctx)).wait_recv()
+        if self.relayed and s == 2:
+            self.relay(lambda copy: copy.start())
+        self.across(s).start()
+
+    def finish(self):
+        p = self.place
+        self.local().wait()
+        for s in self.order:
+            self.direct(s, lambda copy: copy.wait_send())
+        if self.relayed:
+            self.relay(lambda copy: copy.wait_send())
+        for s in range(self.parts):
+            self.across(s).wait_send()
+            block = self.slot(1 - p.dp, p.behind(s))
+            remote(block, block, self.ys.at[s], self.yr.at[s], p.other).wait_recv()
+
+    @property
+    def result(self):
+        whole = self.whole.result
+        return whole.reshape(-1, whole.shape[-1])
+
+
+class Scatter:
+    def __init__(self, call, blocks):
+        self.parts = lax.axis_size(CTX)
+        places, rows, width = blocks.shape
+        self.dtype = blocks.dtype
+        call.far = True
+        self.late = isinstance(blocks, Held)
+        self.blocks = blocks if self.late else call.take(blocks)
+        self.out = call.store((rows, width), jnp.float32)
+        if not self.late:
+            self.mb = call.hold((self.parts, rows, width), blocks.dtype)
+        self.yb = call.hold((self.parts, rows, width), blocks.dtype)
+        self.zb = call.hold((self.parts - 1, rows, width), blocks.dtype)
+        self.zs, self.zr, self.ys, self.yr = (call.flags(self.parts) for _ in range(4))
+        self.l = call.flags(1)
+        self.relayed = self.parts == 4
+        self.order = (3, 1, 2, 0) if self.relayed else tuple(range(self.parts - 1, -1, -1))
+        if self.relayed:
+            self.rb = call.hold((rows, width), blocks.dtype)
+        self.steps = self.parts
+
+    def bind(self, place):
+        self.place = place
+
+    def local(self):
+        mine = self.blocks.at[pl.ds(self.place.dp * self.parts, self.parts)]
+        return pltpu.make_async_copy(mine, self.mb.ref, self.l.at[0])
+
+    def across(self, s):
+        p = self.place
+        block = self.blocks.at[(1 - p.dp) * self.parts + p.ahead(s)]
+        return remote(block, self.yb.at[s], self.ys.at[s], self.yr.at[s], p.other)
+
+    def along(self, s, act):
+        p = self.place
+        target = self.zb.at[s - 1]
+        copy = remote(self.yb.at[s], target, self.zs.at[s], self.zr.at[s], p.along(p.ahead(s)))
+        if not self.relayed or s == 2:
+            act(copy)
+            return
+        end, middle = (0, 1) if s == 3 else (3, 2)
+        way = remote(self.yb.at[s], self.rb.ref, self.zs.at[s], self.zr.at[0], p.along(middle))
+        pl.when(p.ctx != end)(lambda: act(copy))
+        pl.when(p.ctx == end)(lambda: act(way))
+
+    def start(self):
+        for s in self.order:
+            self.across(s).start()
+        if not self.late:
+            self.local().start()
+
+    def step(self, k):
+        p = self.place
+        s = self.order[k]
+        if k == 0 and not self.late:
+            self.local().wait()
+        self.across(s).wait()
+        if self.late:
+            mine = self.blocks[p.dp * self.parts + p.ahead(s)]
+        else:
+            mine = self.mb[p.ahead(s)]
+        both = mine.astype(jnp.float32) + self.yb[s].astype(jnp.float32)
+        if s == 0:
+            self.out[...] = both
+            return
+        self.yb[s] = both.astype(self.dtype)
+        if self.relayed and s == 2:
+
+            def add_ends():
+                way = remote(self.rb.ref, self.rb.ref, self.zs.at[0], self.zr.at[0], p.other)
+                way.wait_recv()
+                through = self.yb[s].astype(jnp.float32) + self.rb[...].astype(jnp.float32)
+                self.yb[s] = through.astype(self.dtype)
+
+            pl.when((p.ctx == 1) | (p.ctx == 2))(add_ends)
+        self.along(s, lambda copy: copy.start())
+
+    def finish(self):
+        p = self.place
+
+        def add(s):
+            block = self.zb.at[s - 1]
+            remote(block, block, self.zs.at[s], self.zr.at[s], p.other).wait_recv()
+            self.out[...] += self.zb[s - 1].astype(jnp.float32)
+
+        for s in self.order:
+            if s == 0:
+                continue
+            self.along(s, lambda copy: copy.wait_send())
+            if self.relayed and s != 2:
+                pl.when(p.ctx != (3 if s == 3 else 0))(functools.partial(add, s))
+            else:
+                add(s)
+        self.out.put()
+
+    @property
+    def result(self):
+        return self.out.result
+
+
+class Deal:
+    def __init__(self, call, blocks, wide=False):
+        self.parts, self.wide = lax.axis_size(CTX), wide
+        self.share = blocks.shape[1] // (2 if wide else 4)
+        call.far = True
+        self.source = call.take(blocks)
+        self.target = call.give(blocks.shape, blocks.dtype)
+        self.held = call.hold(blocks.shape[1:], blocks.dtype)
+        self.l = call.flags(2)
+        self.zf, self.af, self.xf, self.bf = (
+            tuple(call.flags(self.parts) for _ in range(2)) for _ in range(4)
+        )
+        self.steps = (self.parts - 1) * (1 if wide else 2)
+
+    def bind(self, place):
+        self.place = place
+        self.own = place.side if self.wide else place.mp
+
+    def rows(self, index):
+        return pl.ds(pl.multiple_of(index * self.share, self.share), self.share)
+
+    def local(self, k):
+        p = self.place
+        refs = (self.source.at[p.ctx], self.held.ref, self.target.at[p.ctx])
+        return pltpu.make_async_copy(refs[k], refs[k + 1], self.l.at[k])
+
+    def along(self, s):
+        p = self.place
+        rows = self.rows(self.own)
+        return remote(
+            self.source.at[p.ahead(s), rows],
+            self.target.at[p.ctx, rows],
+            self.zf[0].at[s],
+            self.zf[1].at[s],
+            p.along(p.ahead(s)),
+        )
+
+    def piece(self, s, index, flags, peer):
+        ref = self.target.at[self.place.behind(s), self.rows(index)]
+        return remote(ref, ref, flags[0].at[s], flags[1].at[s], peer)
+
+    def start(self):
+        for s in range(self.parts - 1, 0, -1):
+            self.along(s).start()
+        self.local(0).start()
+
+    def step(self, k):
+        p = self.place
+        if k == 0:
+            self.local(0).wait()
+            self.local(1).start()
+        if self.wide:
+            s = self.parts - 1 - k
+            self.piece(s, self.own, self.zf, p.along(p.ctx)).wait_recv()
+            self.piece(s, self.own, self.af, p.pair).start()
+            return
+        s = self.parts - 1 - k // 2
+        far = lax.rem(p.mp + 2, 4)
+        if k % 2 == 0:
+            self.piece(s, p.mp, self.zf, p.along(p.ctx)).wait_recv()
+            self.piece(s, p.mp, self.xf, p.cross).start()
+            self.piece(s, p.mp, self.af, p.pair).start()
+        else:
+            self.piece(s, far, self.xf, p.cross).wait_recv()
+            self.piece(s, far, self.bf, p.pair).start()
+
+    def finish(self):
+        p = self.place
+        self.local(1).wait()
+        if self.wide:
+            for s in range(1, self.parts):
+                self.along(s).wait_send()
+                self.piece(s, self.own, self.af, p.pair).wait_send()
+                self.piece(s, 1 - self.own, self.af, p.pair).wait_recv()
+            return
+        far = lax.rem(p.mp + 2, 4)
+        near = p.mp + 1 - 2 * p.side
+        near_far = lax.rem(near + 2, 4)
+        for s in range(1, self.parts):
+            self.along(s).wait_send()
+            self.piece(s, p.mp, self.xf, p.cross).wait_send()
+            self.piece(s, p.mp, self.af, p.pair).wait_send()
+            self.piece(s, far, self.bf, p.pair).wait_send()
+            self.piece(s, near, self.af, p.pair).wait_recv()
+            self.piece(s, near_far, self.bf, p.pair).wait_recv()
+
+    @property
+    def result(self):
+        whole = self.target.result
+        return whole.reshape(-1, whole.shape[-1])
+
+
+LATE = "late"
+
+
+class Jobs:
+    def __init__(self, jobs, span=40.0, order=None):
+        self.jobs = list(jobs)
+        self.queue = [(job, k) for job in self.jobs for k in range(job.steps)]
+        if order is not None:
+            left = [list(range(job.steps)) for job in self.jobs]
+            self.queue = [(self.jobs[j], left[j].pop(0)) for j in order]
+        self.span, self.at = span, 0
+
+    def start(self, place):
+        self.at = 0
+        for job in self.jobs:
+            job.bind(place)
+        for job in self.jobs:
+            if not getattr(job, LATE, False):
+                job.start()
+
+    def advance(self, reached):
+        stop = min(len(self.queue), int(len(self.queue) * reached / self.span))
+        while self.at < stop:
+            job, k = self.queue[self.at]
+            job.step(k)
+            self.at += 1
+
+    def finish(self):
+        self.advance(self.span)
+        for job in self.jobs:
+            job.finish()
+
+
+def begin(call, total, jobs, backward=False):
+    place = Place()
+    if total is not None:
+        total.bind(place)
+    place.greet(call.far)
+    call.start_loads(backward)
+    place.enter(call.far)
+    jobs.start(place)
+
+
+def dot_nn(a, b):
+    return lax.dot_general(a, b, (((1,), (0,)), ((), ())), preferred_element_type=jnp.float32)
+
+
+def dot_nt(a, b):
+    return lax.dot_general(a, b, (((1,), (1,)), ((), ())), preferred_element_type=jnp.float32)
+
+
+def dot_tn(a, b):
+    return lax.dot_general(a, b, (((0,), (0,)), ((), ())), preferred_element_type=jnp.float32)
+
+
+def lane_number(width):
+    return lax.broadcasted_iota(jnp.int32, (1, width), 1)
+
+
+LANES = 128
+BLOCKS = 4
+
+
+def turn(values, cosine, signed_sine, back):
+    half = HEAD_DIM // 2
+    leading = lax.rem(lane_number(LANES), HEAD_DIM) < half
+    pieces = []
+    for at in range(0, values.shape[1], LANES):
+        piece = values[:, at : at + LANES]
+        swapped = jnp.where(leading, pltpu.roll(piece, LANES - half, 1), pltpu.roll(piece, half, 1))
+        moved = swapped * signed_sine
+        pieces.append(piece * cosine - moved if back else piece * cosine + moved)
+    return jnp.concatenate(pieces, axis=1)
+
+
+def write_bias(bias, seg_col, seg_row, i, rows, keys):
+    query_at = i * rows + lax.broadcasted_iota(jnp.int32, (rows, 1), 0)
+    key_at = lax.broadcasted_iota(jnp.int32, (1, keys), 1)
+    same = seg_col[pl.ds(i * rows, rows), :1] == seg_row[:1, :keys]
+    bias[:, :keys] = jnp.where(same & (key_at <= query_at), 0.0, neg_large)
+
+
+class Opening:
+    def __init__(self, call, inputs, segment_ids, layers, gain_rows, angle_row, places):
+        self.call, self.places = call, places
+        parts, length, width = inputs.shape
+        self.count = count = parts * length
+        (q1, k1, v1, o1, *tall1), (q2, k2, v2, o2, *tall2) = layers
+        self.shard, self.hid = shard, hid = q1.shape
+        units = tall1[0].shape[0]
+        low = jnp.bfloat16
+        self.first = [call.load(array) for array in (q1, k1, v1, o1)]
+        self.gain_rows = call.load(gain_rows)
+        self.ids, self.angle = call.load(segment_ids), call.load(angle_row)
+        self.tall = [call.load(array) for array in tall1]
+        self.second = [call.load(array) for array in (q2, k2, v2, o2)]
+        self.tall += [call.load(array) for array in tall2]
+        self.shards_one = [call.hold((shard, units), low) for _ in tall1]
+        self.shards_two = [call.store((shard, units), low) for _ in tall2]
+        self.wa_one = call.hold((shard, 4 * hid), low)
+        self.wa_two = call.store((shard, 4 * hid), low)
+        self.gains_wide = call.hold(gain_rows.shape, jnp.float32)
+        self.cosine, self.sine, self.seg_col = (
+            call.store((count, LANES), jnp.float32, BLOCKS) for _ in range(3)
+        )
+        self.seg_row = call.store((8, count), jnp.float32)
+        self.gather = Gather(call, self.wa_one, places)
+        self.deal = Deal(call, inputs)
+        self.gather_gains = Gather(call, self.gains_wide, places)
+        self.jobs = Jobs([self.gather_gains, self.deal, self.gather])
+        self.x = call.hold((count, width), low)
+        self.wa = call.hold((width, 4 * hid), low)
+        self.gain_blocks = call.hold((places,) + gain_rows.shape, jnp.float32)
+        self.gains = call.store((gain_rows.shape[0], width), jnp.float32)
+        self.flag = call.flags(2 + 2 * parts)
+
+    def tables(self):
+        return (self.cosine, self.sine, self.seg_col, self.seg_row)
+
+    def run(self, total, jobs):
+        call, hid = self.call, self.hid
+        place = Place()
+        total.bind(place)
+        place.greet(call.far)
+        call.start_loads()
+        for j, held in enumerate(self.first):
+            held.need()
+            values = held[...]
+            self.wa_one[:, j * hid : (j + 1) * hid] = values.T if j == 3 else values
+        self.gain_rows.need()
+        self.gains_wide[...] = self.gain_rows[...].astype(jnp.float32)
+        place.enter(call.far)
+        self.jobs.start(place)
+        for tall, shard in zip(self.tall, self.shards_one + self.shards_two):
+            tall.need()
+            shard[...] = tall[...].T
+            if shard.out is not None:
+                shard.put()
+        for j, held in enumerate(self.second):
+            held.need()
+            values = held[...]
+            self.wa_two[:, j * hid : (j + 1) * hid] = values.T if j == 3 else values
+        self.wa_two.put()
+        self.ids.need()
+        self.angle.need()
+        ids = self.ids[...].astype(jnp.float32)
+        mine = lax.broadcasted_iota(jnp.int32, ids.shape, 0) == place.ctx
+        own = jnp.sum(jnp.where(mine, ids, 0.0), axis=0, keepdims=True)
+        self.seg_row[...] = jnp.broadcast_to(own, self.seg_row.shape)
+        self.seg_row.put()
+        self.seg_col[...] = jnp.broadcast_to(own, (LANES, self.count)).T
+        self.seg_col.put()
+        rows = self.count // BLOCKS
+        for i in range(BLOCKS):
+            at = pl.ds(i * rows, rows)
+            index = i * rows + lax.broadcasted_iota(jnp.int32, (rows, 1), 0)
+            angles = index.astype(jnp.float32) * self.angle[:1, :]
+            self.cosine[at, :] = jnp.cos(angles)
+            self.sine[at, :] = jnp.sin(angles) * self.angle[1:2, :]
+        self.cosine.put()
+        self.sine.put()
+        self.jobs.advance(self.jobs.span)
+        jobs.start(place)
+        self.jobs.finish()
+        shard = self.shard
+        copies = [
+            pltpu.make_async_copy(
+                self.gather_gains.whole.ref, self.gain_blocks.ref, self.flag.at[0]
+            )
+        ]
+        parts = self.deal.parts
+        length = self.count // parts
+        for k in range(parts):
+            copies.append(
+                pltpu.make_async_copy(
+                    self.deal.target.at[k],
+                    self.x.at[pl.ds(k * length, length)],
+                    self.flag.at[1 + k],
+                )
+            )
+        for k in range(self.places):
+            copies.append(
+                pltpu.make_async_copy(
+                    self.gather.whole.at[k],
+                    self.wa.at[pl.ds(k * shard, shard)],
+                    self.flag.at[1 + parts],
+                )
+            )
+        for copy in copies:
+            copy.start()
+        for copy in copies:
+            copy.wait()
+        for k in range(self.places):
+            self.gains[:, k * shard : (k + 1) * shard] = self.gain_blocks[k]
+        self.gains.put()
+
+
+def attention_layer(number, x, first_v, wa, gains, which, tables, jobs_of, opening=None, span=40.0):
+    call = Call(number)
+    if opening is None:
+        start = None
+        x, gains, wa = call.load(x, BLOCKS), call.load(gains), call.load(wa)
+        cosine, sine, seg_col = (call.load(table, BLOCKS) for table in tables[:3])
+        seg_row = call.load(tables[3])
+    else:
+        start = opening(call)
+        x, gains, wa = start.x, start.gains, start.wa
+        cosine, sine, seg_col, seg_row = start.tables()
+    count, width = x.shape
+    hid = wa.shape[1] // 4
+    heads = hid // HEAD_DIM
+    rows = count // BLOCKS
+    if first_v is not None:
+        first_v = call.load(first_v, BLOCKS)
+    else:
+        v = call.store((count, hid), jnp.float32, BLOCKS)
+    x1 = call.store((count, width), jnp.float32, BLOCKS)
+    h = call.store((count, width), jnp.bfloat16, BLOCKS)
+    q, k, m, o = (call.store((count, hid), jnp.bfloat16, BLOCKS) for _ in range(4))
+    lse = call.store((heads, count, 1), jnp.float32, BLOCKS)
+    bias = call.hold((rows, count), jnp.float32)
+    acc = call.hold((rows, hid), jnp.float32)
+    total = HeadSum(call, BLOCKS, rows, width)
+    carried = jobs_of(call, start)
+    jobs = Jobs(carried, span)
+
+    def body():
+        if start is None:
+            begin(call, total, jobs)
+        else:
+            start.run(total, jobs)
+        lane = lane_number(hid)
+        for i in range(BLOCKS):
+            at = pl.ds(i * rows, rows)
+            x.need(i)
+            gains.need()
+            stream = x[at, :].astype(jnp.float32)
+            inverse = lax.rsqrt(jnp.mean(stream * stream, axis=-1, keepdims=True) + epsilon)
+            normed = (stream * inverse * gains[which : which + 1, :]).astype(jnp.bfloat16)
+            h[at, :] = normed
+            h.put(i)
+            wa.need()
+            projected = dot_nn(normed, wa[:, : 3 * hid])
+            cosine.need(i)
+            sine.need(i)
+            cos, sin = cosine[at, :], sine[at, :]
+            queries = turn(projected[:, :hid], cos, sin, False).astype(jnp.bfloat16)
+            q[at, :] = queries * jnp.bfloat16(HEAD_DIM**-0.5)
+            k[at, :] = turn(projected[:, hid : 2 * hid], cos, sin, False).astype(jnp.bfloat16)
+            values = projected[:, 2 * hid :]
+            if first_v is None:
+                v[at, :] = values
+                v.put(i)
+            else:
+                first_v.need(i)
+                values = 0.5 * values + 0.5 * first_v[at, :]
+            m[at, :] = values.astype(jnp.bfloat16)
+            for held in (q, k, m):
+                held.put(i)
+            keys = (i + 1) * rows
+            seg_col.need(i)
+            seg_row.need()
+            write_bias(bias, seg_col, seg_row, i, rows, keys)
+            jobs.advance(5.0 * i + 3.0)
+
+            def one_head(index, unused):
+                mask = lane // HEAD_DIM == index
+                query = jnp.where(mask, q[at, :], jnp.bfloat16(0))
+                scores = dot_nt(query, k[:keys, :]) + bias[:, :keys]
+                top = jnp.max(scores, axis=-1, keepdims=True)
+                exponent = jnp.exp(scores - top)
+                summed = jnp.sum(exponent, axis=-1, keepdims=True)
+                weighted = dot_nn(exponent.astype(jnp.bfloat16), m[:keys, :])
+                acc[...] = jnp.where(mask, weighted / summed, acc[...])
+                lse[index, at, :] = top + jnp.log(summed)
+                return unused
+
+            lax.fori_loop(0, heads, one_head, 0)
+            attended = acc[...].astype(jnp.bfloat16)
+            o[at, :] = attended
+            o.put(i)
+            lse.put(i)
+            total.send(i, dot_nt(attended, wa[:, 3 * hid :]))
+            if i:
+                total.middle(i - 1)
+            jobs.advance(5.0 * i + 5.5)
+        total.middle(BLOCKS - 1)
+        for i in range(BLOCKS):
+            total.last(i)
+            jobs.advance(23.0 + 4.0 * i)
+        for i in range(BLOCKS):
+            at = pl.ds(i * rows, rows)
+            x1[at, :] = x[at, :].astype(jnp.float32) + total.total(i)
+            x1.put(i)
+        jobs.finish()
+
+    call.run(body)
+    return SimpleNamespace(
+        x1=x1.result,
+        h=h.result,
+        q=q.result,
+        k=k.result,
+        m=m.result,
+        o=o.result,
+        lse=lse.result,
+        v=v.result if first_v is None else None,
+        carried=[job.result for job in carried],
+        start=start,
+    )
+
+
+def feed_forward_layer(number, x1, gate, up, down, gains, which, jobs_of, span=30.0):
+    count, width = x1.shape
+    units = gate.shape[1]
+    rows = count // BLOCKS
+    call = Call(number)
+    x1 = call.load(x1, BLOCKS)
+    gains, gate, up, down = (call.load(array) for array in (gains, gate, up, down))
+    y = call.store_from(x1, (count, width), jnp.float32, BLOCKS)
+    y_low, h2 = (call.store((count, width), jnp.bfloat16, BLOCKS) for _ in range(2))
+    z, u, a = (call.store((count, units), jnp.bfloat16, BLOCKS) for _ in range(3))
+    total = HeadSum(call, BLOCKS, rows, width)
+    carried = jobs_of(call)
+    jobs = Jobs(carried, span)
+
+    def body():
+        begin(call, total, jobs)
+        for i in range(BLOCKS):
+            at = pl.ds(i * rows, rows)
+            x1.need(i)
+            gains.need()
+            stream = x1[at, :]
+            inverse = lax.rsqrt(jnp.mean(stream * stream, axis=-1, keepdims=True) + epsilon)
+            normed = (stream * inverse * gains[which : which + 1, :]).astype(jnp.bfloat16)
+            h2[at, :] = normed
+            gate.need()
+            gated = dot_nn(normed, gate[...])
+            up.need()
+            raised = dot_nn(normed, up[...])
+            active = (gated * lax.logistic(gated) * raised).astype(jnp.bfloat16)
+            z[at, :] = gated.astype(jnp.bfloat16)
+            u[at, :] = raised.astype(jnp.bfloat16)
+            a[at, :] = active
+            for held in (h2, z, u, a):
+                held.put(i)
+            down.need()
+            total.send(i, dot_nt(active, down[...]))
+            if i:
+                total.middle(i - 1)
+            jobs.advance(2.5 * i + 4.0)
+        total.middle(BLOCKS - 1)
+        for i in range(BLOCKS):
+            total.last(i)
+            jobs.advance(14.0 + 5.0 * i)
+        for i in range(BLOCKS):
+            at = pl.ds(i * rows, rows)
+            result = x1[at, :] + total.total(i)
+            x1[at, :] = result
+            y_low[at, :] = result.astype(jnp.bfloat16)
+            y.put(i)
+            y_low.put(i)
+        jobs.finish()
+
+    call.run(body)
+    return SimpleNamespace(
+        y=y.result,
+        y_low=y_low.result,
+        h2=h2.result,
+        z=z.result,
+        u=u.result,
+        a=a.result,
+        carried=[job.result for job in carried],
+    )
+
+
+def norm_back(gain, grad, stream, gain_sum):
+    inverse = lax.rsqrt(jnp.mean(stream * stream, axis=-1, keepdims=True) + epsilon)
+    scaled = stream * inverse
+    grad_scaled = grad * gain
+    products = jnp.mean(grad_scaled * scaled, axis=-1, keepdims=True)
+    gain_sum = gain_sum + jnp.sum(grad * scaled, axis=0, keepdims=True)
+    return inverse * (grad_scaled - scaled * products), gain_sum
+
+
+def feed_forward_back(number, gy, x1, saved, gate, up, down, gains, which, jobs_of, span=30.0):
+    count, width = x1.shape
+    units = gate.shape[1]
+    rows = count // BLOCKS
+    call = Call(number)
+    gy = call.load(gy, BLOCKS)
+    a, down = call.load(saved.a), call.load(down)
+    z, u = call.load(saved.z, BLOCKS), call.load(saved.u, BLOCKS)
+    gate, up, h2, gains = (call.load(w) for w in (gate, up, saved.h2, gains))
+    x1 = call.load(x1, BLOCKS)
+    gx1 = call.store_from(x1, (count, width), jnp.float32, BLOCKS)
+    gain = call.store((1, width), jnp.float32)
+    d_gate, d_up = (call.store((width, units), jnp.bfloat16, 4) for _ in range(2))
+    places = lax.axis_size(DP) * lax.axis_size(CTX)
+    shard = width // places
+    d_down = call.hold((places, shard, units), jnp.bfloat16)
+    low = call.hold((count, width), jnp.bfloat16)
+    gz, gu = (call.hold((count, units), jnp.bfloat16) for _ in range(2))
+    total = HeadSum(call, BLOCKS, rows, width)
+    down_sum = Scatter(call, d_down)
+    carried = jobs_of(call, down_sum)
+    jobs = Jobs(carried, span)
+
+    def body():
+        begin(call, total, jobs)
+        for i in range(BLOCKS):
+            at = pl.ds(i * rows, rows)
+            gy.need(i)
+            low[at, :] = gy[at, :].astype(jnp.bfloat16)
+        a.need()
+        for j in range(places // 2):
+            cut = slice(j * 2 * shard, (j + 1) * 2 * shard)
+            part = dot_tn(low[:, cut], a[...]).astype(jnp.bfloat16)
+            d_down[2 * j : 2 * j + 2] = part.reshape(2, shard, units)
+        down_sum.start()
+        for i in range(BLOCKS):
+            at = pl.ds(i * rows, rows)
+            down.need()
+            ga = dot_nn(low[at, :], down[...])
+            z.need(i)
+            u.need(i)
+            gated = z[at, :].astype(jnp.float32)
+            sigma = lax.logistic(gated)
+            raised = u[at, :].astype(jnp.float32)
+            slope = sigma * (1.0 + gated * (1.0 - sigma))
+            gz[at, :] = (ga * raised * slope).astype(jnp.bfloat16)
+            gu[at, :] = (ga * gated * sigma).astype(jnp.bfloat16)
+            gate.need()
+            up.need()
+            total.send(i, dot_nt(gz[at, :], gate[...]) + dot_nt(gu[at, :], up[...]))
+            if i:
+                total.middle(i - 1)
+            jobs.advance(2.5 * i + 6.0)
+        total.middle(BLOCKS - 1)
+        cols = width // 4
+        h2.need()
+        for reached, left, right, out in ((17.0, h2, gz, d_gate), (20.0, h2, gu, d_up)):
+            for j in range(4):
+                cut = slice(j * cols, (j + 1) * cols)
+                out[cut, :] = dot_tn(left[:, cut], right[...]).astype(jnp.bfloat16)
+                out.put(j)
+            jobs.advance(reached)
+        gains.need()
+        for i in range(BLOCKS):
+            total.last(i)
+            jobs.advance(22.0 + 4.0 * i)
+        gain_sum = jnp.zeros((1, width), jnp.float32)
+        for i in range(BLOCKS):
+            at = pl.ds(i * rows, rows)
+            x1.need(i)
+            step, gain_sum = norm_back(
+                gains[which : which + 1, :], total.total(i), x1[at, :], gain_sum
+            )
+            x1[at, :] = gy[at, :].astype(jnp.float32) + step
+            gx1.put(i)
+        gain[...] = gain_sum
+        gain.put()
+        jobs.finish()
+
+    call.run(body)
+    return SimpleNamespace(
+        gx1=gx1.result,
+        gain=gain.result,
+        d_gate=d_gate.result,
+        d_up=d_up.result,
+        carried=[job.result for job in carried],
+    )
+
+
+def attention_back(number, gx1, x, saved, extra, wa, gains, which, tables, jobs_of, span=50.0):
+    count, width = x.shape
+    hid = wa.shape[1] // 4
+    heads = hid // HEAD_DIM
+    rows = count // BLOCKS
+    call = Call(number)
+    gx1, wa = call.load(gx1, BLOCKS), call.load(wa)
+    q, k, m, o = (
+        call.load(array, blocks)
+        for array, blocks in ((saved.q, BLOCKS), (saved.k, 1), (saved.m, 1), (saved.o, BLOCKS))
+    )
+    lse = call.load(saved.lse, BLOCKS)
+    cosine, sine, seg_col = (call.load(table, BLOCKS) for table in tables[:3])
+    seg_row = call.load(tables[3])
+    if extra is not None:
+        extra = call.load(extra, BLOCKS)
+    h, gains, x = call.load(saved.h), call.load(gains), call.load(x, BLOCKS)
+    if extra is not None:
+        gx = call.store((count, width), jnp.bfloat16, BLOCKS)
+        gx_held = gx
+    else:
+        gx_held = gx1
+        gx = call.store_from(gx1, (count, width), jnp.float32, BLOCKS)
+        passed = call.store((count, hid), jnp.float32, BLOCKS)
+    gain = call.store((1, width), jnp.float32)
+    d_wa = call.store((width, 4 * hid), jnp.bfloat16, 4)
+    low = call.hold((count, width), jnp.bfloat16)
+    bias = call.hold((rows, count), jnp.float32)
+    go = call.hold((rows, hid), jnp.bfloat16)
+    gq = call.hold((rows, hid), jnp.float32)
+    gk, gm = (call.hold((count, hid), jnp.float32) for _ in range(2))
+    g3 = call.hold((count, 3 * hid), jnp.bfloat16)
+    total = HeadSum(call, BLOCKS, rows, width)
+    carried = jobs_of(call)
+    jobs = Jobs(carried, span)
+
+    def body():
+        begin(call, total, jobs, True)
+        lane = lane_number(hid)
+        gk[...] = jnp.zeros(gk.shape, gk.dtype)
+        gm[...] = jnp.zeros(gm.shape, gm.dtype)
+        order = list(range(BLOCKS))[::-1]
+        for turn_index, i in enumerate(order):
+            at = pl.ds(i * rows, rows)
+            gx1.need(i)
+            low[at, :] = gx1[at, :].astype(jnp.bfloat16)
+            wa.need()
+            go[...] = dot_nn(low[at, :], wa[:, 3 * hid :]).astype(jnp.bfloat16)
+            keys = (i + 1) * rows
+            for held in (seg_row, seg_col, q, o, lse, k, m):
+                held.need(i)
+            write_bias(bias, seg_col, seg_row, i, rows, keys)
+            gq[...] = jnp.zeros(gq.shape, gq.dtype)
+
+            def one_head(index, unused):
+                mask = lane // HEAD_DIM == index
+                zero = jnp.bfloat16(0)
+                query = jnp.where(mask, q[at, :], zero)
+                grad = jnp.where(mask, go[...], zero)
+                both = grad.astype(jnp.float32) * o[at, :].astype(jnp.float32)
+                delta = jnp.sum(both, axis=-1, keepdims=True)
+                scores = dot_nt(query, k[:keys, :]) + bias[:, :keys]
+                prob = jnp.exp(scores - lse[index, at, :])
+                grad_prob = dot_nt(grad, m[:keys, :])
+                grad_score = (prob * (grad_prob - delta)).astype(jnp.bfloat16)
+                part = dot_nn(grad_score, k[:keys, :])
+                gq[...] = jnp.where(mask, part, gq[...])
+                gk[:keys, :] += dot_tn(grad_score, query)
+                gm[:keys, :] += dot_tn(prob.astype(jnp.bfloat16), grad)
+                return unused
+
+            lax.fori_loop(0, heads, one_head, 0)
+            cosine.need(i)
+            sine.need(i)
+            cos, sin = cosine[at, :], sine[at, :]
+            values = gm[at, :]
+            if extra is None:
+                values = 0.5 * values
+                passed[at, :] = values
+                passed.put(i)
+            else:
+                extra.need(i)
+                values = values + extra[at, :]
+            back = turn(gq[...] * HEAD_DIM**-0.5, cos, sin, True)
+            g3[at, :hid] = back.astype(jnp.bfloat16)
+            g3[at, hid : 2 * hid] = turn(gk[at, :], cos, sin, True).astype(jnp.bfloat16)
+            g3[at, 2 * hid :] = values.astype(jnp.bfloat16)
+            total.send(i, dot_nt(g3[at, :], wa[:, : 3 * hid]))
+            if turn_index:
+                total.middle(order[turn_index - 1])
+            jobs.advance((8.0, 14.0, 18.0, 21.0)[turn_index])
+        total.middle(order[-1])
+        cols = width // 4
+        h.need()
+        for j in range(4):
+            cut = slice(j * cols, (j + 1) * cols)
+            d_wa[cut, : 3 * hid] = dot_tn(h[:, cut], g3[...]).astype(jnp.bfloat16)
+            d_wa[cut, 3 * hid :] = dot_tn(low[:, cut], o[...]).astype(jnp.bfloat16)
+            d_wa.put(j)
+        jobs.advance(25.0)
+        gains.need()
+        for turn_index, i in enumerate(order):
+            total.last(i)
+            jobs.advance(28.0 + 4.0 * turn_index)
+        gain_sum = jnp.zeros((1, width), jnp.float32)
+        for i in order:
+            at = pl.ds(i * rows, rows)
+            x.need(i)
+            stream = x[at, :].astype(jnp.float32)
+            step, gain_sum = norm_back(
+                gains[which : which + 1, :], total.total(i), stream, gain_sum
+            )
+            gx_held[at, :] = (gx1[at, :] + step).astype(gx_held.dtype)
+            gx.put(i)
+        gain[...] = gain_sum
+        gain.put()
+        jobs.finish()
+
+    call.run(body)
+    return SimpleNamespace(
+        gx=gx.result,
+        passed=passed.result if extra is None else None,
+        gain=gain.result,
+        d_wa=d_wa.result,
+        carried=[job.result for job in carried],
+    )
+
+
+def transfers(number, jobs_of, order):
+    call = Call(number)
+    carried = jobs_of(call)
+    jobs = Jobs(carried, order=order)
+
+    def body():
+        begin(call, None, jobs)
+        jobs.finish()
+
+    call.run(body)
+    return [job.result for job in carried]
+
+
+def leave_step(moved, grad, packs, turned, gains):
+    call = Call(0)
+    kept = [call.load(array, BLOCKS) for array in moved]
+    kept_to = [call.store_from(held, held.shape, held.dtype, BLOCKS) for held in kept]
+    grad = call.load(grad, BLOCKS)
+    wide = call.store(grad.shape, jnp.float32, BLOCKS)
+    shard, hid = packs[0].shape[0], packs[0].shape[1] // 4
+    flag = call.flags(3 * len(packs))
+    packs = [call.load(array) for array in packs]
+    unpacked = [[call.give((shard, hid), pack.dtype) for _ in range(3)] for pack in packs]
+    upright = [call.store((hid, shard), pack.dtype) for pack in packs]
+    turned = [call.load(array) for array in turned]
+    turned_to = [call.store(held.shape[::-1], held.dtype) for held in turned]
+    gains = call.load(gains)
+    gain_to = [call.store((1, shard), gains.dtype) for _ in range(4)]
+
+    def body():
+        call.start_loads()
+        copies = []
+        for at, pack in enumerate(packs):
+            pack.need()
+            for j in range(3):
+                source = pack.at[:, j * hid : (j + 1) * hid]
+                copies.append(
+                    pltpu.make_async_copy(source, unpacked[at][j].ref, flag.at[3 * at + j])
+                )
+                copies[-1].start()
+            upright[at][...] = pack[:, 3 * hid :].T
+            upright[at].put()
+        for held, target in zip(turned, turned_to):
+            held.need()
+            target[...] = held[...].T
+            target.put()
+        gains.need()
+        for j, target in enumerate(gain_to):
+            target[...] = gains[j : j + 1, :]
+            target.put()
+        rows = grad.shape[0] // BLOCKS
+        for i in range(BLOCKS):
+            at = pl.ds(i * rows, rows)
+            grad.need(i)
+            wide[at, :] = grad[at, :].astype(jnp.float32)
+            wide.put(i)
+            for held, target in zip(kept, kept_to):
+                held.need(i)
+                target.put(i)
+        for copy in copies:
+            copy.wait()
+
+    call.run(body, False)
+    return SimpleNamespace(
+        kept=[target.result for target in kept_to],
+        grad=wide.result,
+        packs=[
+            [part.result for part in parts] + [last.result]
+            for parts, last in zip(unpacked, upright)
+        ],
+        turned=[target.result for target in turned_to],
+        gains=[target.result.reshape(-1) for target in gain_to],
+    )
+
+
+def dealt_device(
+    inputs,
+    segment_ids,
+    norm_attn_one,
+    query_one,
+    key_one,
+    value_one,
+    output_one,
+    norm_ffn_one,
+    gate_one,
+    up_one,
+    down_one,
+    norm_attn_two,
+    query_two,
+    key_two,
+    value_two,
+    output_two,
+    norm_ffn_two,
+    gate_two,
+    up_two,
+    down_two,
+    cotangent,
+):
+    parts, length, width = inputs.shape
+    places = lax.axis_size(DP) * lax.axis_size(CTX)
+    shard = width // places
+    gain_rows = jnp.stack([norm_attn_one, norm_ffn_one, norm_attn_two, norm_ffn_two] * 2)
+    half = HEAD_DIM // 2
+    frequency = 10000.0 ** (-np.arange(half, dtype=np.float32) / np.float32(half))
+    repeat = LANES // HEAD_DIM
+    signs = np.concatenate([-np.ones(half), np.ones(half)])
+    angle_row = np.zeros((8, LANES), np.float32)
+    angle_row[0] = np.tile(frequency, 2 * repeat)
+    angle_row[1] = np.tile(signs, repeat)
+
+    def split(array):
+        return array.reshape(places, shard, array.shape[-1])
+
+    def deal(array):
+        return array.reshape(parts, length, width)
+
+    def opening(call):
+        return Opening(
+            call,
+            inputs,
+            segment_ids,
+            (
+                (query_one, key_one, value_one, output_one, gate_one.T, up_one.T, down_one),
+                (query_two, key_two, value_two, output_two, gate_two.T, up_two.T, down_two),
+            ),
+            gain_rows,
+            jnp.asarray(angle_row),
+            places,
+        )
+
+    attn_one = attention_layer(
+        1,
+        None,
+        None,
+        None,
+        None,
+        0,
+        None,
+        lambda c, start: [Gather(c, held, places) for held in start.shards_one],
+        opening,
+        26.0,
+    )
+    start = attn_one.start
+    x, wa_one, gains = start.deal.result, start.gather.result, start.gains.result
+    tables = [table.result for table in start.tables()]
+    ffn_one_w = attn_one.carried
+    wa_two_shard = start.wa_two.result
+    shards_two = [held.result for held in start.shards_two]
+    ffn_one = feed_forward_layer(
+        2,
+        attn_one.x1,
+        *ffn_one_w,
+        gains,
+        1,
+        lambda c: [Gather(c, wa_two_shard, places), Gather(c, shards_two[0], places)],
+        30.0,
+    )
+    wa_two, gate_two_w = ffn_one.carried
+    attn_two = attention_layer(
+        3,
+        ffn_one.y,
+        attn_one.v,
+        wa_two,
+        gains,
+        2,
+        tables,
+        lambda c, start: [Gather(c, array, places) for array in shards_two[1:]],
+        span=26.0,
+    )
+    ffn_two_w = (gate_two_w, *attn_two.carried)
+    ffn_two = feed_forward_layer(
+        4,
+        attn_two.x1,
+        *ffn_two_w,
+        gains,
+        3,
+        lambda c: [Deal(c, cotangent, True), Deal(c, deal(ffn_one.y_low))],
+        90.0,
+    )
+    out_one = ffn_two.carried[1]
+    back_ffn_two = feed_forward_back(
+        5,
+        ffn_two.carried[0],
+        attn_two.x1,
+        ffn_two,
+        *ffn_two_w,
+        gains,
+        3,
+        lambda c, down_sum: [down_sum, Deal(c, deal(ffn_two.y_low), True)],
+        36.0,
+    )
+    down_g2, out_two = back_ffn_two.carried
+
+    def ffn_grads(back):
+        return lambda c: [Scatter(c, split(array)) for array in (back.d_gate, back.d_up)]
+
+    back_attn_two = attention_back(
+        6,
+        back_ffn_two.gx1,
+        ffn_one.y,
+        attn_two,
+        None,
+        wa_two,
+        gains,
+        2,
+        tables,
+        ffn_grads(back_ffn_two),
+    )
+    back_ffn_one = feed_forward_back(
+        7,
+        back_attn_two.gx,
+        attn_one.x1,
+        ffn_one,
+        *ffn_one_w,
+        gains,
+        1,
+        lambda c, down_sum: [Scatter(c, split(back_attn_two.d_wa)), down_sum],
+        40.0,
+    )
+    packed_two, down_g1 = back_ffn_one.carried
+    back_attn_one = attention_back(
+        8,
+        back_ffn_one.gx1,
+        x,
+        attn_one,
+        back_attn_two.passed,
+        wa_one,
+        gains,
+        0,
+        tables,
+        ffn_grads(back_ffn_one),
+    )
+    gain_grads = jnp.concatenate(
+        [back_attn_one.gain, back_ffn_one.gain, back_attn_two.gain, back_ffn_two.gain] * 2
+    )
+    gain_grads = jnp.transpose(gain_grads.reshape(-1, places, shard), (1, 0, 2))
+    gain_shards, packed_one, grad = transfers(
+        9,
+        lambda c: [
+            Scatter(c, gain_grads),
+            Scatter(c, split(back_attn_one.d_wa)),
+            Deal(c, deal(back_attn_one.gx)),
+        ],
+        (1, 0, 2, 0, 1, 0, 2, 2, 0, 1, 2, 2, 2, 1),
+    )
+    final = leave_step(
+        (out_one, out_two),
+        grad,
+        (packed_one, packed_two),
+        back_attn_one.carried + [down_g1] + back_attn_two.carried + [down_g2],
+        gain_shards,
+    )
+    gate_g1, up_g1, down_g1, gate_g2, up_g2, down_g2 = final.turned
+    return (
+        deal(final.kept[0]),
+        deal(final.kept[1]),
+        deal(final.grad),
+        final.gains[0],
+        *final.packs[0],
+        final.gains[1],
+        gate_g1.T,
+        up_g1.T,
+        down_g1,
+        final.gains[2],
+        *final.packs[1],
+        final.gains[3],
+        gate_g2.T,
+        up_g2.T,
+        down_g2,
+    )
+
+
 def solution(mesh):
     placed = (
-        P("dp", "ctx", None),
-        P("dp", None),
-        P(("dp", "ctx")),
-        P(("dp", "ctx"), "mp"),
-        P(("dp", "ctx"), "mp"),
-        P(("dp", "ctx"), "mp"),
-        P("mp", ("dp", "ctx")),
-        P(("dp", "ctx")),
-        P(("dp", "ctx"), "mp"),
-        P(("dp", "ctx"), "mp"),
-        P("mp", ("dp", "ctx")),
-        P(("dp", "ctx")),
-        P(("dp", "ctx"), "mp"),
-        P(("dp", "ctx"), "mp"),
-        P(("dp", "ctx"), "mp"),
-        P("mp", ("dp", "ctx")),
-        P(("dp", "ctx")),
-        P(("dp", "ctx"), "mp"),
-        P(("dp", "ctx"), "mp"),
-        P("mp", ("dp", "ctx")),
-        P("dp", "ctx", None),
-    )
+        P(DP, CTX, None),
+        P(DP, None),
+        P((DP, CTX)),
+        P((DP, CTX), MP),
+        P((DP, CTX), MP),
+        P((DP, CTX), MP),
+        P(MP, (DP, CTX)),
+        P((DP, CTX)),
+        P((DP, CTX), MP),
+        P((DP, CTX), MP),
+        P(MP, (DP, CTX)),
+        P((DP, CTX)),
+        P((DP, CTX), MP),
+        P((DP, CTX), MP),
+        P((DP, CTX), MP),
+        P(MP, (DP, CTX)),
+        P((DP, CTX)),
+        P((DP, CTX), MP),
+        P((DP, CTX), MP),
+        P(MP, (DP, CTX)),
+        P(DP, CTX, None),
+    )
+    sizes = dict(mesh.shape)
+
+    def per_device(*operands):
+        fits = sizes[DP] == 2 and sizes[MP] == 4 and operands[0].shape[0] == sizes[CTX]
+        return (dealt_device if fits else on_device)(*operands)
+
     return jax.shard_map(
-        on_device,
+        per_device,
         mesh=mesh,
         in_specs=placed,
         out_specs=(
-            P("dp", "ctx", None),
-            P("dp", "ctx", None),
-            P("dp", "ctx", None),
-            P(("dp", "ctx")),
-            P(("dp", "ctx"), "mp"),
-            P(("dp", "ctx"), "mp"),
-            P(("dp", "ctx"), "mp"),
-            P("mp", ("dp", "ctx")),
-            P(("dp", "ctx")),
-            P(("dp", "ctx"), "mp"),
-            P(("dp", "ctx"), "mp"),
-            P("mp", ("dp", "ctx")),
-            P(("dp", "ctx")),
-            P(("dp", "ctx"), "mp"),
-            P(("dp", "ctx"), "mp"),
-            P(("dp", "ctx"), "mp"),
-            P("mp", ("dp", "ctx")),
-            P(("dp", "ctx")),
-            P(("dp", "ctx"), "mp"),
-            P(("dp", "ctx"), "mp"),
-            P("mp", ("dp", "ctx")),
+            P(DP, CTX, None),
+            P(DP, CTX, None),
+            P(DP, CTX, None),
+            P((DP, CTX)),
+            P((DP, CTX), MP),
+            P((DP, CTX), MP),
+            P((DP, CTX), MP),
+            P(MP, (DP, CTX)),
+            P((DP, CTX)),
+            P((DP, CTX), MP),
+            P((DP, CTX), MP),
+            P(MP, (DP, CTX)),
+            P((DP, CTX)),
+            P((DP, CTX), MP),
+            P((DP, CTX), MP),
+            P((DP, CTX), MP),
+            P(MP, (DP, CTX)),
+            P((DP, CTX)),
+            P((DP, CTX), MP),
+            P((DP, CTX), MP),
+            P(MP, (DP, CTX)),
         ),
         check_vma=False,
     )

time: 1370 us -> 510 us (0.37)
  waiting for transfers between devices: 718 us -> 0 us
  Pallas kernels: 227 us -> 499 us
  matrix products: 151 us -> 0 us
  local copies, waits for them, and re-layouts: 141 us -> 2.79 us
  other arithmetic: 47.8 us -> 0 us
  blocking collectives: 40.1 us -> 0 us
  between operations: 17.9 us -> 0.99 us
    unnamed x18 -> x0, waiting for transfers between devices: 284 us -> none
    pallas_call x8 -> x10, Pallas kernels: 227 us -> 499 us  [run(): pl.pallas_call(kernel, out_shape=tuple(self.shapes), in_specs=[space] * i...]
    all_gather x6 -> x0, waiting for transfers between devices: 217 us -> none  [the longest x2 92.4 us: gather_layer(): whole = lax.all_gather(packed, both, axis=0, tiled=True)]
    reduce_scatter x4 -> x0, waiting for transfers between devices: 216 us -> none  [the longest x2 145 us: attend_back_gather(): lax.psum_scatter(key_grad.reshape(seq_count, length, -1).astype(jnp.bfloa...]
    dot_general x56 -> x0, matrix products: 151 us -> none  [the longest x14 43.5 us: project_back(): jnp.einsum('sbe,de->sbd', left_operand, right_operand, preferred_element_...]
    unnamed x224 -> x6, local copies, waits for them, and re-layouts: 56.2 us -> 0.01 us
    dynamic_update_slice x4 -> x0, local copies, waits for them, and re-layouts: 41.6 us -> none  [the longest x2 20.8 us: attend_compute(): key_acc = lax.dynamic_update_slice_in_dim(key_acc, key_part, first_key, 1)]
    all_gather x2 -> x0, blocking collectives: 40.1 us -> none  [gather_layer(): lax.all_gather(jnp.stack([gain_attn, gain_ffn]), both, axis=1, tiled=True)]
  transfers between devices with their start and end apart: 14 -> 0, of which waited for: 13 -> 0; matrix products, arithmetic and copies ran while one was open for 12% -> 0% of each run, Pallas kernels for 6% -> 0%
where the time goes in v3:
time: 510 us; the launch traced here: 503 us
  Pallas kernels  499 us (98%)
    pallas_call x10, Pallas kernels, run(): pl.pallas_call(kernel, out_shape=tuple(self.shapes), in_specs=[space] * i...  499 us

profile of v3, /device:TPU:0, one launch (start us, length us, event | category | flops | bytes accessed | tf_op | source)
XLA Modules:
  0.0 503.0 jit_solution(18210647196789230602)
XLA Ops:
  0.7 1.4 stack.23.refs_4_
  2.0 102.6 %shard_map.373 = (bf16[128,704]{1,0:T(8,128)(2,1)}, bf16[128,704]{1,0:T(8,128)(2,1)}, bf16[128,704]{1,0:T(8,128)(2,1)}, bf16[128,1024]{1,0:T(8,128)(2,1)}, f32[1...) custom-call(bf16[128,256]{1,0:T(8,128)(2,1)} %refs_0_.1, ...), custom_call_target="tpu_custom_call" | custom-call | tf_op jit(solution)/shard_map/pallas_call | solution.py:776
  104.7 46.8 %shard_map.374 = (f32[1024,1024]{1,0:T(8,128)}, bf16[1024,1024]{1,0:T(8,128)(2,1)}, bf16[1024,1024]{1,0:T(8,128)(2,1)}, bf16[1024,704]{1,0:T(8,128)(2,1)}, bf16[...) custom-call(f32[1024,1024]{1,0:T(8,128)} %get-tuple-element.114.refs, ...), custom_call_target="tpu_custom_call" | custom-call | tf_op jit(solution)/shard_map/pallas_call | solution.py:776
  151.5 48.3 %shard_map.375 = (f32[1024,1024]{1,0:T(8,128)}, bf16[1024,1024]{1,0:T(8,128)(2,1)}, bf16[1024,256]{1,0:T(8,128)(2,1)}, bf16[1024,256]{1,0:T(8,128)(2,1)}, bf16[1...) custom-call(f32[1024,1024]{1,0:T(8,128)} %get-tuple-element.121.refs, ...), custom_call_target="tpu_custom_call" | custom-call | tf_op jit(solution)/shard_map/pallas_call | solution.py:776
  199.8 51.7 %shard_map.376 = (f32[1024,1024]{1,0:T(8,128)}, bf16[1024,1024]{1,0:T(8,128)(2,1)}, bf16[1024,1024]{1,0:T(8,128)(2,1)}, bf16[1024,704]{1,0:T(8,128)(2,1)}, bf16[...) custom-call(f32[1024,1024]{1,0:T(8,128)} %get-tuple-element.130.refs, ...), custom_call_target="tpu_custom_call" | custom-call | tf_op jit(solution)/shard_map/pallas_call | solution.py:776
  251.5 46.5 %shard_map.377 = (f32[1024,1024]{1,0:T(8,128)}, f32[1,1024]{1,0:T(1,128)}, bf16[1024,704]{1,0:T(8,128)(2,1)}, bf16[1024,704]{1,0:T(8,128)(2,1)}, f32[128,704]{1,0:T(8,128)}, /*index=5*/bf16[4,256,1024]{2,1,0:T(8,128)(2,1)}) custom-call(bf16[1024,1024]{1,0:T(8,128)(2,1)} %bitcast.62, bf16[1024,704]{1,0:T(8,128)(2,1)} %get-tuple-element.137.refs_1_, ...), custom_call_target="tpu_custom_call" | custom-call | tf_op jit(solution)/shard_map/pallas_call | solution.py:776
  298.0 52.9 %shard_map.378 = (f32[1024,1024]{1,0:T(8,128)}, f32[1024,256]{1,0:T(8,128)}, f32[1,1024]{1,0:T(1,128)}, bf16[1024,1024]{1,0:T(8,128)(2,1)}, f32[128,704]{1,0:T(8,128)}, /*index=5*/f32[128,704]{1,0:T(8,128)}) custom-call(f32[1024,1024]{1,0:T(8,128)} %get-tuple-element.143.refs_0_, bf16[1024,1024]{1,0:T(8,128)(2,1)} %bitcast.45, ...), custom_call_target="tpu_custom_call" | custom-call | tf_op jit(solution)/shard_map/pallas_call | solution.py:776
  350.9 53.7 %shard_map.379 = (f32[1024,1024]{1,0:T(8,128)}, f32[1,1024]{1,0:T(1,128)}, bf16[1024,704]{1,0:T(8,128)(2,1)}, bf16[1024,704]{1,0:T(8,128)(2,1)}, f32[128,704]{1,0:T(8,128)}, /*index=5*/f32[128,1024]{1,0:T(8,128)}) custom-call(f32[1024,1024]{1,0:T(8,128)} %get-tuple-element.152.refs_0_, bf16[1024,704]{1,0:T(8,128)(2,1)} %get-tuple-element.153.refs_1_, ...), custom_call_target="tpu_custom_call" | custom-call | tf_op jit(solution)/shard_map/pallas_call | solution.py:776
  404.6 0.0 copy-start
  404.6 0.0 copy-start.1
  404.6 0.0 copy-start.2
  404.6 53.7 %shard_map.380 = (bf16[1024,1024]{1,0:T(8,128)(2,1)}, f32[1,1024]{1,0:T(1,128)}, bf16[1024,1024]{1,0:T(8,128)(2,1)}, f32[128,704]{1,0:T(8,128)}, f32[128,704]{1,0:T(8,128)}) custom-call(f32[1024,1024]{1,0:T(8,128)} %get-tuple-element.158.refs_0_, bf16[1024,1024]{1,0:T(8,128)(2,1)} %bitcast.58, bf16[1024,256]{1,0:T(8,128)(2,1)} %get-tuple-element.160.refs_2_, ...), custom_call_target="tpu_custom_call" | custom-call | tf_op jit(solution)/shard_map/pallas_call | solution.py:776
  458.4 0.0 copy-done
  458.4 0.0 copy-done.1
  458.4 0.0 copy-done.2
  458.4 1.4 concatenate.3
  459.8 35.4 %shard_map.381 = (f32[8,128]{1,0:T(8,128)}, f32[128,1024]{1,0:T(8,128)}, bf16[4,256,1024]{2,1,0:T(8,128)(2,1)}) custom-call(f32[8,8,128]{2,1,0:T(8,128)} %bitcast.77, bf16[8,128,1024]{2,1,0:T(8,128)(2,1)} %bitcast.64, bf16[4,256,1024]{2,1,0:T(8,128)(2,1)} %bitcast.63), custom_call_target="tpu_custom_call" | custom-call | tf_op jit(solution)/shard_map/pallas_call | solution.py:776
  495.2 7.6 %shard_map.382 = (bf16[1024,1024]{1,0:T(8,128)(2,1)}, bf16[1024,1024]{1,0:T(8,128)(2,1)}, f32[1024,1024]{1,0:T(8,128)}, f32[128,256]{1,0:T(8,128)}, f32[128,256]...) custom-call(bf16[1024,1024]{1,0:T(8,128)(2,1)} %bitcast.65, ...), custom_call_target="tpu_custom_call" | custom-call | tf_op jit(solution)/shard_map/pallas_call | solution.py:776
Async XLA Ops:
  404.6 53.8 %copy-start = (f32[1,1024]{1,0:T(1,128)S(1)}, f32[1,1024]{1,0:T(1,128)}, u32[]{:S(2)}) copy-start(f32[1,1024]{1,0:T(1,128)} %get-tuple-element.173) | copy-start | bytes 12292
  404.6 53.8 %copy-start.1 = (f32[1,1024]{1,0:T(1,128)S(1)}, f32[1,1024]{1,0:T(1,128)}, u32[]{:S(2)}) copy-start(f32[1,1024]{1,0:T(1,128)} %get-tuple-element.172) | copy-start | bytes 12292
  404.6 53.8 %copy-start.2 = (f32[1,1024]{1,0:T(1,128)S(1)}, f32[1,1024]{1,0:T(1,128)}, u32[]{:S(2)}) copy-start(f32[1,1024]{1,0:T(1,128)} %get-tuple-element.171) | copy-start | bytes 12292

commit v4 on v3

--- a/solution.py
+++ b/solution.py
@@ -716,7 +716,7 @@
         self.number = number
         self.operands, self.shapes, self.scratch = [], [], []
         self.loads, self.stores, self.jobs = [], [], []
-        self.far = False
+        self.far = self.in_turn = False
 
     def take(self, array):
         self.operands.append(array)
@@ -754,6 +754,11 @@
         return Store(self, held, shape, dtype, blocks)
 
     def start_loads(self, backward=False):
+        if self.in_turn:
+            for held in self.loads:
+                for k in range(held.blocks):
+                    held.load_copy(k).start()
+            return
         for k in range(max([held.blocks for held in self.loads], default=0)):
             for held in self.loads:
                 if k < held.blocks:
@@ -892,19 +897,24 @@
 
 
 class Gather:
-    def __init__(self, call, shard, places):
+    def __init__(self, call, shard, places, swap=False):
         self.parts = lax.axis_size(CTX)
         call.far = True
-        self.shard = shard if isinstance(shard, Held) else call.load(shard)
+        if isinstance(shard, Held):
+            self.shard = shard
+        else:
+            self.shard = call.load(shard)
+            call.loads.insert(0, call.loads.pop())
         self.whole = call.give((places,) + shard.shape, shard.dtype)
         self.zs, self.zr, self.ys, self.yr = (call.flags(self.parts) for _ in range(4))
-        self.l = call.flags(1)
+        self.l, self.ss, self.sr = (call.flags(1) for _ in range(3))
         self.relayed = self.parts == 4
+        self.swap = swap and self.relayed
         self.order = (2, 1, 3) if self.relayed else tuple(range(self.parts - 1, 0, -1))
         self.steps = len(self.order)
 
     def bind(self, place):
-        self.place = place
+        self.place, self.crossed = place, False
 
     def slot(self, dp, ctx):
         return self.whole.at[dp * self.parts + ctx]
@@ -937,11 +947,34 @@
         source = self.shard.ref if s == 0 else block
         return remote(source, block, self.ys.at[s], self.yr.at[s], p.other)
 
+    def arrive(self, s):
+        p = self.place
+        block = self.slot(1 - p.dp, p.behind(s))
+        return remote(block, block, self.ys.at[s], self.yr.at[s], p.other)
+
+    def when_crossing(self, s, act):
+        if self.swap and s in (1, 3):
+            pl.when(lax.rem(self.place.ctx, 2) == (0 if s == 1 else 1))(act)
+        else:
+            act()
+
+    def swapped(self, ctx):
+        p = self.place
+        block = self.slot(1 - p.dp, ctx)
+        neighbour = p.ctx + 1 - 2 * lax.rem(p.ctx, 2)
+        return remote(block, block, self.ss.at[0], self.sr.at[0], p.along(neighbour))
+
+    def cross(self):
+        self.crossed = True
+        self.shard.need()
+        self.across(0).start()
+
     def start(self):
         self.shard.need()
         for s in self.order:
             self.direct(s, lambda copy: copy.start())
-        self.across(0).start()
+        if not self.crossed:
+            self.cross()
         self.local().start()
 
     def step(self, k):
@@ -951,7 +984,10 @@
         remote(block, block, self.zs.at[s], self.zr.at[s], p.along(p.ctx)).wait_recv()
         if self.relayed and s == 2:
             self.relay(lambda copy: copy.start())
-        self.across(s).start()
+        self.when_crossing(s, lambda: self.across(s).start())
+        if self.swap and k == 0:
+            self.arrive(0).wait_recv()
+            self.swapped(p.ctx).start()
 
     def finish(self):
         p = self.place
@@ -960,10 +996,19 @@
             self.direct(s, lambda copy: copy.wait_send())
         if self.relayed:
             self.relay(lambda copy: copy.wait_send())
-        for s in range(self.parts):
+
+        def both(s):
             self.across(s).wait_send()
-            block = self.slot(1 - p.dp, p.behind(s))
-            remote(block, block, self.ys.at[s], self.yr.at[s], p.other).wait_recv()
+            self.arrive(s).wait_recv()
+
+        for s in self.order:
+            self.when_crossing(s, functools.partial(both, s))
+        self.across(0).wait_send()
+        if self.swap:
+            self.swapped(p.ctx).wait_send()
+            self.swapped(p.ctx + 1 - 2 * lax.rem(p.ctx, 2)).wait_recv()
+        else:
+            self.arrive(0).wait_recv()
 
     @property
     def result(self):
@@ -972,7 +1017,7 @@
 
 
 class Scatter:
-    def __init__(self, call, blocks):
+    def __init__(self, call, blocks, swap=False):
         self.parts = lax.axis_size(CTX)
         places, rows, width = blocks.shape
         self.dtype = blocks.dtype
@@ -985,24 +1030,46 @@
         self.yb = call.hold((self.parts, rows, width), blocks.dtype)
         self.zb = call.hold((self.parts - 1, rows, width), blocks.dtype)
         self.zs, self.zr, self.ys, self.yr = (call.flags(self.parts) for _ in range(4))
-        self.l = call.flags(1)
+        self.l, self.ss, self.sr = (call.flags(2) for _ in range(3))
         self.relayed = self.parts == 4
+        self.swap = swap and self.relayed
         self.order = (3, 1, 2, 0) if self.relayed else tuple(range(self.parts - 1, -1, -1))
         if self.relayed:
             self.rb = call.hold((rows, width), blocks.dtype)
+        if self.swap:
+            self.tb, self.wb = (call.hold((rows, width), blocks.dtype) for _ in range(2))
         self.steps = self.parts
 
     def bind(self, place):
         self.place = place
+
+    def block_of(self, dp, ctx):
+        return self.blocks.at[dp * self.parts + ctx]
 
     def local(self):
         mine = self.blocks.at[pl.ds(self.place.dp * self.parts, self.parts)]
         return pltpu.make_async_copy(mine, self.mb.ref, self.l.at[0])
 
+    def local_twin(self):
+        p = self.place
+        return pltpu.make_async_copy(self.block_of(1 - p.dp, p.ctx), self.tb.ref, self.l.at[1])
+
+    def swapped(self):
+        p = self.place
+        neighbour = p.ctx + 1 - 2 * lax.rem(p.ctx, 2)
+        block = self.block_of(1 - p.dp, neighbour)
+        return remote(block, self.wb.ref, self.ss.at[0], self.sr.at[0], p.along(neighbour))
+
     def across(self, s):
         p = self.place
-        block = self.blocks.at[(1 - p.dp) * self.parts + p.ahead(s)]
+        block = self.tb.ref if self.swap and s == 0 else self.block_of(1 - p.dp, p.ahead(s))
         return remote(block, self.yb.at[s], self.ys.at[s], self.yr.at[s], p.other)
+
+    def when_crossing(self, s, act):
+        if self.swap and s in (1, 3):
+            pl.when(lax.rem(self.place.ctx, 2) == (1 if s == 1 else 0))(act)
+        else:
+            act()
 
     def along(self, s, act):
         p = self.place
@@ -1016,28 +1083,59 @@
         pl.when(p.ctx != end)(lambda: act(copy))
         pl.when(p.ctx == end)(lambda: act(way))
 
+    def early(self, act):
+        p = self.place
+        for s, odd in ((1, 0), (3, 1)):
+            block, target = self.block_of(p.dp, p.ahead(s)), self.zb.at[s - 1]
+            copy = remote(block, target, self.zs.at[s], self.zr.at[s], p.along(p.ahead(s)))
+            pl.when(lax.rem(p.ctx, 2) == odd)(lambda copy=copy: act(copy))
+
     def start(self):
+        if self.swap:
+            self.swapped().start()
+            self.local_twin().start()
+            self.early(lambda copy: copy.start())
         for s in self.order:
-            self.across(s).start()
+            if s or not self.swap:
+                self.when_crossing(s, lambda s=s: self.across(s).start())
         if not self.late:
             self.local().start()
+
+    def send_twin(self):
+        self.local_twin().wait()
+        self.swapped().wait()
+        both = self.tb[...].astype(jnp.float32) + self.wb[...].astype(jnp.float32)
+        self.tb[...] = both.astype(self.dtype)
+        self.across(0).start()
 
     def step(self, k):
         p = self.place
         s = self.order[k]
-        if k == 0 and not self.late:
-            self.local().wait()
-        self.across(s).wait()
+        if k == 0:
+            if not self.late:
+                self.local().wait()
+            if self.swap:
+                self.send_twin()
         if self.late:
             mine = self.blocks[p.dp * self.parts + p.ahead(s)]
         else:
             mine = self.mb[p.ahead(s)]
-        both = mine.astype(jnp.float32) + self.yb[s].astype(jnp.float32)
+        mine = mine.astype(jnp.float32)
+
+        def add_crossed():
+            self.across(s).wait()
+            self.yb[s] = (mine + self.yb[s].astype(jnp.float32)).astype(self.dtype)
+            if s != 2:
+                self.along(s, lambda copy: copy.start())
+
         if s == 0:
-            self.out[...] = both
+            self.across(s).wait()
+            self.out[...] = mine + self.yb[s].astype(jnp.float32)
             return
-        self.yb[s] = both.astype(self.dtype)
-        if self.relayed and s == 2:
+        self.when_crossing(s, add_crossed)
+        if s != 2:
+            return
+        if self.relayed:
 
             def add_ends():
                 way = remote(self.rb.ref, self.rb.ref, self.zs.at[0], self.zr.at[0], p.other)
@@ -1127,9 +1225,9 @@
             self.piece(s, self.own, self.zf, p.along(p.ctx)).wait_recv()
             self.piece(s, self.own, self.af, p.pair).start()
             return
-        s = self.parts - 1 - k // 2
+        s = self.parts - 1 - k % (self.parts - 1)
         far = lax.rem(p.mp + 2, 4)
-        if k % 2 == 0:
+        if k < self.parts - 1:
             self.piece(s, p.mp, self.zf, p.along(p.ctx)).wait_recv()
             self.piece(s, p.mp, self.xf, p.cross).start()
             self.piece(s, p.mp, self.af, p.pair).start()
@@ -1167,31 +1265,33 @@
 
 
 class Jobs:
-    def __init__(self, jobs, span=40.0, order=None):
+    def __init__(self, jobs, plan):
         self.jobs = list(jobs)
-        self.queue = [(job, k) for job in self.jobs for k in range(job.steps)]
-        if order is not None:
-            left = [list(range(job.steps)) for job in self.jobs]
-            self.queue = [(self.jobs[j], left[j].pop(0)) for j in order]
-        self.span, self.at = span, 0
-
-    def start(self, place):
+        self.queue = sorted(
+            (times[k] if len(times) > 2 else times[0] + k * times[1], j, k)
+            for j, (job, times) in enumerate(zip(self.jobs, plan))
+            for k in range(job.steps)
+        )
+        self.at = 0
+
+    def bind(self, place):
         self.at = 0
         for job in self.jobs:
             job.bind(place)
+
+    def start(self):
         for job in self.jobs:
             if not getattr(job, LATE, False):
                 job.start()
 
     def advance(self, reached):
-        stop = min(len(self.queue), int(len(self.queue) * reached / self.span))
-        while self.at < stop:
-            job, k = self.queue[self.at]
-            job.step(k)
+        while self.at < len(self.queue) and self.queue[self.at][0] <= reached:
+            _, j, k = self.queue[self.at]
+            self.jobs[j].step(k)
             self.at += 1
 
     def finish(self):
-        self.advance(self.span)
+        self.advance(math.inf)
         for job in self.jobs:
             job.finish()
 
@@ -1200,10 +1300,11 @@
     place = Place()
     if total is not None:
         total.bind(place)
+    jobs.bind(place)
     place.greet(call.far)
     call.start_loads(backward)
     place.enter(call.far)
-    jobs.start(place)
+    jobs.start()
 
 
 def dot_nn(a, b):
@@ -1272,7 +1373,9 @@
         self.gather = Gather(call, self.wa_one, places)
         self.deal = Deal(call, inputs)
         self.gather_gains = Gather(call, self.gains_wide, places)
-        self.jobs = Jobs([self.gather_gains, self.deal, self.gather])
+        plan = ((2.0, 0.1), (5.0, 4.0), (14.0, 6.0))
+        self.jobs = Jobs([self.gather_gains, self.deal, self.gather], plan)
+        self.deal.late = True
         self.x = call.hold((count, width), low)
         self.wa = call.hold((width, 4 * hid), low)
         self.gain_blocks = call.hold((places,) + gain_rows.shape, jnp.float32)
@@ -1286,16 +1389,19 @@
         call, hid = self.call, self.hid
         place = Place()
         total.bind(place)
+        self.jobs.bind(place)
+        jobs.bind(place)
         place.greet(call.far)
         call.start_loads()
+        place.enter(call.far)
+        self.deal.start()
         for j, held in enumerate(self.first):
             held.need()
             values = held[...]
             self.wa_one[:, j * hid : (j + 1) * hid] = values.T if j == 3 else values
         self.gain_rows.need()
         self.gains_wide[...] = self.gain_rows[...].astype(jnp.float32)
-        place.enter(call.far)
-        self.jobs.start(place)
+        self.jobs.start()
         for tall, shard in zip(self.tall, self.shards_one + self.shards_two):
             tall.need()
             shard[...] = tall[...].T
@@ -1306,6 +1412,8 @@
             values = held[...]
             self.wa_two[:, j * hid : (j + 1) * hid] = values.T if j == 3 else values
         self.wa_two.put()
+        for job in jobs.jobs:
+            job.cross()
         self.ids.need()
         self.angle.need()
         ids = self.ids[...].astype(jnp.float32)
@@ -1324,8 +1432,8 @@
             self.sine[at, :] = jnp.sin(angles) * self.angle[1:2, :]
         self.cosine.put()
         self.sine.put()
-        self.jobs.advance(self.jobs.span)
-        jobs.start(place)
+        self.jobs.advance(math.inf)
+        jobs.start()
         self.jobs.finish()
         shard = self.shard
         copies = [
@@ -1360,7 +1468,7 @@
         self.gains.put()
 
 
-def attention_layer(number, x, first_v, wa, gains, which, tables, jobs_of, opening=None, span=40.0):
+def attention_layer(number, x, first_v, wa, gains, which, tables, jobs_of, plan, opening=None):
     call = Call(number)
     if opening is None:
         start = None
@@ -1387,7 +1495,7 @@
     acc = call.hold((rows, hid), jnp.float32)
     total = HeadSum(call, BLOCKS, rows, width)
     carried = jobs_of(call, start)
-    jobs = Jobs(carried, span)
+    jobs = Jobs(carried, plan)
 
     def body():
         if start is None:
@@ -1426,7 +1534,9 @@
             seg_col.need(i)
             seg_row.need()
             write_bias(bias, seg_col, seg_row, i, rows, keys)
-            jobs.advance(5.0 * i + 3.0)
+            if i:
+                total.middle(i - 1)
+            jobs.advance((4.5, 8.0, 12.5, 18.0)[i])
 
             def one_head(index, unused):
                 mask = lane // HEAD_DIM == index
@@ -1446,13 +1556,11 @@
             o.put(i)
             lse.put(i)
             total.send(i, dot_nt(attended, wa[:, 3 * hid :]))
-            if i:
-                total.middle(i - 1)
-            jobs.advance(5.0 * i + 5.5)
+            jobs.advance((6.0, 10.5, 16.0, 22.5)[i])
         total.middle(BLOCKS - 1)
         for i in range(BLOCKS):
             total.last(i)
-            jobs.advance(23.0 + 4.0 * i)
+            jobs.advance((23.0, 24.0, 28.0, 33.0)[i])
         for i in range(BLOCKS):
             at = pl.ds(i * rows, rows)
             x1[at, :] = x[at, :].astype(jnp.float32) + total.total(i)
@@ -1474,7 +1582,7 @@
     )
 
 
-def feed_forward_layer(number, x1, gate, up, down, gains, which, jobs_of, span=30.0):
+def feed_forward_layer(number, x1, gate, up, down, gains, which, jobs_of, plan):
     count, width = x1.shape
     units = gate.shape[1]
     rows = count // BLOCKS
@@ -1486,7 +1594,7 @@
     z, u, a = (call.store((count, units), jnp.bfloat16, BLOCKS) for _ in range(3))
     total = HeadSum(call, BLOCKS, rows, width)
     carried = jobs_of(call)
-    jobs = Jobs(carried, span)
+    jobs = Jobs(carried, plan)
 
     def body():
         begin(call, total, jobs)
@@ -1500,6 +1608,9 @@
             h2[at, :] = normed
             gate.need()
             gated = dot_nn(normed, gate[...])
+            if i:
+                total.middle(i - 1)
+            jobs.advance(2.5 * i + 4.0)
             up.need()
             raised = dot_nn(normed, up[...])
             active = (gated * lax.logistic(gated) * raised).astype(jnp.bfloat16)
@@ -1510,13 +1621,11 @@
                 held.put(i)
             down.need()
             total.send(i, dot_nt(active, down[...]))
-            if i:
-                total.middle(i - 1)
-            jobs.advance(2.5 * i + 4.0)
+            jobs.advance(2.5 * i + 5.5)
         total.middle(BLOCKS - 1)
         for i in range(BLOCKS):
             total.last(i)
-            jobs.advance(14.0 + 5.0 * i)
+            jobs.advance(13.0 + 5.7 * i)
         for i in range(BLOCKS):
             at = pl.ds(i * rows, rows)
             result = x1[at, :] + total.total(i)
@@ -1547,15 +1656,16 @@
     return inverse * (grad_scaled - scaled * products), gain_sum
 
 
-def feed_forward_back(number, gy, x1, saved, gate, up, down, gains, which, jobs_of, span=30.0):
+def feed_forward_back(number, gy, x1, saved, gate, up, down, gains, which, jobs_of, plan):
     count, width = x1.shape
     units = gate.shape[1]
     rows = count // BLOCKS
     call = Call(number)
+    call.in_turn = True
     gy = call.load(gy, BLOCKS)
-    a, down = call.load(saved.a), call.load(down)
+    down = call.load(down)
     z, u = call.load(saved.z, BLOCKS), call.load(saved.u, BLOCKS)
-    gate, up, h2, gains = (call.load(w) for w in (gate, up, saved.h2, gains))
+    gate, up, a, h2, gains = (call.load(w) for w in (gate, up, saved.a, saved.h2, gains))
     x1 = call.load(x1, BLOCKS)
     gx1 = call.store_from(x1, (count, width), jnp.float32, BLOCKS)
     gain = call.store((1, width), jnp.float32)
@@ -1568,7 +1678,7 @@
     total = HeadSum(call, BLOCKS, rows, width)
     down_sum = Scatter(call, d_down)
     carried = jobs_of(call, down_sum)
-    jobs = Jobs(carried, span)
+    jobs = Jobs(carried, plan)
 
     def body():
         begin(call, total, jobs)
@@ -1576,12 +1686,6 @@
             at = pl.ds(i * rows, rows)
             gy.need(i)
             low[at, :] = gy[at, :].astype(jnp.bfloat16)
-        a.need()
-        for j in range(places // 2):
-            cut = slice(j * 2 * shard, (j + 1) * 2 * shard)
-            part = dot_tn(low[:, cut], a[...]).astype(jnp.bfloat16)
-            d_down[2 * j : 2 * j + 2] = part.reshape(2, shard, units)
-        down_sum.start()
         for i in range(BLOCKS):
             at = pl.ds(i * rows, rows)
             down.need()
@@ -1594,16 +1698,25 @@
             slope = sigma * (1.0 + gated * (1.0 - sigma))
             gz[at, :] = (ga * raised * slope).astype(jnp.bfloat16)
             gu[at, :] = (ga * gated * sigma).astype(jnp.bfloat16)
+            if i > 1:
+                total.middle(i - 1)
             gate.need()
             up.need()
             total.send(i, dot_nt(gz[at, :], gate[...]) + dot_nt(gu[at, :], up[...]))
-            if i:
-                total.middle(i - 1)
-            jobs.advance(2.5 * i + 6.0)
+            if i == 0:
+                a.need()
+                for j in range(places // 2):
+                    cut = slice(j * 2 * shard, (j + 1) * 2 * shard)
+                    part = dot_tn(low[:, cut], a[...]).astype(jnp.bfloat16)
+                    d_down[2 * j : 2 * j + 2] = part.reshape(2, shard, units)
+                    if j == 0:
+                        total.middle(0)
+                down_sum.start()
+            jobs.advance(3.0 * i + 9.0)
         total.middle(BLOCKS - 1)
         cols = width // 4
         h2.need()
-        for reached, left, right, out in ((17.0, h2, gz, d_gate), (20.0, h2, gu, d_up)):
+        for reached, left, right, out in ((21.0, h2, gz, d_gate), (24.0, h2, gu, d_up)):
             for j in range(4):
                 cut = slice(j * cols, (j + 1) * cols)
                 out[cut, :] = dot_tn(left[:, cut], right[...]).astype(jnp.bfloat16)
@@ -1612,7 +1725,7 @@
         gains.need()
         for i in range(BLOCKS):
             total.last(i)
-            jobs.advance(22.0 + 4.0 * i)
+            jobs.advance((24.0, 24.0, 28.0, 34.0)[i])
         gain_sum = jnp.zeros((1, width), jnp.float32)
         for i in range(BLOCKS):
             at = pl.ds(i * rows, rows)
@@ -1636,7 +1749,7 @@
     )
 
 
-def attention_back(number, gx1, x, saved, extra, wa, gains, which, tables, jobs_of, span=50.0):
+def attention_back(number, gx1, x, saved, extra, wa, gains, which, tables, jobs_of, plan):
     count, width = x.shape
     hid = wa.shape[1] // 4
     heads = hid // HEAD_DIM
@@ -1670,7 +1783,7 @@
     g3 = call.hold((count, 3 * hid), jnp.bfloat16)
     total = HeadSum(call, BLOCKS, rows, width)
     carried = jobs_of(call)
-    jobs = Jobs(carried, span)
+    jobs = Jobs(carried, plan)
 
     def body():
         begin(call, total, jobs, True)
@@ -1689,6 +1802,8 @@
                 held.need(i)
             write_bias(bias, seg_col, seg_row, i, rows, keys)
             gq[...] = jnp.zeros(gq.shape, gq.dtype)
+            if turn_index:
+                total.middle(order[turn_index - 1])
 
             def one_head(index, unused):
                 mask = lane // HEAD_DIM == index
@@ -1724,9 +1839,7 @@
             g3[at, hid : 2 * hid] = turn(gk[at, :], cos, sin, True).astype(jnp.bfloat16)
             g3[at, 2 * hid :] = values.astype(jnp.bfloat16)
             total.send(i, dot_nt(g3[at, :], wa[:, : 3 * hid]))
-            if turn_index:
-                total.middle(order[turn_index - 1])
-            jobs.advance((8.0, 14.0, 18.0, 21.0)[turn_index])
+            jobs.advance((11.0, 17.5, 22.0, 25.0)[turn_index])
         total.middle(order[-1])
         cols = width // 4
         h.need()
@@ -1735,11 +1848,11 @@
             d_wa[cut, : 3 * hid] = dot_tn(h[:, cut], g3[...]).astype(jnp.bfloat16)
             d_wa[cut, 3 * hid :] = dot_tn(low[:, cut], o[...]).astype(jnp.bfloat16)
             d_wa.put(j)
-        jobs.advance(25.0)
+        jobs.advance(30.0)
         gains.need()
         for turn_index, i in enumerate(order):
             total.last(i)
-            jobs.advance(28.0 + 4.0 * turn_index)
+            jobs.advance((30.0, 30.0, 32.0, 37.0)[turn_index])
         gain_sum = jnp.zeros((1, width), jnp.float32)
         for i in order:
             at = pl.ds(i * rows, rows)
@@ -1764,10 +1877,10 @@
     )
 
 
-def transfers(number, jobs_of, order):
+def transfers(number, jobs_of, plan):
     call = Call(number)
     carried = jobs_of(call)
-    jobs = Jobs(carried, order=order)
+    jobs = Jobs(carried, plan)
 
     def body():
         begin(call, None, jobs)
@@ -1903,8 +2016,8 @@
         0,
         None,
         lambda c, start: [Gather(c, held, places) for held in start.shards_one],
+        ((2.0, 4.1), (14.3, 4.1), (26.6, 4.1)),
         opening,
-        26.0,
     )
     start = attn_one.start
     x, wa_one, gains = start.deal.result, start.gather.result, start.gains.result
@@ -1918,8 +2031,8 @@
         *ffn_one_w,
         gains,
         1,
-        lambda c: [Gather(c, wa_two_shard, places), Gather(c, shards_two[0], places)],
-        30.0,
+        lambda c: [Gather(c, wa_two_shard, places, True), Gather(c, shards_two[0], places)],
+        ((7.0, 4.0), (20.0, 4.1)),
     )
     wa_two, gate_two_w = ffn_one.carried
     attn_two = attention_layer(
@@ -1930,8 +2043,11 @@
         gains,
         2,
         tables,
-        lambda c, start: [Gather(c, array, places) for array in shards_two[1:]],
-        span=26.0,
+        lambda c, start: [
+            Gather(c, shards_two[1], places),
+            Gather(c, shards_two[2], places, True),
+        ],
+        ((8.0, 3.0), (18.0, 3.0)),
     )
     ffn_two_w = (gate_two_w, *attn_two.carried)
     ffn_two = feed_forward_layer(
@@ -1940,10 +2056,9 @@
         *ffn_two_w,
         gains,
         3,
-        lambda c: [Deal(c, cotangent, True), Deal(c, deal(ffn_one.y_low))],
-        90.0,
-    )
-    out_one = ffn_two.carried[1]
+        lambda c: [Deal(c, cotangent, True)],
+        ((9.5, 7.3),),
+    )
     back_ffn_two = feed_forward_back(
         5,
         ffn_two.carried[0],
@@ -1953,9 +2068,11 @@
         gains,
         3,
         lambda c, down_sum: [down_sum, Deal(c, deal(ffn_two.y_low), True)],
-        36.0,
+        ((13.0, 4.2), (10.0, 7.3)),
     )
     down_g2, out_two = back_ffn_two.carried
+
+    grads_plan = ((10.0, 3.0), (25.0, 3.0))
 
     def ffn_grads(back):
         return lambda c: [Scatter(c, split(array)) for array in (back.d_gate, back.d_up)]
@@ -1971,7 +2088,9 @@
         2,
         tables,
         ffn_grads(back_ffn_two),
-    )
+        grads_plan,
+    )
+    gate_g2, up_g2 = back_attn_two.carried
     back_ffn_one = feed_forward_back(
         7,
         back_attn_two.gx,
@@ -1980,10 +2099,14 @@
         *ffn_one_w,
         gains,
         1,
-        lambda c, down_sum: [Scatter(c, split(back_attn_two.d_wa)), down_sum],
-        40.0,
-    )
-    packed_two, down_g1 = back_ffn_one.carried
+        lambda c, down_sum: [
+            Scatter(c, split(back_attn_two.d_wa)),
+            down_sum,
+            Deal(c, deal(ffn_one.y_low)),
+        ],
+        ((8.0, 5.8), (30.0, 4.2), (33.0, 33.1, 33.2, 37.0, 37.1, 37.2)),
+    )
+    packed_two, down_g1, out_one = back_ffn_one.carried
     back_attn_one = attention_back(
         8,
         back_ffn_one.gx1,
@@ -1995,6 +2118,7 @@
         0,
         tables,
         ffn_grads(back_ffn_one),
+        grads_plan,
     )
     gain_grads = jnp.concatenate(
         [back_attn_one.gain, back_ffn_one.gain, back_attn_two.gain, back_ffn_two.gain] * 2
@@ -2007,13 +2131,13 @@
             Scatter(c, split(back_attn_one.d_wa)),
             Deal(c, deal(back_attn_one.gx)),
         ],
-        (1, 0, 2, 0, 1, 0, 2, 2, 0, 1, 2, 2, 2, 1),
+        ((4.0, 0.1), (7.0, 5.8), (6.0, 4.0)),
     )
     final = leave_step(
         (out_one, out_two),
         grad,
         (packed_one, packed_two),
-        back_attn_one.carried + [down_g1] + back_attn_two.carried + [down_g2],
+        back_attn_one.carried + [down_g1, gate_g2, up_g2, down_g2],
         gain_shards,
     )
     gate_g1, up_g1, down_g1, gate_g2, up_g2, down_g2 = final.turned

time: 510 us -> 478 us (0.937)
  Pallas kernels: 499 us -> 468 us
    pallas_call x10, Pallas kernels: 499 us -> 468 us  [run(): pl.pallas_call(kernel, out_shape=tuple(self.shapes), in_specs=[space] * i...]
where the time goes in v4:
time: 478 us; the launch traced here: 472 us
  Pallas kernels  468 us (98%)
    pallas_call x10, Pallas kernels, run(): pl.pallas_call(kernel, out_shape=tuple(self.shapes), in_specs=[space] * i...  468 us

profile of v4, /device:TPU:0, one launch (start us, length us, event | category | flops | bytes accessed | tf_op | source)
XLA Modules:
  0.0 472.3 jit_solution(9378582284626409122)
XLA Ops:
  0.7 1.4 stack.23.refs_4_
  2.0 97.5 %shard_map.373 = (bf16[128,704]{1,0:T(8,128)(2,1)}, bf16[128,704]{1,0:T(8,128)(2,1)}, bf16[128,704]{1,0:T(8,128)(2,1)}, bf16[128,1024]{1,0:T(8,128)(2,1)}, f32[1...) custom-call(bf16[128,256]{1,0:T(8,128)(2,1)} %refs_0_.1, ...), custom_call_target="tpu_custom_call" | custom-call | tf_op jit(solution)/shard_map/pallas_call | solution.py:781
  99.5 47.5 %shard_map.374 = (f32[1024,1024]{1,0:T(8,128)}, bf16[1024,1024]{1,0:T(8,128)(2,1)}, bf16[1024,1024]{1,0:T(8,128)(2,1)}, bf16[1024,704]{1,0:T(8,128)(2,1)}, bf16[...) custom-call(f32[1024,1024]{1,0:T(8,128)} %get-tuple-element.114.refs, ...), custom_call_target="tpu_custom_call" | custom-call | tf_op jit(solution)/shard_map/pallas_call | solution.py:781
  147.0 49.6 %shard_map.375 = (f32[1024,1024]{1,0:T(8,128)}, bf16[1024,1024]{1,0:T(8,128)(2,1)}, bf16[1024,256]{1,0:T(8,128)(2,1)}, bf16[1024,256]{1,0:T(8,128)(2,1)}, bf16[1...) custom-call(f32[1024,1024]{1,0:T(8,128)} %get-tuple-element.121.refs, ...), custom_call_target="tpu_custom_call" | custom-call | tf_op jit(solution)/shard_map/pallas_call | solution.py:781
  196.6 33.9 %shard_map.376 = (f32[1024,1024]{1,0:T(8,128)}, bf16[1024,1024]{1,0:T(8,128)(2,1)}, bf16[1024,1024]{1,0:T(8,128)(2,1)}, bf16[1024,704]{1,0:T(8,128)(2,1)}, bf16[...) custom-call(f32[1024,1024]{1,0:T(8,128)} %get-tuple-element.130.refs_0_.refs_9_, ...), custom_call_target="tpu_custom_call" | custom-call | tf_op jit(solution)/shard_map/pallas_call | solution.py:781
  230.4 40.7 %shard_map.377 = (f32[1024,1024]{1,0:T(8,128)}, f32[1,1024]{1,0:T(1,128)}, bf16[1024,704]{1,0:T(8,128)(2,1)}, bf16[1024,704]{1,0:T(8,128)(2,1)}, f32[128,704]{1,0:T(8,128)}, /*index=5*/bf16[4,256,1024]{2,1,0:T(8,128)(2,1)}) custom-call(bf16[1024,1024]{1,0:T(8,128)(2,1)} %bitcast.63, bf16[1024,704]{1,0:T(8,128)(2,1)} %bitcast.57, ...), custom_call_target="tpu_custom_call" | custom-call | tf_op jit(solution)/shard_map/pallas_call | solution.py:781
  271.1 51.3 %shard_map.378 = (f32[1024,1024]{1,0:T(8,128)}, f32[1024,256]{1,0:T(8,128)}, f32[1,1024]{1,0:T(1,128)}, bf16[1024,1024]{1,0:T(8,128)(2,1)}, f32[128,704]{1,0:T(8,128)}, /*index=5*/f32[128,704]{1,0:T(8,128)}) custom-call(f32[1024,1024]{1,0:T(8,128)} %get-tuple-element.140.refs_0_, bf16[1024,1024]{1,0:T(8,128)(2,1)} %bitcast.45, ...), custom_call_target="tpu_custom_call" | custom-call | tf_op jit(solution)/shard_map/pallas_call | solution.py:781
  322.4 56.0 %shard_map.379 = (f32[1024,1024]{1,0:T(8,128)}, f32[1,1024]{1,0:T(1,128)}, bf16[1024,704]{1,0:T(8,128)(2,1)}, bf16[1024,704]{1,0:T(8,128)(2,1)}, f32[128,704]{1,...) custom-call(f32[1024,1024]{1,0:T(8,128)} %get-tuple-element.149.refs_0_, bf16[1024,704]{1,0:T(8,128)(2,1)} %bitcast.51, ...), custom_call_target="tpu_custom_call" | custom-call | tf_op jit(solution)/shard_map/pallas_call | solution.py:781
  378.3 0.0 copy-start
  378.3 0.0 copy-start.1
  378.3 0.0 copy-start.2
  378.4 47.5 %shard_map.380 = (bf16[1024,1024]{1,0:T(8,128)(2,1)}, f32[1,1024]{1,0:T(1,128)}, bf16[1024,1024]{1,0:T(8,128)(2,1)}, f32[128,704]{1,0:T(8,128)}, f32[128,704]{1,0:T(8,128)}) custom-call(f32[1024,1024]{1,0:T(8,128)} %get-tuple-element.158.refs_0_, bf16[1024,1024]{1,0:T(8,128)(2,1)} %bitcast.58, bf16[1024,256]{1,0:T(8,128)(2,1)} %get-tuple-element.160.refs_2_, ...), custom_call_target="tpu_custom_call" | custom-call | tf_op jit(solution)/shard_map/pallas_call | solution.py:781
  425.9 0.0 copy-done
  425.9 0.0 copy-done.1
  425.9 0.0 copy-done.2
  425.9 1.4 concatenate.3
  427.3 37.1 %shard_map.381 = (f32[8,128]{1,0:T(8,128)}, f32[128,1024]{1,0:T(8,128)}, bf16[4,256,1024]{2,1,0:T(8,128)(2,1)}) custom-call(f32[8,8,128]{2,1,0:T(8,128)} %bitcast.77, bf16[8,128,1024]{2,1,0:T(8,128)(2,1)} %bitcast.65, bf16[4,256,1024]{2,1,0:T(8,128)(2,1)} %bitcast.64), custom_call_target="tpu_custom_call" | custom-call | tf_op jit(solution)/shard_map/pallas_call | solution.py:781
  464.4 7.6 %shard_map.382 = (bf16[1024,1024]{1,0:T(8,128)(2,1)}, bf16[1024,1024]{1,0:T(8,128)(2,1)}, f32[1024,1024]{1,0:T(8,128)}, f32[128,256]{1,0:T(8,128)}, f32[128,256]...) custom-call(bf16[1024,1024]{1,0:T(8,128)(2,1)} %bitcast.67, ...), custom_call_target="tpu_custom_call" | custom-call | tf_op jit(solution)/shard_map/pallas_call | solution.py:781
Async XLA Ops:
  378.3 47.6 %copy-start = (f32[1,1024]{1,0:T(1,128)S(1)}, f32[1,1024]{1,0:T(1,128)}, u32[]{:S(2)}) copy-start(f32[1,1024]{1,0:T(1,128)} %get-tuple-element.173) | copy-start | bytes 12292
  378.3 47.6 %copy-start.1 = (f32[1,1024]{1,0:T(1,128)S(1)}, f32[1,1024]{1,0:T(1,128)}, u32[]{:S(2)}) copy-start(f32[1,1024]{1,0:T(1,128)} %get-tuple-element.172) | copy-start | bytes 12292
  378.3 47.6 %copy-start.2 = (f32[1,1024]{1,0:T(1,128)S(1)}, f32[1,1024]{1,0:T(1,128)}, u32[]{:S(2)}) copy-start(f32[1,1024]{1,0:T(1,128)} %get-tuple-element.171) | copy-start | bytes 12292

commit v5 on v4

--- a/solution.py
+++ b/solution.py
@@ -896,6 +896,28 @@
         return self.part[i].astype(jnp.float32)
 
 
+class QuarterSum(HeadSum):
+    def __init__(self, call, blocks, rows, width):
+        self.half, self.quarter = rows // 2, rows // 4
+        self.part = call.hold((blocks, rows, width), jnp.bfloat16)
+        self.near = call.hold((blocks, rows // 2, width), jnp.bfloat16)
+        self.far = call.hold((blocks, rows // 4, width), jnp.bfloat16)
+        self.out = call.store((blocks, rows // 4, width), jnp.bfloat16)
+        self.sa, self.ra, self.sb, self.rb = (call.flags(blocks) for _ in range(4))
+
+    def rows_of(self, index):
+        return pl.ds(pl.multiple_of(index * self.quarter, self.quarter), self.quarter)
+
+    def second(self, i):
+        source = self.near.at[i, self.rows_of(1 - self.place.mp // 2)]
+        return remote(source, self.far.at[i], self.sb.at[i], self.rb.at[i], self.place.cross)
+
+    def last(self, i):
+        self.second(i).wait()
+        mine = self.near[i, self.rows_of(self.place.mp // 2)].astype(jnp.float32)
+        self.out[i] = (mine + self.far[i].astype(jnp.float32)).astype(jnp.bfloat16)
+
+
 class Gather:
     def __init__(self, call, shard, places, swap=False):
         self.parts = lax.axis_size(CTX)
@@ -1170,49 +1192,60 @@
 
 
 class Deal:
-    def __init__(self, call, blocks, wide=False):
-        self.parts, self.wide = lax.axis_size(CTX), wide
-        self.share = blocks.shape[1] // (2 if wide else 4)
+    def __init__(self, call, blocks, rows=None):
+        self.parts, self.compact = lax.axis_size(CTX), rows is not None
+        length, width = rows or blocks.shape[1], blocks.shape[2]
+        self.share = length // 4
         call.far = True
         self.source = call.take(blocks)
-        self.target = call.give(blocks.shape, blocks.dtype)
+        self.target = call.give((self.parts, length, width), blocks.dtype)
         self.held = call.hold(blocks.shape[1:], blocks.dtype)
         self.l = call.flags(2)
         self.zf, self.af, self.xf, self.bf = (
             tuple(call.flags(self.parts) for _ in range(2)) for _ in range(4)
         )
-        self.steps = (self.parts - 1) * (1 if wide else 2)
+        self.order = list(range(self.parts - 1, 0, -1))
+        if self.compact:
+            self.order.insert(0, 0)
+        self.steps = 2 * len(self.order)
 
     def bind(self, place):
         self.place = place
-        self.own = place.side if self.wide else place.mp
+        if self.compact:
+            x, side = place.mp // 2, place.side
+            self.own, self.far = side * 2 + x, side * 2 + 1 - x
+            self.near, self.near_far = (1 - side) * 2 + x, (1 - side) * 2 + 1 - x
+        else:
+            self.own, self.far = place.mp, lax.rem(place.mp + 2, 4)
+            self.near = place.mp + 1 - 2 * place.side
+            self.near_far = lax.rem(self.near + 2, 4)
 
     def rows(self, index):
         return pl.ds(pl.multiple_of(index * self.share, self.share), self.share)
 
     def local(self, k):
         p = self.place
-        refs = (self.source.at[p.ctx], self.held.ref, self.target.at[p.ctx])
+        target = self.target.at[p.ctx]
+        if self.compact:
+            target = self.target.at[p.ctx, self.rows(self.own)]
+        refs = (self.source.at[p.ctx], self.held.ref, target)
         return pltpu.make_async_copy(refs[k], refs[k + 1], self.l.at[k])
 
     def along(self, s):
         p = self.place
         rows = self.rows(self.own)
-        return remote(
-            self.source.at[p.ahead(s), rows],
-            self.target.at[p.ctx, rows],
-            self.zf[0].at[s],
-            self.zf[1].at[s],
-            p.along(p.ahead(s)),
-        )
+        source = self.source.at[p.ahead(s)] if self.compact else self.source.at[p.ahead(s), rows]
+        target = self.target.at[p.ctx, rows]
+        return remote(source, target, self.zf[0].at[s], self.zf[1].at[s], p.along(p.ahead(s)))
 
     def piece(self, s, index, flags, peer):
         ref = self.target.at[self.place.behind(s), self.rows(index)]
         return remote(ref, ref, flags[0].at[s], flags[1].at[s], peer)
 
     def start(self):
-        for s in range(self.parts - 1, 0, -1):
-            self.along(s).start()
+        for s in self.order:
+            if s:
+                self.along(s).start()
         self.local(0).start()
 
     def step(self, k):
@@ -1220,40 +1253,30 @@
         if k == 0:
             self.local(0).wait()
             self.local(1).start()
-        if self.wide:
-            s = self.parts - 1 - k
-            self.piece(s, self.own, self.zf, p.along(p.ctx)).wait_recv()
+        s = self.order[k % len(self.order)]
+        if k < len(self.order):
+            if s:
+                self.piece(s, self.own, self.zf, p.along(p.ctx)).wait_recv()
+            else:
+                self.local(1).wait()
+            self.piece(s, self.own, self.xf, p.cross).start()
             self.piece(s, self.own, self.af, p.pair).start()
-            return
-        s = self.parts - 1 - k % (self.parts - 1)
-        far = lax.rem(p.mp + 2, 4)
-        if k < self.parts - 1:
-            self.piece(s, p.mp, self.zf, p.along(p.ctx)).wait_recv()
-            self.piece(s, p.mp, self.xf, p.cross).start()
-            self.piece(s, p.mp, self.af, p.pair).start()
         else:
-            self.piece(s, far, self.xf, p.cross).wait_recv()
-            self.piece(s, far, self.bf, p.pair).start()
+            self.piece(s, self.far, self.xf, p.cross).wait_recv()
+            self.piece(s, self.far, self.bf, p.pair).start()
 
     def finish(self):
         p = self.place
-        self.local(1).wait()
-        if self.wide:
-            for s in range(1, self.parts):
+        if not self.compact:
+            self.local(1).wait()
+        for s in self.order:
+            if s:
                 self.along(s).wait_send()
-                self.piece(s, self.own, self.af, p.pair).wait_send()
-                self.piece(s, 1 - self.own, self.af, p.pair).wait_recv()
-            return
-        far = lax.rem(p.mp + 2, 4)
-        near = p.mp + 1 - 2 * p.side
-        near_far = lax.rem(near + 2, 4)
-        for s in range(1, self.parts):
-            self.along(s).wait_send()
-            self.piece(s, p.mp, self.xf, p.cross).wait_send()
-            self.piece(s, p.mp, self.af, p.pair).wait_send()
-            self.piece(s, far, self.bf, p.pair).wait_send()
-            self.piece(s, near, self.af, p.pair).wait_recv()
-            self.piece(s, near_far, self.bf, p.pair).wait_recv()
+            self.piece(s, self.own, self.xf, p.cross).wait_send()
+            self.piece(s, self.own, self.af, p.pair).wait_send()
+            self.piece(s, self.far, self.bf, p.pair).wait_send()
+            self.piece(s, self.near, self.af, p.pair).wait_recv()
+            self.piece(s, self.near_far, self.bf, p.pair).wait_recv()
 
     @property
     def result(self):
@@ -1305,6 +1328,7 @@
     call.start_loads(backward)
     place.enter(call.far)
     jobs.start()
+    return place
 
 
 def dot_nn(a, b):
@@ -1435,6 +1459,7 @@
         self.jobs.advance(math.inf)
         jobs.start()
         self.jobs.finish()
+        jobs.advance(0.5)
         shard = self.shard
         copies = [
             pltpu.make_async_copy(
@@ -1662,11 +1687,21 @@
     rows = count // BLOCKS
     call = Call(number)
     call.in_turn = True
-    gy = call.load(gy, BLOCKS)
-    down = call.load(down)
-    z, u = call.load(saved.z, BLOCKS), call.load(saved.u, BLOCKS)
-    gate, up, a, h2, gains = (call.load(w) for w in (gate, up, saved.a, saved.h2, gains))
-    x1 = call.load(x1, BLOCKS)
+    if saved is not None:
+        gy = call.load(gy, BLOCKS)
+        down = call.load(down)
+        z, u = call.load(saved.z, BLOCKS), call.load(saved.u, BLOCKS)
+        gate, up, a, h2, gains = (call.load(w) for w in (gate, up, saved.a, saved.h2, gains))
+        x1 = call.load(x1, BLOCKS)
+        later = 0.0
+    else:
+        x1, gains = call.load(x1, BLOCKS), call.load(gains)
+        gate, up, down = (call.load(w) for w in (gate, up, down))
+        gy = call.load(gy, BLOCKS)
+        h2 = call.hold((count, width), jnp.bfloat16)
+        z, u, a = (call.hold((count, units), jnp.bfloat16) for _ in range(3))
+        quarters = QuarterSum(call, BLOCKS, rows, width)
+        later = 10.0
     gx1 = call.store_from(x1, (count, width), jnp.float32, BLOCKS)
     gain = call.store((1, width), jnp.float32)
     d_gate, d_up = (call.store((width, units), jnp.bfloat16, 4) for _ in range(2))
@@ -1680,8 +1715,35 @@
     carried = jobs_of(call, down_sum)
     jobs = Jobs(carried, plan)
 
+    def forward():
+        for i in range(BLOCKS):
+            at = pl.ds(i * rows, rows)
+            x1.need(i)
+            gains.need()
+            stream = x1[at, :]
+            inverse = lax.rsqrt(jnp.mean(stream * stream, axis=-1, keepdims=True) + epsilon)
+            normed = (stream * inverse * gains[which : which + 1, :]).astype(jnp.bfloat16)
+            h2[at, :] = normed
+            gate.need()
+            gated = dot_nn(normed, gate[...])
+            up.need()
+            raised = dot_nn(normed, up[...])
+            active = (gated * lax.logistic(gated) * raised).astype(jnp.bfloat16)
+            z[at, :] = gated.astype(jnp.bfloat16)
+            u[at, :] = raised.astype(jnp.bfloat16)
+            a[at, :] = active
+            down.need()
+            if i:
+                quarters.middle(i - 1)
+            quarters.send(i, dot_nt(active, down[...]) + stream * 0.25)
+        quarters.middle(BLOCKS - 1)
+
     def body():
-        begin(call, total, jobs)
+        if saved is None:
+            quarters.bind(begin(call, total, jobs))
+            forward()
+        else:
+            begin(call, total, jobs)
         for i in range(BLOCKS):
             at = pl.ds(i * rows, rows)
             gy.need(i)
@@ -1712,7 +1774,7 @@
                     if j == 0:
                         total.middle(0)
                 down_sum.start()
-            jobs.advance(3.0 * i + 9.0)
+            jobs.advance(3.0 * i + 9.0 + later)
         total.middle(BLOCKS - 1)
         cols = width // 4
         h2.need()
@@ -1721,11 +1783,15 @@
                 cut = slice(j * cols, (j + 1) * cols)
                 out[cut, :] = dot_tn(left[:, cut], right[...]).astype(jnp.bfloat16)
                 out.put(j)
-            jobs.advance(reached)
+            jobs.advance(reached + later)
         gains.need()
+        if saved is None:
+            for i in range(BLOCKS):
+                quarters.last(i)
+            quarters.out.put()
         for i in range(BLOCKS):
             total.last(i)
-            jobs.advance((24.0, 24.0, 28.0, 34.0)[i])
+            jobs.advance((24.0, 24.0, 28.0, 34.0)[i] + later)
         gain_sum = jnp.zeros((1, width), jnp.float32)
         for i in range(BLOCKS):
             at = pl.ds(i * rows, rows)
@@ -1745,6 +1811,7 @@
         gain=gain.result,
         d_gate=d_gate.result,
         d_up=d_up.result,
+        quarters=quarters.out.result if saved is None else None,
         carried=[job.result for job in carried],
     )
 
@@ -1804,6 +1871,8 @@
             gq[...] = jnp.zeros(gq.shape, gq.dtype)
             if turn_index:
                 total.middle(order[turn_index - 1])
+            else:
+                jobs.advance(5.0)
 
             def one_head(index, unused):
                 mask = lane // HEAD_DIM == index
@@ -2016,7 +2085,7 @@
         0,
         None,
         lambda c, start: [Gather(c, held, places) for held in start.shards_one],
-        ((2.0, 4.1), (14.3, 4.1), (26.6, 4.1)),
+        ((0.1, 0.2, 2.0), (5.0, 8.0, 12.0), (15.0, 18.0, 22.0)),
         opening,
     )
     start = attn_one.start
@@ -2044,38 +2113,30 @@
         2,
         tables,
         lambda c, start: [
+            Deal(c, cotangent),
             Gather(c, shards_two[1], places),
             Gather(c, shards_two[2], places, True),
         ],
-        ((8.0, 3.0), (18.0, 3.0)),
-    )
-    ffn_two_w = (gate_two_w, *attn_two.carried)
-    ffn_two = feed_forward_layer(
+        ((8.0, 12.5, 16.0, 22.5, 22.6, 22.7), (16.0, 3.0), (26.0, 3.0)),
+    )
+    dealt_cotangent = attn_two.carried[0]
+    ffn_two_w = (gate_two_w, *attn_two.carried[1:])
+    back_ffn_two = feed_forward_back(
         4,
+        dealt_cotangent,
         attn_two.x1,
+        None,
         *ffn_two_w,
         gains,
         3,
-        lambda c: [Deal(c, cotangent, True)],
-        ((9.5, 7.3),),
-    )
-    back_ffn_two = feed_forward_back(
-        5,
-        ffn_two.carried[0],
-        attn_two.x1,
-        ffn_two,
-        *ffn_two_w,
-        gains,
-        3,
-        lambda c, down_sum: [down_sum, Deal(c, deal(ffn_two.y_low), True)],
-        ((13.0, 4.2), (10.0, 7.3)),
-    )
-    down_g2, out_two = back_ffn_two.carried
-
+        lambda c, down_sum: [down_sum],
+        ((23.0, 4.2),),
+    )
+    (down_g2,) = back_ffn_two.carried
     grads_plan = ((10.0, 3.0), (25.0, 3.0))
 
     def ffn_grads(back):
-        return lambda c: [Scatter(c, split(array)) for array in (back.d_gate, back.d_up)]
+        return [split(array) for array in (back.d_gate, back.d_up)]
 
     back_attn_two = attention_back(
         6,
@@ -2087,10 +2148,11 @@
         gains,
         2,
         tables,
-        ffn_grads(back_ffn_two),
-        grads_plan,
-    )
-    gate_g2, up_g2 = back_attn_two.carried
+        lambda c: [Scatter(c, array) for array in ffn_grads(back_ffn_two)]
+        + [Deal(c, back_ffn_two.quarters, length)],
+        grads_plan + ((4.9, 5.0, 11.0, 11.1, 11.2, 35.0, 35.1, 35.2),),
+    )
+    gate_g2, up_g2, out_two = back_attn_two.carried
     back_ffn_one = feed_forward_back(
         7,
         back_attn_two.gx,
@@ -2117,9 +2179,10 @@
         gains,
         0,
         tables,
-        ffn_grads(back_ffn_one),
+        lambda c: [Scatter(c, array) for array in ffn_grads(back_ffn_one)],
         grads_plan,
     )
+    gate_g1, up_g1 = back_attn_one.carried
     gain_grads = jnp.concatenate(
         [back_attn_one.gain, back_ffn_one.gain, back_attn_two.gain, back_ffn_two.gain] * 2
     )
@@ -2137,7 +2200,7 @@
         (out_one, out_two),
         grad,
         (packed_one, packed_two),
-        back_attn_one.carried + [down_g1, gate_g2, up_g2, down_g2],
+        [gate_g1, up_g1, down_g1, gate_g2, up_g2, down_g2],
         gain_shards,
     )
     gate_g1, up_g1, down_g1, gate_g2, up_g2, down_g2 = final.turned

time: 478 us -> 461 us (0.964)
  Pallas kernels: 468 us -> 450 us
    pallas_call x10 -> x9, Pallas kernels: 468 us -> 450 us  [run(): pl.pallas_call(kernel, out_shape=tuple(self.shapes), in_specs=[space] * i...]
where the time goes in v5:
time: 461 us; the launch traced here: 454 us
  Pallas kernels  450 us (98%)
    pallas_call x9, Pallas kernels, run(): pl.pallas_call(kernel, out_shape=tuple(self.shapes), in_specs=[space] * i...  450 us

profile of v5, /device:TPU:0, one launch (start us, length us, event | category | flops | bytes accessed | tf_op | source)
XLA Modules:
  0.0 454.0 jit_solution(6475438771165900918)
XLA Ops:
  0.7 1.4 stack.23.refs_4_
  2.0 96.4 %shard_map.373 = (bf16[128,704]{1,0:T(8,128)(2,1)}, bf16[128,704]{1,0:T(8,128)(2,1)}, bf16[128,704]{1,0:T(8,128)(2,1)}, bf16[128,1024]{1,0:T(8,128)(2,1)}, f32[1...) custom-call(bf16[128,256]{1,0:T(8,128)(2,1)} %refs_0_.1, ...), custom_call_target="tpu_custom_call" | custom-call | tf_op jit(solution)/shard_map/pallas_call | solution.py:781
  98.4 49.8 %shard_map.374 = (f32[1024,1024]{1,0:T(8,128)}, bf16[1024,1024]{1,0:T(8,128)(2,1)}, bf16[1024,1024]{1,0:T(8,128)(2,1)}, bf16[1024,704]{1,0:T(8,128)(2,1)}, bf16[...) custom-call(f32[1024,1024]{1,0:T(8,128)} %get-tuple-element.110.refs, ...), custom_call_target="tpu_custom_call" | custom-call | tf_op jit(solution)/shard_map/pallas_call | solution.py:781
  148.3 53.8 %shard_map.375 = (f32[1024,1024]{1,0:T(8,128)}, bf16[1024,1024]{1,0:T(8,128)(2,1)}, bf16[1024,256]{1,0:T(8,128)(2,1)}, bf16[1024,256]{1,0:T(8,128)(2,1)}, bf16[1...) custom-call(f32[1024,1024]{1,0:T(8,128)} %get-tuple-element.117.refs, ...), custom_call_target="tpu_custom_call" | custom-call | tf_op jit(solution)/shard_map/pallas_call | solution.py:781
  202.0 45.9 %shard_map.376 = (bf16[4,64,1024]{2,1,0:T(8,128)(2,1)}, f32[1024,1024]{1,0:T(8,128)}, f32[1,1024]{1,0:T(1,128)}, bf16[1024,704]{1,0:T(8,128)(2,1)}, bf16[1024,704]{1,0:T(8,128)(2,1)}, /*index=5*/f32[128,704]{1,0:T(8,128)}) custom-call(f32[1024,1024]{1,0:T(8,128)} %get-tuple-element.126.refs_0_, ...), custom_call_target="tpu_custom_call" | custom-call | tf_op jit(solution)/shard_map/pallas_call | solution.py:781
  248.0 52.4 %shard_map.377 = (f32[1024,1024]{1,0:T(8,128)}, f32[1024,256]{1,0:T(8,128)}, f32[1,1024]{1,0:T(1,128)}, bf16[1024,1024]{1,0:T(8,128)(2,1)}, f32[128,704]{1,0:T(8...) custom-call(f32[1024,1024]{1,0:T(8,128)} %get-tuple-element.131.refs_0_, bf16[1024,1024]{1,0:T(8,128)(2,1)} %bitcast.44, ...), custom_call_target="tpu_custom_call" | custom-call | tf_op jit(solution)/shard_map/pallas_call | solution.py:781
  300.3 58.4 %shard_map.378 = (f32[1024,1024]{1,0:T(8,128)}, f32[1,1024]{1,0:T(1,128)}, bf16[1024,704]{1,0:T(8,128)(2,1)}, bf16[1024,704]{1,0:T(8,128)(2,1)}, f32[128,704]{1,...) custom-call(f32[1024,1024]{1,0:T(8,128)} %get-tuple-element.141.refs_0_, bf16[1024,704]{1,0:T(8,128)(2,1)} %bitcast.50, ...), custom_call_target="tpu_custom_call" | custom-call | tf_op jit(solution)/shard_map/pallas_call | solution.py:781
  358.7 0.0 copy-start
  358.7 0.0 copy-start.1
  358.7 0.0 copy-start.2
  358.7 48.8 %shard_map.379 = (bf16[1024,1024]{1,0:T(8,128)(2,1)}, f32[1,1024]{1,0:T(1,128)}, bf16[1024,1024]{1,0:T(8,128)(2,1)}, f32[128,704]{1,0:T(8,128)}, f32[128,704]{1,0:T(8,128)}) custom-call(f32[1024,1024]{1,0:T(8,128)} %get-tuple-element.150.refs_0_, bf16[1024,1024]{1,0:T(8,128)(2,1)} %bitcast.51, bf16[1024,256]{1,0:T(8,128)(2,1)} %get-tuple-element.152.refs_2_, ...), custom_call_target="tpu_custom_call" | custom-call | tf_op jit(solution)/shard_map/pallas_call | solution.py:781
  407.5 0.0 copy-done
  407.5 0.0 copy-done.1
  407.5 0.0 copy-done.2
  407.5 1.4 concatenate.3
  409.0 37.2 %shard_map.380 = (f32[8,128]{1,0:T(8,128)}, f32[128,1024]{1,0:T(8,128)}, bf16[4,256,1024]{2,1,0:T(8,128)(2,1)}) custom-call(f32[8,8,128]{2,1,0:T(8,128)} %bitcast.72, bf16[8,128,1024]{2,1,0:T(8,128)(2,1)} %bitcast.56, bf16[4,256,1024]{2,1,0:T(8,128)(2,1)} %bitcast.55), custom_call_target="tpu_custom_call" | custom-call | tf_op jit(solution)/shard_map/pallas_call | solution.py:781
  446.2 7.6 %shard_map.381 = (bf16[1024,1024]{1,0:T(8,128)(2,1)}, bf16[1024,1024]{1,0:T(8,128)(2,1)}, f32[1024,1024]{1,0:T(8,128)}, f32[128,256]{1,0:T(8,128)}, f32[128,256]...) custom-call(bf16[1024,1024]{1,0:T(8,128)(2,1)} %bitcast.58, ...), custom_call_target="tpu_custom_call" | custom-call | tf_op jit(solution)/shard_map/pallas_call | solution.py:781
Async XLA Ops:
  358.7 48.8 %copy-start = (f32[1,1024]{1,0:T(1,128)S(1)}, f32[1,1024]{1,0:T(1,128)}, u32[]{:S(2)}) copy-start(f32[1,1024]{1,0:T(1,128)} %get-tuple-element.165) | copy-start | bytes 12292
  358.7 48.8 %copy-start.1 = (f32[1,1024]{1,0:T(1,128)S(1)}, f32[1,1024]{1,0:T(1,128)}, u32[]{:S(2)}) copy-start(f32[1,1024]{1,0:T(1,128)} %get-tuple-element.164) | copy-start | bytes 12292
  358.7 48.8 %copy-start.2 = (f32[1,1024]{1,0:T(1,128)S(1)}, f32[1,1024]{1,0:T(1,128)}, u32[]{:S(2)}) copy-start(f32[1,1024]{1,0:T(1,128)} %get-tuple-element.163) | copy-start | bytes 12292

commit v6 on v5

--- a/solution.py
+++ b/solution.py
@@ -919,7 +919,7 @@
 
 
 class Gather:
-    def __init__(self, call, shard, places, swap=False):
+    def __init__(self, call, shard, places, swap=False, land=False):
         self.parts = lax.axis_size(CTX)
         call.far = True
         if isinstance(shard, Held):
@@ -927,7 +927,9 @@
         else:
             self.shard = call.load(shard)
             call.loads.insert(0, call.loads.pop())
-        self.whole = call.give((places,) + shard.shape, shard.dtype)
+        self.land = land
+        whole = (places,) + shard.shape
+        self.whole = (call.store if land else call.give)(whole, shard.dtype)
         self.zs, self.zr, self.ys, self.yr = (call.flags(self.parts) for _ in range(4))
         self.l, self.ss, self.sr = (call.flags(1) for _ in range(3))
         self.relayed = self.parts == 4
@@ -1031,6 +1033,8 @@
             self.swapped(p.ctx + 1 - 2 * lax.rem(p.ctx, 2)).wait_recv()
         else:
             self.arrive(0).wait_recv()
+        if self.land:
+            self.whole.put()
 
     @property
     def result(self):
@@ -1192,13 +1196,15 @@
 
 
 class Deal:
-    def __init__(self, call, blocks, rows=None):
+    def __init__(self, call, blocks, rows=None, land=False):
         self.parts, self.compact = lax.axis_size(CTX), rows is not None
         length, width = rows or blocks.shape[1], blocks.shape[2]
         self.share = length // 4
         call.far = True
         self.source = call.take(blocks)
-        self.target = call.give((self.parts, length, width), blocks.dtype)
+        self.land = land
+        target = (self.parts, length, width)
+        self.target = (call.store if land else call.give)(target, blocks.dtype)
         self.held = call.hold(blocks.shape[1:], blocks.dtype)
         self.l = call.flags(2)
         self.zf, self.af, self.xf, self.bf = (
@@ -1277,6 +1283,8 @@
             self.piece(s, self.far, self.bf, p.pair).wait_send()
             self.piece(s, self.near, self.af, p.pair).wait_recv()
             self.piece(s, self.near_far, self.bf, p.pair).wait_recv()
+        if self.land:
+            self.target.put()
 
     @property
     def result(self):
@@ -1368,6 +1376,23 @@
     key_at = lax.broadcasted_iota(jnp.int32, (1, keys), 1)
     same = seg_col[pl.ds(i * rows, rows), :1] == seg_row[:1, :keys]
     bias[:, :keys] = jnp.where(same & (key_at <= query_at), 0.0, neg_large)
+
+
+class Stacked:
+    def __init__(self, held):
+        self.held, self.dtype = held, held.dtype
+        blocks, rows, width = held.shape
+        self.shape = (blocks * rows, width)
+
+    def need(self, i=None):
+        pass
+
+    def __getitem__(self, key):
+        rows, columns = key
+        if isinstance(rows, slice):
+            block = self.held[:, :, columns]
+            return block.reshape(-1, block.shape[-1])
+        return self.held[rows.start // self.held.shape[1], :, columns]
 
 
 class Opening:
@@ -1394,17 +1419,14 @@
             call.store((count, LANES), jnp.float32, BLOCKS) for _ in range(3)
         )
         self.seg_row = call.store((8, count), jnp.float32)
-        self.gather = Gather(call, self.wa_one, places)
-        self.deal = Deal(call, inputs)
-        self.gather_gains = Gather(call, self.gains_wide, places)
+        self.gather = Gather(call, self.wa_one, places, land=True)
+        self.deal = Deal(call, inputs, land=True)
+        self.gather_gains = Gather(call, self.gains_wide, places, land=True)
         plan = ((2.0, 0.1), (5.0, 4.0), (14.0, 6.0))
         self.jobs = Jobs([self.gather_gains, self.deal, self.gather], plan)
         self.deal.late = True
-        self.x = call.hold((count, width), low)
-        self.wa = call.hold((width, 4 * hid), low)
-        self.gain_blocks = call.hold((places,) + gain_rows.shape, jnp.float32)
+        self.x, self.wa = Stacked(self.deal.target), Stacked(self.gather.whole)
         self.gains = call.store((gain_rows.shape[0], width), jnp.float32)
-        self.flag = call.flags(2 + 2 * parts)
 
     def tables(self):
         return (self.cosine, self.sine, self.seg_col, self.seg_row)
@@ -1461,35 +1483,8 @@
         self.jobs.finish()
         jobs.advance(0.5)
         shard = self.shard
-        copies = [
-            pltpu.make_async_copy(
-                self.gather_gains.whole.ref, self.gain_blocks.ref, self.flag.at[0]
-            )
-        ]
-        parts = self.deal.parts
-        length = self.count // parts
-        for k in range(parts):
-            copies.append(
-                pltpu.make_async_copy(
-                    self.deal.target.at[k],
-                    self.x.at[pl.ds(k * length, length)],
-                    self.flag.at[1 + k],
-                )
-            )
         for k in range(self.places):
-            copies.append(
-                pltpu.make_async_copy(
-                    self.gather.whole.at[k],
-                    self.wa.at[pl.ds(k * shard, shard)],
-                    self.flag.at[1 + parts],
-                )
-            )
-        for copy in copies:
-            copy.start()
-        for copy in copies:
-            copy.wait()
-        for k in range(self.places):
-            self.gains[:, k * shard : (k + 1) * shard] = self.gain_blocks[k]
+            self.gains[:, k * shard : (k + 1) * shard] = self.gather_gains.whole[k]
         self.gains.put()
 
 
@@ -2114,7 +2109,7 @@
         tables,
         lambda c, start: [
             Deal(c, cotangent),
-            Gather(c, shards_two[1], places),
+            Gather(c, shards_two[1], places, True),
             Gather(c, shards_two[2], places, True),
         ],
         ((8.0, 12.5, 16.0, 22.5, 22.6, 22.7), (16.0, 3.0), (26.0, 3.0)),
@@ -2250,7 +2245,7 @@
     sizes = dict(mesh.shape)
 
     def per_device(*operands):
-        fits = sizes[DP] == 2 and sizes[MP] == 4 and operands[0].shape[0] == sizes[CTX]
+        fits = sizes[DP] == 2 and sizes[MP] == 4 and operands[0].shape[0] == sizes[CTX] == BLOCKS
         return (dealt_device if fits else on_device)(*operands)
 
     return jax.shard_map(

time: 461 us -> 458 us (level)
  no operation moved by 1% of the time
where the time goes in v6:
time: 458 us; the launch traced here: 451 us
  Pallas kernels  447 us (98%)
    pallas_call x9, Pallas kernels, run(): pl.pallas_call(kernel, out_shape=tuple(self.shapes), in_specs=[space] * i...  447 us

profile of v6, /device:TPU:0, one launch (start us, length us, event | category | flops | bytes accessed | tf_op | source)
XLA Modules:
  0.0 450.5 jit_solution(17866105433209356908)
XLA Ops:
  0.7 1.4 stack.23.refs_4_
  2.0 95.1 %shard_map.373 = (bf16[128,704]{1,0:T(8,128)(2,1)}, bf16[128,704]{1,0:T(8,128)(2,1)}, bf16[128,704]{1,0:T(8,128)(2,1)}, bf16[128,1024]{1,0:T(8,128)(2,1)}, f32[1...) custom-call(bf16[128,256]{1,0:T(8,128)(2,1)} %refs_0_.1, ...), custom_call_target="tpu_custom_call" | custom-call | tf_op jit(solution)/shard_map/pallas_call | solution.py:781
  97.2 49.2 %shard_map.374 = (f32[1024,1024]{1,0:T(8,128)}, bf16[1024,1024]{1,0:T(8,128)(2,1)}, bf16[1024,1024]{1,0:T(8,128)(2,1)}, bf16[1024,704]{1,0:T(8,128)(2,1)}, bf16[...) custom-call(f32[1024,1024]{1,0:T(8,128)} %get-tuple-element.110.refs, ...), custom_call_target="tpu_custom_call" | custom-call | tf_op jit(solution)/shard_map/pallas_call | solution.py:781
  146.4 52.9 %shard_map.375 = (f32[1024,1024]{1,0:T(8,128)}, bf16[1024,1024]{1,0:T(8,128)(2,1)}, bf16[1024,256]{1,0:T(8,128)(2,1)}, bf16[1024,256]{1,0:T(8,128)(2,1)}, bf16[1...) custom-call(f32[1024,1024]{1,0:T(8,128)} %get-tuple-element.117.refs, ...), custom_call_target="tpu_custom_call" | custom-call | tf_op jit(solution)/shard_map/pallas_call | solution.py:781
  199.2 46.0 %shard_map.376 = (bf16[4,64,1024]{2,1,0:T(8,128)(2,1)}, f32[1024,1024]{1,0:T(8,128)}, f32[1,1024]{1,0:T(1,128)}, bf16[1024,704]{1,0:T(8,128)(2,1)}, bf16[1024,704]{1,0:T(8,128)(2,1)}, /*index=5*/f32[128,704]{1,0:T(8,128)}) custom-call(f32[1024,1024]{1,0:T(8,128)} %get-tuple-element.126.refs_0_, ...), custom_call_target="tpu_custom_call" | custom-call | tf_op jit(solution)/shard_map/pallas_call | solution.py:781
  245.3 52.6 %shard_map.377 = (f32[1024,1024]{1,0:T(8,128)}, f32[1024,256]{1,0:T(8,128)}, f32[1,1024]{1,0:T(1,128)}, bf16[1024,1024]{1,0:T(8,128)(2,1)}, f32[128,704]{1,0:T(8...) custom-call(f32[1024,1024]{1,0:T(8,128)} %get-tuple-element.131.refs_0_, bf16[1024,1024]{1,0:T(8,128)(2,1)} %bitcast.44, ...), custom_call_target="tpu_custom_call" | custom-call | tf_op jit(solution)/shard_map/pallas_call | solution.py:781
  297.9 58.0 %shard_map.378 = (f32[1024,1024]{1,0:T(8,128)}, f32[1,1024]{1,0:T(1,128)}, bf16[1024,704]{1,0:T(8,128)(2,1)}, bf16[1024,704]{1,0:T(8,128)(2,1)}, f32[128,704]{1,...) custom-call(f32[1024,1024]{1,0:T(8,128)} %get-tuple-element.141.refs_0_, bf16[1024,704]{1,0:T(8,128)(2,1)} %bitcast.50, ...), custom_call_target="tpu_custom_call" | custom-call | tf_op jit(solution)/shard_map/pallas_call | solution.py:781
  355.8 0.0 copy-start
  355.9 0.0 copy-start.1
  355.9 0.0 copy-start.2
  355.9 48.7 %shard_map.379 = (bf16[1024,1024]{1,0:T(8,128)(2,1)}, f32[1,1024]{1,0:T(1,128)}, bf16[1024,1024]{1,0:T(8,128)(2,1)}, f32[128,704]{1,0:T(8,128)}, f32[128,704]{1,0:T(8,128)}) custom-call(f32[1024,1024]{1,0:T(8,128)} %get-tuple-element.150.refs_0_, bf16[1024,1024]{1,0:T(8,128)(2,1)} %bitcast.51, bf16[1024,256]{1,0:T(8,128)(2,1)} %get-tuple-element.152.refs_2_, ...), custom_call_target="tpu_custom_call" | custom-call | tf_op jit(solution)/shard_map/pallas_call | solution.py:781
  404.6 0.0 copy-done
  404.6 0.0 copy-done.1
  404.6 0.0 copy-done.2
  404.6 1.4 concatenate.3
  406.0 36.7 %shard_map.380 = (f32[8,128]{1,0:T(8,128)}, f32[128,1024]{1,0:T(8,128)}, bf16[4,256,1024]{2,1,0:T(8,128)(2,1)}) custom-call(f32[8,8,128]{2,1,0:T(8,128)} %bitcast.72, bf16[8,128,1024]{2,1,0:T(8,128)(2,1)} %bitcast.56, bf16[4,256,1024]{2,1,0:T(8,128)(2,1)} %bitcast.55), custom_call_target="tpu_custom_call" | custom-call | tf_op jit(solution)/shard_map/pallas_call | solution.py:781
  442.7 7.6 %shard_map.381 = (bf16[1024,1024]{1,0:T(8,128)(2,1)}, bf16[1024,1024]{1,0:T(8,128)(2,1)}, f32[1024,1024]{1,0:T(8,128)}, f32[128,256]{1,0:T(8,128)}, f32[128,256]...) custom-call(bf16[1024,1024]{1,0:T(8,128)(2,1)} %bitcast.58, ...), custom_call_target="tpu_custom_call" | custom-call | tf_op jit(solution)/shard_map/pallas_call | solution.py:781
Async XLA Ops:
  355.8 48.7 %copy-start = (f32[1,1024]{1,0:T(1,128)S(1)}, f32[1,1024]{1,0:T(1,128)}, u32[]{:S(2)}) copy-start(f32[1,1024]{1,0:T(1,128)} %get-tuple-element.165) | copy-start | bytes 12292
  355.9 48.7 %copy-start.1 = (f32[1,1024]{1,0:T(1,128)S(1)}, f32[1,1024]{1,0:T(1,128)}, u32[]{:S(2)}) copy-start(f32[1,1024]{1,0:T(1,128)} %get-tuple-element.164) | copy-start | bytes 12292
  355.9 48.7 %copy-start.2 = (f32[1,1024]{1,0:T(1,128)S(1)}, f32[1,1024]{1,0:T(1,128)}, u32[]{:S(2)}) copy-start(f32[1,1024]{1,0:T(1,128)} %get-tuple-element.163) | copy-start | bytes 12292

commit v7 on v6

--- a/solution.py
+++ b/solution.py
@@ -2175,7 +2175,7 @@
         0,
         tables,
         lambda c: [Scatter(c, array) for array in ffn_grads(back_ffn_one)],
-        grads_plan,
+        ((11.0, 3.5), (24.0, 6.0)),
     )
     gate_g1, up_g1 = back_attn_one.carried
     gain_grads = jnp.concatenate(

time: 458 us -> 462 us (level)
  Pallas kernels: 447 us -> 455 us
    pallas_call x9, Pallas kernels: 447 us -> 455 us  [run(): pl.pallas_call(kernel, out_shape=tuple(self.shapes), in_specs=[space] * i...]
where the time goes in v7:
time: 462 us; the launch traced here: 459 us
  Pallas kernels  455 us (98%)
    pallas_call x9, Pallas kernels, run(): pl.pallas_call(kernel, out_shape=tuple(self.shapes), in_specs=[space] * i...  455 us

profile of v7, /device:TPU:0, one launch (start us, length us, event | category | flops | bytes accessed | tf_op | source)
XLA Modules:
  0.0 458.6 jit_solution(16904162466180587570)
XLA Ops:
  0.7 1.4 stack.23.refs_4_
  2.0 95.1 %shard_map.373 = (bf16[128,704]{1,0:T(8,128)(2,1)}, bf16[128,704]{1,0:T(8,128)(2,1)}, bf16[128,704]{1,0:T(8,128)(2,1)}, bf16[128,1024]{1,0:T(8,128)(2,1)}, f32[1...) custom-call(bf16[128,256]{1,0:T(8,128)(2,1)} %refs_0_.1, ...), custom_call_target="tpu_custom_call" | custom-call | tf_op jit(solution)/shard_map/pallas_call | solution.py:781
  97.2 49.2 %shard_map.374 = (f32[1024,1024]{1,0:T(8,128)}, bf16[1024,1024]{1,0:T(8,128)(2,1)}, bf16[1024,1024]{1,0:T(8,128)(2,1)}, bf16[1024,704]{1,0:T(8,128)(2,1)}, bf16[...) custom-call(f32[1024,1024]{1,0:T(8,128)} %get-tuple-element.110.refs, ...), custom_call_target="tpu_custom_call" | custom-call | tf_op jit(solution)/shard_map/pallas_call | solution.py:781
  146.4 61.3 %shard_map.375 = (f32[1024,1024]{1,0:T(8,128)}, bf16[1024,1024]{1,0:T(8,128)(2,1)}, bf16[1024,256]{1,0:T(8,128)(2,1)}, bf16[1024,256]{1,0:T(8,128)(2,1)}, bf16[1...) custom-call(f32[1024,1024]{1,0:T(8,128)} %get-tuple-element.117.refs, ...), custom_call_target="tpu_custom_call" | custom-call | tf_op jit(solution)/shard_map/pallas_call | solution.py:781
  207.7 46.0 %shard_map.376 = (bf16[4,64,1024]{2,1,0:T(8,128)(2,1)}, f32[1024,1024]{1,0:T(8,128)}, f32[1,1024]{1,0:T(1,128)}, bf16[1024,704]{1,0:T(8,128)(2,1)}, bf16[1024,704]{1,0:T(8,128)(2,1)}, /*index=5*/f32[128,704]{1,0:T(8,128)}) custom-call(f32[1024,1024]{1,0:T(8,128)} %get-tuple-element.126.refs_0_, ...), custom_call_target="tpu_custom_call" | custom-call | tf_op jit(solution)/shard_map/pallas_call | solution.py:781
  253.7 52.6 %shard_map.377 = (f32[1024,1024]{1,0:T(8,128)}, f32[1024,256]{1,0:T(8,128)}, f32[1,1024]{1,0:T(1,128)}, bf16[1024,1024]{1,0:T(8,128)(2,1)}, f32[128,704]{1,0:T(8...) custom-call(f32[1024,1024]{1,0:T(8,128)} %get-tuple-element.131.refs_0_, bf16[1024,1024]{1,0:T(8,128)(2,1)} %bitcast.44, ...), custom_call_target="tpu_custom_call" | custom-call | tf_op jit(solution)/shard_map/pallas_call | solution.py:781
  306.3 58.0 %shard_map.378 = (f32[1024,1024]{1,0:T(8,128)}, f32[1,1024]{1,0:T(1,128)}, bf16[1024,704]{1,0:T(8,128)(2,1)}, bf16[1024,704]{1,0:T(8,128)(2,1)}, f32[128,704]{1,...) custom-call(f32[1024,1024]{1,0:T(8,128)} %get-tuple-element.141.refs_0_, bf16[1024,704]{1,0:T(8,128)(2,1)} %bitcast.50, ...), custom_call_target="tpu_custom_call" | custom-call | tf_op jit(solution)/shard_map/pallas_call | solution.py:781
  364.3 0.0 copy-start
  364.3 0.0 copy-start.1
  364.3 0.0 copy-start.2
  364.3 47.8 %shard_map.379 = (bf16[1024,1024]{1,0:T(8,128)(2,1)}, f32[1,1024]{1,0:T(1,128)}, bf16[1024,1024]{1,0:T(8,128)(2,1)}, f32[128,704]{1,0:T(8,128)}, f32[128,704]{1,0:T(8,128)}) custom-call(f32[1024,1024]{1,0:T(8,128)} %get-tuple-element.150.refs_0_, bf16[1024,1024]{1,0:T(8,128)(2,1)} %bitcast.51, bf16[1024,256]{1,0:T(8,128)(2,1)} %get-tuple-element.152.refs_2_, ...), custom_call_target="tpu_custom_call" | custom-call | tf_op jit(solution)/shard_map/pallas_call | solution.py:781
  412.1 0.0 copy-done
  412.1 0.0 copy-done.1
  412.1 0.0 copy-done.2
  412.2 1.4 concatenate.3
  413.6 37.2 %shard_map.380 = (f32[8,128]{1,0:T(8,128)}, f32[128,1024]{1,0:T(8,128)}, bf16[4,256,1024]{2,1,0:T(8,128)(2,1)}) custom-call(f32[8,8,128]{2,1,0:T(8,128)} %bitcast.72, bf16[8,128,1024]{2,1,0:T(8,128)(2,1)} %bitcast.56, bf16[4,256,1024]{2,1,0:T(8,128)(2,1)} %bitcast.55), custom_call_target="tpu_custom_call" | custom-call | tf_op jit(solution)/shard_map/pallas_call | solution.py:781
  450.8 7.6 %shard_map.381 = (bf16[1024,1024]{1,0:T(8,128)(2,1)}, bf16[1024,1024]{1,0:T(8,128)(2,1)}, f32[1024,1024]{1,0:T(8,128)}, f32[128,256]{1,0:T(8,128)}, f32[128,256]...) custom-call(bf16[1024,1024]{1,0:T(8,128)(2,1)} %bitcast.58, ...), custom_call_target="tpu_custom_call" | custom-call | tf_op jit(solution)/shard_map/pallas_call | solution.py:781
Async XLA Ops:
  364.3 47.8 %copy-start = (f32[1,1024]{1,0:T(1,128)S(1)}, f32[1,1024]{1,0:T(1,128)}, u32[]{:S(2)}) copy-start(f32[1,1024]{1,0:T(1,128)} %get-tuple-element.165) | copy-start | bytes 12292
  364.3 47.8 %copy-start.1 = (f32[1,1024]{1,0:T(1,128)S(1)}, f32[1,1024]{1,0:T(1,128)}, u32[]{:S(2)}) copy-start(f32[1,1024]{1,0:T(1,128)} %get-tuple-element.164) | copy-start | bytes 12292
  364.3 47.8 %copy-start.2 = (f32[1,1024]{1,0:T(1,128)S(1)}, f32[1,1024]{1,0:T(1,128)}, u32[]{:S(2)}) copy-start(f32[1,1024]{1,0:T(1,128)} %get-tuple-element.163) | copy-start | bytes 12292
